TPU v7x, 32 devices: a whole 2x2x4 slice. The times are simulated.
32 devices in a mesh: groups: 2 (over y), seq: 4 (over z), head: 2 (over x), batch: 2 (over core).
Axes of the slice: x: 2, y: 2, z: 4, core: 2. Of those that a mesh axis runs over, the one named last changes fastest.
Arguments:
- queries: bfloat16 [4, 512, 2560], P(('groups', 'batch'), 'seq', 'head'), parts along dimension 0, may hold values from -6 to 6
- keys: bfloat16 [4, 512, 2560], P(('groups', 'batch'), 'seq', 'head'), parts along dimension 0, may hold values from -6 to 6
- values: bfloat16 [4, 512, 2560], P(('groups', 'batch'), 'seq', 'head'), parts along dimension 0, may hold values from -6 to 6
- cache_keys: bfloat16 [4, 8, 32, 2560], P(('groups', 'batch'), 'seq', None, 'head'), parts along dimension 0, may hold values from -6 to 6
- cache_values: bfloat16 [4, 8, 32, 2560], P(('groups', 'batch'), 'seq', None, 'head'), parts along dimension 0, may hold values from -6 to 6
- frame_list: int32 [4, 3], P(('groups', 'batch')), parts along dimension 0, may hold values from 0 to 7, as said below
- frame_place: int32 [4, 8], P(('groups', 'batch')), parts along dimension 0, may hold values from 0 to 7, each once within a row
- tile_mask: int32 [4, 4, 4], P(('groups', 'batch'), 'seq'), parts along dimension 0, may hold values from 0 to 1, as said below
Outputs:
- attention: bfloat16 [4, 512, 2560], P(('groups', 'batch'), 'seq', 'head'), parts along dimension 0
There are 2 independent parts, one for each index of `groups`. A program takes and returns all parts, laid end to end along the dimension named above; each array names one. Nothing has to cross between parts.
Inputs may be any that keep to these rules, and one draw needn't show every extreme that they name: `frame_list`: each row holds frame 0 and then 3 - 1 consecutive frame numbers. `tile_mask`: ones on the diagonal of each video's tile matrix.
All inputs are finite; a program needn't handle non-finite values.
Results may differ from a plain program's by a relative error of at most 0.006.
Values may be sent and summed in bfloat16 or wider, within the bound.
No kernel may reach another device: no remote copies, remote signals or barrier semaphores. Data moves between devices by JAX's collectives and lax.ppermute only.
A program may use at most 128 MiB of HBM per device.

v0:
```python
import math

import jax
import jax.numpy as jnp
from jax import lax
from jax.sharding import PartitionSpec as P

HD = 128
TILE = 128


NEG_FILL = -1e30


def attend(running, key_part, value_part, live, query_heads):
    videos, length, col_count = key_part.shape
    head_count = col_count // HD

    def update(previous):
        peak_old, total_old, summed_old = previous
        key_heads = key_part.reshape(videos, length, head_count, HD)
        value_heads = value_part.reshape(videos, length, head_count, HD)
        scores = jnp.einsum(
            "vqhd,vkhd->vhqk", query_heads, key_heads, preferred_element_type=jnp.float32
        ) * (1.0 / math.sqrt(HD))
        allowed = live[:, None, :, :]
        scores = jnp.where(allowed, scores, NEG_FILL)
        peak_new = jnp.maximum(peak_old, jnp.max(scores, axis=3))
        weights = jnp.where(allowed, jnp.exp(scores - peak_new[..., None]), 0.0)
        factor = jnp.exp(peak_old - peak_new)
        total_new = total_old * factor + jnp.sum(weights, axis=3)
        product = jnp.einsum(
            "vhqk,vkhd->vhqd",
            weights.astype(jnp.bfloat16),
            value_heads,
            preferred_element_type=jnp.float32,
        )
        summed_new = summed_old * factor[..., None] + product
        return (peak_new, total_new, summed_new)

    def unchanged(previous):
        return previous

    return lax.cond(jnp.any(live), update, unchanged, running)


def body(queries, keys, values, cache_keys, cache_values, frame_list, frame_place, tile_mask):
    videos, tok_rows, col_count = queries.shape
    head_count = col_count // HD
    query_heads = queries.reshape(videos, tok_rows, head_count, HD)
    running = (
        jnp.full((videos, head_count, tok_rows), NEG_FILL, jnp.float32),
        jnp.zeros((videos, head_count, tok_rows), jnp.float32),
        jnp.zeros((videos, head_count, tok_rows, HD), jnp.float32),
    )
    frame_tok = cache_keys.shape[2]
    listed = jnp.any(frame_place[:, :, None] == frame_list[:, None, :], axis=2)
    key_piece = lax.all_gather(cache_keys, "seq", axis=1, tiled=True)
    value_piece = lax.all_gather(cache_values, "seq", axis=1, tiled=True)
    count_frames = key_piece.shape[1]
    token_flags = jnp.repeat(listed, frame_tok, axis=1)
    live = jnp.broadcast_to(token_flags[:, None, :], (videos, tok_rows, count_frames * frame_tok))
    key_flat = key_piece.reshape(videos, count_frames * frame_tok, col_count)
    value_flat = value_piece.reshape(videos, count_frames * frame_tok, col_count)
    running = attend(running, key_flat, value_flat, live, query_heads)
    key_piece = lax.all_gather(keys, "seq", axis=1, tiled=True)
    value_piece = lax.all_gather(values, "seq", axis=1, tiled=True)
    length = key_piece.shape[1]
    key_tiles = jnp.arange(length, dtype=jnp.int32) // TILE
    tile_live = jnp.take(tile_mask, key_tiles, axis=2)
    running = attend(
        running, key_piece, value_piece, jnp.repeat(tile_live, TILE, axis=1) > 0, query_heads
    )
    peak, total, summed = running
    result = summed / total[..., None]
    return result.transpose(0, 2, 1, 3).reshape(videos, tok_rows, col_count).astype(jnp.bfloat16)


def solution(mesh):
    return jax.shard_map(
        body,
        mesh=mesh,
        in_specs=(
            P(("groups", "batch"), "seq", "head"),
            P(("groups", "batch"), "seq", "head"),
            P(("groups", "batch"), "seq", "head"),
            P(("groups", "batch"), "seq", None, "head"),
            P(("groups", "batch"), "seq", None, "head"),
            P(("groups", "batch"), None),
            P(("groups", "batch"), None),
            P(("groups", "batch"), "seq", None),
        ),
        out_specs=P(("groups", "batch"), "seq", "head"),
        check_vma=False,
    )
```

profile of v0, /device:TPU:0, one launch (start us, length us, event | category | flops | bytes accessed | tf_op | source)
XLA Modules:
  0.0 110.2 jit_solution(18014833076720647111)
XLA Ops:
  6.5 0.0 copy-start.3
  6.5 0.0 copy-start.5
  6.5 0.0 copy-start.6
  6.5 0.0 copy-start
  6.5 0.0 copy-start.1
  6.5 0.0 all-gather.3.cloned.1.call-start
  6.6 1.9 %copy.50 = bf16[1,128,1280]{1,2,0:T(8,128)(2,1)} copy(bf16[1,128,1280]{2,1,0:T(8,128)(2,1)} %param.13) | data formatting | bytes 655360 | tf_op args[1]
  8.5 0.0 all-gather.3.cloned.1.call-update
  8.6 0.0 copy-start.2
  8.6 0.0 all-gather.5.cloned.1.call-start
  8.6 1.9 %copy.51 = bf16[1,128,1280]{1,2,0:T(8,128)(2,1)} copy(bf16[1,128,1280]{2,1,0:T(8,128)(2,1)} %param.14) | data formatting | bytes 655360 | tf_op args[2]
  10.5 0.0 all-gather.5.cloned.1.call-update
  10.5 0.0 copy-done.3
  10.6 0.7 fusion.41
  11.2 2.7 %compare_select_fusion.1 = s32[512,1]{0,1:T(1,128)S(1)} fusion(s32[]{:T(128)} %bitcast.15, s32[]{:T(128)} %bitcast.16, s32[]{:T(128)} %bitcast.18, s32[]{:T(128)} %bitcast.17), kind=kLoop, calls=%fused_computation.45 | loop fusion | flops 8704 | bytes 2064 | tf_op jit(solution)/shard_map/jit(_take)/gather | solution.py:70
  14.0 0.8 broadcast_reduce_fusion
  15.4 0.0 copy-done.5
  15.4 0.0 copy-done.6
  15.4 0.1 compare_reduce_fusion
  15.5 0.1 broadcast_in_dim.88
  15.6 0.1 broadcast_in_dim.89
  15.7 0.7 broadcast_reduce_fusion.1
  17.1 0.0 copy-done
  17.2 0.2 copy.44
  17.4 0.0 copy-done.1
  17.4 27.2 %all_gather.12 = bf16[1,8,32,1280]{3,2,0,1:T(8,128)(2,1)S(1)} all-gather(bf16[1,2,32,1280]{3,2,0,1:T(8,128)(2,1)S(1)} %bitcast.73), channel_id=1, replica_groups=mesh['groups'=2,'seq'=4,'head'=2,'batch'=2] {'seq'}, dimensions={1}, use_global_device_ids=true | all-gather | bytes 819200 | tf_op jit(solution)/shard_map/all_gather | solution.py:58
  44.6 0.0 copy-done.2
  44.6 21.8 %all_gather.13 = bf16[1,8,32,1280]{3,2,0,1:T(8,128)(2,1)S(1)} all-gather(bf16[1,2,32,1280]{3,2,0,1:T(8,128)(2,1)S(1)} %bitcast.74), channel_id=1, replica_groups=mesh['groups'=2,'seq'=4,'head'=2,'batch'=2] {'seq'}, dimensions={1}, use_global_device_ids=true | all-gather | bytes 819200 | tf_op jit(solution)/shard_map/all_gather | solution.py:59
  66.3 3.3 %conditional.2 = (f32[1,10,128]{2,1,0:T(8,128)S(1)}, f32[1,10,128]{2,1,0:T(8,128)S(1)}, f32[1,10,128,128]{3,2,1,0:T(8,128)}) conditional(s32[]{:T(128)} %convert_element_type.32, () %tuple.20, (pred[8]{0:T(512)(128)(4,1)S(1)}, bf16[1,128,10,128]{1,3,2,0:T(8,128)(2,1)S(1)}, bf16[1,8,32,1280]{3,2,0,1:T(8,128)(2,1)S(1)}, ...), branch_computations={%region_3.4_spmd, %region_4.7_spmd} | conditional | flops 170891520 | bytes 8910368 | solution.py:44
  66.3 0.4 reshape.260
  66.7 0.1 broadcast_in_dim.71
  66.8 0.1 reshape.258
  66.9 0.5 fusion.40
  67.4 0.5 fusion.3
  67.9 0.4 reshape.261
  68.3 1.3 %fusion.1 = f32[1,10,128,128]{3,2,1,0:T(8,128)} fusion(f32[10,128,256]{2,1,0:T(8,128)S(1)} %get-tuple-element.99, bf16[256,10,128]{2,1,0:T(8,128)(2,1)S(1)} %reshape.261, f32[10,128]{1,0:T(8,128)S(1)} %get-tuple-element.97, pred[256]{0:T(512)(128)(4,1)S(1)} %reshape.258, f32[10,128]{1,0:T(8,128)S(1)} %get-tuple-element.96), kind=kOutput, calls=%fused_computation.4 | convolution fusion | flops 85032960 | bytes 2631936 | tf_op jit(solution)/shard_map/cond/branch_1_fun/vhqk,vkhd->vhqd/dot_general | solution.py:32
  69.6 0.0 all-gather.3.cloned.1.call-done
  69.6 26.9 %all-gather.5.cloned.1.call-done = bf16[1,512,1280]{1,2,0:T(8,128)(2,1)} async-done(((bf16[1,128,1280]{1,2,0:T(8,128)(2,1)}), bf16[1,512,1280]{1,2,0:T(8,128)(2,1)}) %all-gather.5.cloned.1.call-update) | async-done | bytes 1310736 | tf_op jit(solution)/shard_map/all_gather | solution.py:67
  96.6 5.8 %conditional.3 = (f32[1,10,128]{2,1,0:T(8,128)S(1)}, f32[1,10,128,128]{2,3,1,0:T(8,128)S(1)}) conditional(s32[]{:T(128)} %convert_element_type.31, (f32[1,10,128]{2,1,0:T(8,128)S(1)}, f32[1,10,128,128]{3,2,1,0:T(8,128)}) %tuple.22, (pred[1,128,512]{2,1,0:T(8,128)(4,1)S(1)}, bf16[1,128,10,128]{1,3,2,0:T(8,128)(2,1)S(1)}, ...), branch_computations={%region_7.8_spmd, %region_8.11_spmd} | conditional | flops 344396800 | bytes 18946092 | solution.py:44
  96.6 2.0 %fusion.13 = (f32[10,128]{1,0:T(8,128)S(1)}, f32[10,128,512]{2,1,0:T(8,128)S(1)}) fusion(pred[128,512]{1,0:T(8,128)(4,1)S(1)} %bitcast.70, bf16[512,10,128]{0,2,1:T(8,128)(2,1)} %bitcast.68, bf16[1,128,10,128]{1,3,2,0:T(8,128)(2,1)S(1)} %get-tuple-element.81), kind=kOutput, calls=%fused_computation.20 | convolution fusion | flops 169736960 | bytes 4330496 | tf_op jit(solution)/shard_map/cond/branch_1_fun/vqhd,vkhd->vhqk/dot_general | solution.py:23
  98.6 0.0 copy-start.4
  98.7 0.9 fusion.15
  99.5 0.4 copy-done.4
  100.0 2.2 %fusion.26 = f32[1,10,128,128]{3,2,1,0:T(8,128)S(1)} fusion(bf16[512,10,128]{0,2,1:T(8,128)(2,1)S(1)} %bitcast.77, f32[10,128,512]{2,1,0:T(8,128)S(1)} %get-tuple-element.95, f32[10,128]{1,0:T(8,128)S(1)} %get-tuple-element.93, pred[128,512]{1,0:T(8,128)(4,1)S(1)} %bitcast.72, f32[1,10,128,128]{3,2,1,0:T(8,128)} %get-tuple-element.42, ...), kind=kOutput, calls=%fused_computation.30 | convolution fusion | flops 171376640 | bytes 5318656 | tf_op jit(solution)/shard_map/cond/branch_1_fun/vhqk,vkhd->vhqd/dot_general | solution.py:32
  102.1 0.2 copy.58
  102.4 0.1 divide_convert_fusion
  102.4 0.9 copy.54
  (6 shorter events, 0.1 us)
Async XLA Ops:
  6.5 4.0 %copy-start.3 = (s32[1,1,4]{2,1,0:T(1,128)S(1)}, s32[1,1,4]{2,1,0:T(1,128)}, u32[]{:S(2)}) copy-start(s32[1,1,4]{2,1,0:T(1,128)} %param.19) | copy-start | bytes 52
  6.5 8.9 %copy-start.5 = (s32[1,8]{1,0:T(1,128)S(1)}, s32[1,8]{1,0:T(1,128)}, u32[]{:S(2)}) copy-start(s32[1,8]{1,0:T(1,128)} %param.18) | copy-start | bytes 100
  6.5 8.9 %copy-start.6 = (s32[1,3]{1,0:T(1,128)S(1)}, s32[1,3]{1,0:T(1,128)}, u32[]{:S(2)}) copy-start(s32[1,3]{1,0:T(1,128)} %param.17) | copy-start | bytes 40
  6.5 10.6 %copy-start = (bf16[1,128,1280]{2,1,0:T(8,128)(2,1)S(1)}, bf16[1,128,1280]{2,1,0:T(8,128)(2,1)}, u32[]{:S(2)}) copy-start(bf16[1,128,1280]{2,1,0:T(8,128)(2,1)} %param.12) | copy-start | bytes 983044
  6.5 10.8 %copy-start.1 = (bf16[1,2,32,1280]{3,2,1,0:T(8,128)(2,1)S(1)}, bf16[1,2,32,1280]{3,2,1,0:T(8,128)(2,1)}, u32[]{:S(2)}) copy-start(bf16[1,2,32,1280]{3,2,1,0:T(8,128)(2,1)} %param.15) | copy-start | bytes 491524
  6.5 63.1 %all-gather.3.cloned.1.call-start = ((), (), s32[]{:S(2)}) async-start(), calls=%async_computation | async-start | bytes 1638400 | tf_op jit(solution)/shard_map/all_gather | solution.py:66
  8.6 36.0 %copy-start.2 = (bf16[1,2,32,1280]{3,2,1,0:T(8,128)(2,1)S(1)}, bf16[1,2,32,1280]{3,2,1,0:T(8,128)(2,1)}, u32[]{:S(2)}) copy-start(bf16[1,2,32,1280]{3,2,1,0:T(8,128)(2,1)} %param.16) | copy-start | bytes 491524
  8.6 88.0 %all-gather.5.cloned.1.call-start = ((), (), s32[]{:S(2)}) async-start(), calls=%async_computation.1 | async-start | bytes 1638400 | tf_op jit(solution)/shard_map/all_gather | solution.py:67
  98.6 1.3 %copy-start.4 = (bf16[1,512,1280]{1,2,0:T(8,128)(2,1)S(1)}, bf16[1,512,1280]{1,2,0:T(8,128)(2,1)}, u32[]{:S(2)}) copy-start(bf16[1,512,1280]{1,2,0:T(8,128)(2,1)} %get-tuple-element.43) | copy-start | bytes 3932164 | tf_op jit(solution)/shard_map/cond
Sparse Core Ops, SparseCore 0:
  8.9 54.7 all-gather.2
  65.3 31.2 all-gather.4
where the time goes:
time: 111 us; the launch traced here: 110 us
  blocking collectives  49 us (44%)
  waiting for transfers between devices  27 us (24%)
  between operations  14.9 us (13%)
  local copies, waits for them, and re-layouts  7.46 us (7%)
  matrix products  5.99 us (5%)
  other arithmetic  5.75 us (5%)
    all_gather x1, blocking collectives, body(): key_piece = lax.all_gather(cache_keys, 'seq', axis=1, tiled=True)  27.2 us
    all_gather x1, waiting for transfers between devices, body(): value_piece = lax.all_gather(values, 'seq', axis=1, tiled=True)  26.9 us
    all_gather x1, blocking collectives, body(): value_piece = lax.all_gather(cache_values, 'seq', axis=1, tiled=True)  21.8 us
    unnamed x15, local copies, waits for them, and re-layouts  4.08 us
    dot_general x2, matrix products, update(): jnp.einsum('vhqk,vkhd->vhqd', weights.astype(jnp.bfloat16), value_heads,...  3.49 us
    gather x1, other arithmetic, body(): tile_live = jnp.take(tile_mask, key_tiles, axis=2)  2.7 us
    dot_general x2, matrix products, update(): jnp.einsum('vqhd,vkhd->vhqk', query_heads, key_heads, preferred_element_t...  2.5 us
  transfers between devices with their start and end apart: 2, of which 1 were waited for; matrix products, arithmetic and copies ran while one was open for 10% of the time, Pallas kernels for 0%

commit v1 on v0

--- a/solution.py
+++ b/solution.py
@@ -1,15 +1,22 @@
+import functools
 import math
 
 import jax
 import jax.numpy as jnp
 from jax import lax
+from jax.experimental import pallas as pl
+from jax.experimental.pallas import tpu as pltpu
 from jax.sharding import PartitionSpec as P
 
 HD = 128
 TILE = 128
-
-
 NEG_FILL = -1e30
+FACTOR = math.log2(math.e) / math.sqrt(HD)
+FLAG_ROWS = 16
+VMEM = pl.BlockSpec(memory_space=pltpu.VMEM)
+SMEM = pl.BlockSpec(memory_space=pltpu.SMEM)
+BF16 = jnp.bfloat16
+F32 = jnp.float32
 
 
 def attend(running, key_part, value_part, live, query_heads):
@@ -44,7 +51,7 @@
     return lax.cond(jnp.any(live), update, unchanged, running)
 
 
-def body(queries, keys, values, cache_keys, cache_values, frame_list, frame_place, tile_mask):
+def gathered(queries, keys, values, cache_keys, cache_values, frame_list, frame_place, tile_mask):
     videos, tok_rows, col_count = queries.shape
     head_count = col_count // HD
     query_heads = queries.reshape(videos, tok_rows, head_count, HD)
@@ -76,6 +83,290 @@
     return result.transpose(0, 2, 1, 3).reshape(videos, tok_rows, col_count).astype(jnp.bfloat16)
 
 
+def head_cols(head):
+    start = head * HD
+    if not isinstance(head, int):
+        start = pl.multiple_of(start, HD)
+    return pl.ds(start, HD)
+
+
+def fill(live):
+    return jnp.where(live, 0.0, NEG_FILL)
+
+
+def frame_fills(place_ref, list_ref, device, frames):
+    out = []
+    for slot in range(frames):
+        held = place_ref[0, device * frames + slot]
+        live = held == list_ref[0, 0]
+        for entry in range(1, list_ref.shape[1]):
+            live = live | (held == list_ref[0, entry])
+        out.append(fill(live))
+    return out
+
+
+def rows_of(ref, head):
+    if len(ref.shape) == 3:
+        return ref[0, :, head_cols(head)]
+    return ref[0, :, :, head_cols(head)].reshape(ref.shape[1] * ref.shape[2], HD)
+
+
+def pack_kernel(half, mask_ref, q_ref, k_ref, v_ref, ck_ref, cv_ref, *out_refs):
+    split_refs, whole_refs = out_refs[:3], out_refs[3:]
+    me = lax.axis_index("seq")
+    side = lax.rem(me, 2)
+    parts = (q_ref, k_ref, v_ref, ck_ref, cv_ref)
+    for rel in (1, 2, 3):
+        other = jnp.bitwise_xor(me, rel)
+        group = (1 - side) if rel % 2 else side
+        out = split_refs[rel - 1]
+        row = 0
+        for j in range(half):
+            head = group * half + j
+            for ref in parts if rel == 1 else parts[:1]:
+                block = rows_of(ref, head)
+                out[row : row + block.shape[0], :] = block
+                row += block.shape[0]
+        flags = [fill(mask_ref[0, 0, jnp.bitwise_xor(other, key)] > 0) for key in range(4)]
+        ident = lax.broadcasted_iota(jnp.int32, (FLAG_ROWS, HD), 0)
+        block = jnp.zeros((FLAG_ROWS, HD), F32)
+        for key in range(4):
+            block = jnp.where(ident == key, flags[key], block)
+        out[row : row + FLAG_ROWS, :] = block.astype(BF16)
+        out = whole_refs[rel - 1]
+        row = 0
+        for ref in parts:
+            block = rows_of(ref, 2 * half + other)
+            out[row : row + block.shape[0], :] = block
+            row += block.shape[0]
+
+
+def softmax_part(key_rows, value_rows, query_rows, fills):
+    scores = lax.dot_general(
+        key_rows, query_rows, (((1,), (1,)), ((), ())), preferred_element_type=F32
+    )
+    pieces = []
+    row = 0
+    for count, value in fills:
+        pieces.append(scores[row : row + count, :] * FACTOR + value)
+        row += count
+    scores = jnp.concatenate(pieces, axis=0)
+    peak = jnp.max(scores, axis=0, keepdims=True)
+    weights = jnp.exp2(scores - peak)
+    total = jnp.sum(weights, axis=0, keepdims=True)
+    summed = lax.dot_general(
+        value_rows, weights.astype(BF16), (((0,), (0,)), ((), ())), preferred_element_type=F32
+    )
+    return summed / total, peak + jnp.log2(total)
+
+
+def own_flags(mask_ref, me):
+    return [
+        jnp.full((1, TILE), fill(mask_ref[0, 0, jnp.bitwise_xor(me, key)] > 0), F32)
+        for key in range(4)
+    ]
+
+
+def split_kernel(
+    half, frames, frame_tok,
+    mask_ref, list_ref, place_ref, q_ref, k_ref, v_ref, ck_ref, cv_ref, in1_ref, in2_ref, in3_ref,
+    own_ref, own_log_ref, out1_ref, out2_ref, out3_ref,
+):
+    me = lax.axis_index("seq")
+    side = lax.rem(me, 2)
+    cache = frames * frame_tok
+    span = 3 * TILE + 2 * cache
+    flags = [own_flags(mask_ref, me)]
+    for ref, row in ((in1_ref, half * span), (in2_ref, half * TILE), (in3_ref, half * TILE)):
+        block = ref[row : row + FLAG_ROWS, :].astype(F32)
+        flags.append([block[key : key + 1, :] for key in range(4)])
+    fills = [(TILE, jnp.concatenate([flags[rel][key] for rel in range(4)], axis=1)) for key in range(2)]
+    for rel in range(2):
+        for value in frame_fills(place_ref, list_ref, jnp.bitwise_xor(me, rel), frames):
+            fills.append((frame_tok, value))
+    stats = [[], [], []]
+    for j in range(half):
+        head = side * half + j
+        base = j * span
+        query_rows = jnp.concatenate(
+            [
+                rows_of(q_ref, head),
+                in1_ref[base : base + TILE, :],
+                in2_ref[j * TILE : (j + 1) * TILE, :],
+                in3_ref[j * TILE : (j + 1) * TILE, :],
+            ],
+            axis=0,
+        )
+        key_rows = jnp.concatenate(
+            [
+                rows_of(k_ref, head),
+                in1_ref[base + TILE : base + 2 * TILE, :],
+                rows_of(ck_ref, head),
+                in1_ref[base + 3 * TILE : base + 3 * TILE + cache, :],
+            ],
+            axis=0,
+        )
+        value_rows = jnp.concatenate(
+            [
+                rows_of(v_ref, head),
+                in1_ref[base + 2 * TILE : base + 3 * TILE, :],
+                rows_of(cv_ref, head),
+                in1_ref[base + 3 * TILE + cache : base + 3 * TILE + 2 * cache, :],
+            ],
+            axis=0,
+        )
+        summed, logs = softmax_part(key_rows, value_rows, query_rows, fills)
+        rows = slice(j * HD, (j + 1) * HD)
+        own_ref[rows, :] = summed[:, :TILE]
+        own_log_ref[j : j + 1, :] = logs[:, :TILE]
+        for rel, out in ((1, out1_ref), (2, out2_ref), (3, out3_ref)):
+            cols = slice(rel * TILE, (rel + 1) * TILE)
+            out[rows, :] = summed[:, cols].astype(BF16)
+            rest = logs[:, cols]
+            for _ in range(3):
+                part = rest.astype(BF16).astype(F32)
+                stats[rel - 1].append(part)
+                rest = rest - part
+    spare = FLAG_ROWS - 3 * half
+    for rel, out in ((1, out1_ref), (2, out2_ref), (3, out3_ref)):
+        block = jnp.concatenate(stats[rel - 1] + [jnp.zeros((spare, TILE), F32)], axis=0)
+        out[half * HD : half * HD + FLAG_ROWS, :] = block.astype(BF16)
+
+
+def whole_kernel(
+    half, frames, frame_tok,
+    mask_ref, list_ref, place_ref, q_ref, k_ref, v_ref, ck_ref, cv_ref,
+    flags1_ref, flags2_ref, flags3_ref, in1_ref, in2_ref, in3_ref,
+    own_ref, out1_ref, out2_ref, out3_ref,
+):
+    me = lax.axis_index("seq")
+    cache = frames * frame_tok
+    flags = [own_flags(mask_ref, me)]
+    for ref in (flags1_ref, flags2_ref, flags3_ref):
+        row = ref.shape[0] - FLAG_ROWS
+        block = ref[row : row + FLAG_ROWS, :].astype(F32)
+        flags.append([block[key : key + 1, :] for key in range(4)])
+    fills = [(TILE, jnp.concatenate([flags[rel][key] for rel in range(4)], axis=1)) for key in range(4)]
+    for rel in range(4):
+        for value in frame_fills(place_ref, list_ref, jnp.bitwise_xor(me, rel), frames):
+            fills.append((frame_tok, value))
+    head = 2 * half + me
+    ins = (in1_ref, in2_ref, in3_ref)
+    end = 3 * TILE + cache
+    query_rows = jnp.concatenate([rows_of(q_ref, head)] + [ref[0:TILE, :] for ref in ins], axis=0)
+    key_rows = jnp.concatenate(
+        [rows_of(k_ref, head)] + [ref[TILE : 2 * TILE, :] for ref in ins]
+        + [rows_of(ck_ref, head)] + [ref[3 * TILE : end, :] for ref in ins],
+        axis=0,
+    )
+    value_rows = jnp.concatenate(
+        [rows_of(v_ref, head)] + [ref[2 * TILE : 3 * TILE, :] for ref in ins]
+        + [rows_of(cv_ref, head)] + [ref[end : end + cache, :] for ref in ins],
+        axis=0,
+    )
+    summed, _ = softmax_part(key_rows, value_rows, query_rows, fills)
+    for rel, out in enumerate((own_ref, out1_ref, out2_ref, out3_ref)):
+        out[...] = summed[:, rel * TILE : (rel + 1) * TILE].astype(BF16)
+
+
+def merge_kernel(
+    half,
+    own_ref, own_log_ref, in1_ref, in2_ref, in3_ref,
+    whole0_ref, whole1_ref, whole2_ref, whole3_ref,
+    out_ref,
+):
+    me = lax.axis_index("seq")
+    side = lax.rem(me, 2)
+
+    def logs_of(ref, j):
+        block = ref[half * HD : half * HD + FLAG_ROWS, :].astype(F32)
+        row = 3 * j
+        return block[row : row + 1, :] + block[row + 1 : row + 2, :] + block[row + 2 : row + 3, :]
+
+    def joined(first, first_log, second, second_log):
+        peak = jnp.maximum(first_log, second_log)
+        first_weight = jnp.exp2(first_log - peak)
+        second_weight = jnp.exp2(second_log - peak)
+        return (first * first_weight + second * second_weight) / (first_weight + second_weight)
+
+    for j in range(half):
+        rows = slice(j * HD, (j + 1) * HD)
+        near = joined(
+            own_ref[rows, :], own_log_ref[j : j + 1, :],
+            in2_ref[rows, :].astype(F32), logs_of(in2_ref, j),
+        )
+        out_ref[0, :, head_cols(side * half + j)] = near.T.astype(BF16)
+        far = joined(
+            in1_ref[rows, :].astype(F32), logs_of(in1_ref, j),
+            in3_ref[rows, :].astype(F32), logs_of(in3_ref, j),
+        )
+        out_ref[0, :, head_cols((1 - side) * half + j)] = far.T.astype(BF16)
+    for rel, ref in enumerate((whole0_ref, whole1_ref, whole2_ref, whole3_ref)):
+        block = ref[...].astype(F32).T.astype(BF16)
+        out_ref[0, :, head_cols(2 * half + jnp.bitwise_xor(me, rel))] = block
+
+
+def send(array, rel):
+    return lax.ppermute(array, "seq", [(i, i ^ rel) for i in range(4)])
+
+
+def exchanged(queries, keys, values, cache_keys, cache_values, frame_list, frame_place, tile_mask):
+    head_count = queries.shape[2] // HD
+    half = (head_count - 4) // 2
+    frames, frame_tok = cache_keys.shape[1:3]
+    span = 3 * TILE + 2 * frames * frame_tok
+    shape = jax.ShapeDtypeStruct
+    arrays = (queries, keys, values, cache_keys, cache_values)
+    packed = pl.pallas_call(
+        functools.partial(pack_kernel, half),
+        out_shape=(
+            shape((half * span + FLAG_ROWS, HD), BF16),
+            shape((half * TILE + FLAG_ROWS, HD), BF16),
+            shape((half * TILE + FLAG_ROWS, HD), BF16),
+        ) + (shape((span, HD), BF16),) * 3,
+        in_specs=[SMEM] + [VMEM] * 5,
+        out_specs=(VMEM,) * 6,
+    )(tile_mask, *arrays)
+    split_in = [send(packed[rel - 1], rel) for rel in (1, 2, 3)]
+    whole_in = [send(packed[rel + 2], rel) for rel in (1, 2, 3)]
+    own, own_log, *split_out = pl.pallas_call(
+        functools.partial(split_kernel, half, frames, frame_tok),
+        out_shape=(
+            shape((half * HD, TILE), F32),
+            shape((half, TILE), F32),
+        ) + (shape((half * HD + FLAG_ROWS, TILE), BF16),) * 3,
+        in_specs=[SMEM] * 3 + [VMEM] * 8,
+        out_specs=(VMEM,) * 5,
+    )(tile_mask, frame_list, frame_place, *arrays, *split_in)
+    split_back = [send(split_out[rel - 1], rel) for rel in (1, 2, 3)]
+    whole_out = pl.pallas_call(
+        functools.partial(whole_kernel, half, frames, frame_tok),
+        out_shape=(shape((HD, TILE), BF16),) * 4,
+        in_specs=[SMEM] * 3 + [VMEM] * 11,
+        out_specs=(VMEM,) * 4,
+    )(tile_mask, frame_list, frame_place, *arrays, *split_in, *whole_in)
+    whole_back = [whole_out[0]] + [send(whole_out[rel], rel) for rel in (1, 2, 3)]
+    return pl.pallas_call(
+        functools.partial(merge_kernel, half),
+        out_shape=shape(queries.shape, BF16),
+        in_specs=[VMEM] * 9,
+        out_specs=VMEM,
+    )(own, own_log, *split_back, *whole_back)
+
+
+def body(queries, keys, values, cache_keys, cache_values, frame_list, frame_place, tile_mask):
+    head_count = queries.shape[2] // HD
+    fits = (
+        lax.axis_size("seq") == 4
+        and queries.shape[0] == 1
+        and queries.shape[1] == TILE
+        and head_count % 2 == 0
+        and 6 <= head_count <= 14
+    )
+    run = exchanged if fits else gathered
+    return run(queries, keys, values, cache_keys, cache_values, frame_list, frame_place, tile_mask)
+
+
 def solution(mesh):
     return jax.shard_map(
         body,

time: 111 us -> 52.4 us (0.47)
  blocking collectives: 49 us -> 0 us
  starting transfers between devices: 0.08 us -> 19.2 us
  between operations: 14.9 us -> 0.09 us
  Pallas kernels: 0 us -> 11.2 us
  waiting for transfers between devices: 27 us -> 18.3 us
  matrix products: 5.99 us -> 0 us
  other arithmetic: 5.75 us -> 0 us
  local copies, waits for them, and re-layouts: 7.46 us -> 3.35 us
    all_gather x2 -> x0, blocking collectives: 49 us -> none  [the longest x1 27.2 us: body(): key_piece = lax.all_gather(cache_keys, 'seq', axis=1, tiled=True)]
    all_gather x2 -> x0, waiting for transfers between devices: 26.9 us -> none  [the longest x1 26.9 us: body(): value_piece = lax.all_gather(values, 'seq', axis=1, tiled=True)]
    ppermute x0 -> x12, starting transfers between devices: none -> 19.2 us  [send(): return lax.ppermute(array, 'seq', [(i, i ^ rel) for i in range(4)])]
    ppermute x0 -> x12, waiting for transfers between devices: none -> 18.3 us  [send(): return lax.ppermute(array, 'seq', [(i, i ^ rel) for i in range(4)])]
    pallas_call x0 -> x4, Pallas kernels: none -> 11.2 us  [the longest x1 3.64 us: exchanged(): pl.pallas_call(functools.partial(split_kernel, half, frames, frame_tok),...]
    dot_general x4 -> x0, matrix products: 5.99 us -> none  [the longest x2 3.49 us: update(): jnp.einsum('vhqk,vkhd->vhqd', weights.astype(jnp.bfloat16), value_heads,...]
    gather x1 -> x0, other arithmetic: 2.7 us -> none  [body(): tile_live = jnp.take(tile_mask, key_tiles, axis=2)]
    reduce_or x3 -> x0, other arithmetic: 1.61 us -> none  [the longest x2 1.53 us: attend(): return lax.cond(jnp.any(live), update, unchanged, running)]
  transfers between devices with their start and end apart: 2 -> 12, of which waited for: 1 -> 4; matrix products, arithmetic and copies ran while one was open for 10% -> 0% of each run, Pallas kernels for 0% -> 13%
where the time goes in v1:
time: 52.4 us; the launch traced here: 52.2 us
  starting transfers between devices  19.2 us (37%)
  waiting for transfers between devices  18.3 us (35%)
  Pallas kernels  11.2 us (21%)
  local copies, waits for them, and re-layouts  3.35 us (6%)
    ppermute x12, starting transfers between devices, send(): return lax.ppermute(array, 'seq', [(i, i ^ rel) for i in range(4)])  19.2 us
    ppermute x12, waiting for transfers between devices, send(): return lax.ppermute(array, 'seq', [(i, i ^ rel) for i in range(4)])  18.3 us
    pallas_call x1, Pallas kernels, exchanged(): pl.pallas_call(functools.partial(split_kernel, half, frames, frame_tok),...  3.64 us
    unnamed x24, local copies, waits for them, and re-layouts  3.35 us
    pallas_call x1, Pallas kernels, exchanged(): pl.pallas_call(functools.partial(whole_kernel, half, frames, frame_tok),...  3.06 us
    pallas_call x1, Pallas kernels, exchanged(): pl.pallas_call(functools.partial(pack_kernel, half), out_shape=(shape((ha...  2.42 us
    pallas_call x1, Pallas kernels, exchanged(): pl.pallas_call(functools.partial(merge_kernel, half), out_shape=shape(que...  2.09 us
  transfers between devices with their start and end apart: 12, of which 4 were waited for; matrix products, arithmetic and copies ran while one was open for 0% of the time, Pallas kernels for 13%

profile of v1, /device:TPU:0, one launch (start us, length us, event | category | flops | bytes accessed | tf_op | source)
XLA Modules:
  0.0 52.2 jit_solution(9247090923846418698)
XLA Ops:
  0.0 2.4 %shard_map.82 = (bf16[1552,128]{1,0:T(8,128)(2,1)}, bf16[400,128]{1,0:T(8,128)(2,1)}, bf16[400,128]{1,0:T(8,128)(2,1)}, bf16[512,128]{1,0:T(8,128)(2,1)}, bf16[5...) custom-call(s32[1,1,4]{2,1,0:T(1,128)} %mask_ref.5, bf16[1,128,1280]{2,1,0:T(8,128)(2,1)} %q_ref.5, ...), custom_call_target="tpu_custom_call" | custom-call | tf_op jit(solution)/shard_map/pallas_call | solution.py:320
  2.4 3.0 %collective-permute-start = (bf16[1552,128]{1,0:T(8,128)(2,1)}, bf16[1552,128]{1,0:T(8,128)(2,1)S(1)}, u32[]{:S(2)}, u32[]{:S(2)}) collective-permute-start(bf16[1552,128]{1,0:T(8,128)(2,1)} %get-tuple-element.20), channel_id=1, source_target_pairs={{0,4},{4,0},{8,12},{12,8},{1,5},{5,1},{9,13},{13,9},{2,6},{6,2},{1... | collective-permute-start | bytes 1191944 | tf_op jit(solution)/shard_map/ppermute | solution.py:310
  5.4 2.6 %collective-permute-start.1 = (bf16[400,128]{1,0:T(8,128)(2,1)}, bf16[400,128]{1,0:T(8,128)(2,1)S(1)}, u32[]{:S(2)}, u32[]{:S(2)}) collective-permute-start(bf16[400,128]{1,0:T(8,128)(2,1)} %get-tuple-element.21), channel_id=1, source_target_pairs={{0,8},{4,12},{8,0},{12,4},{1,9},{5,13},{9,1},{13,5},{2,10},{6,14},... | collective-permute-start | bytes 307208 | tf_op jit(solution)/shard_map/ppermute | solution.py:310
  8.0 0.4 collective-permute-start.6
  8.5 1.3 %collective-permute-start.2 = (bf16[400,128]{1,0:T(8,128)(2,1)}, bf16[400,128]{1,0:T(8,128)(2,1)S(1)}, u32[]{:S(2)}, u32[]{:S(2)}) collective-permute-start(bf16[400,128]{1,0:T(8,128)(2,1)} %get-tuple-element.22), channel_id=1, source_target_pairs={{0,12},{4,8},{8,4},{12,0},{1,13},{5,9},{9,5},{13,1},{2,14},{6,10},... | collective-permute-start | bytes 307208 | tf_op jit(solution)/shard_map/ppermute | solution.py:310
  9.8 1.7 %collective-permute-start.7 = (bf16[512,128]{1,0:T(8,128)(2,1)}, bf16[512,128]{1,0:T(8,128)(2,1)S(1)}, u32[]{:S(2)}, u32[]{:S(2)}) collective-permute-start(bf16[512,128]{1,0:T(8,128)(2,1)} %get-tuple-element.29), channel_id=1, source_target_pairs={{0,8},{4,12},{8,0},{12,4},{1,9},{5,13},{9,1},{13,5},{2,10},{6,14},... | collective-permute-start | bytes 393224 | tf_op jit(solution)/shard_map/ppermute | solution.py:310
  11.5 6.0 %collective-permute-done.1.in2_ref.flags2_ref = bf16[400,128]{1,0:T(8,128)(2,1)S(1)} collective-permute-done((bf16[400,128]{1,0:T(8,128)(2,1)}, bf16[400,128]{1,0:T(8,128)(2,1)S(1)}, u32[]{:S(2)}, u32[]{:S(2)}) %collective-permute-start.1) | collective-permute-done | bytes 102432 | tf_op jit(solution)/shard_map/ppermute | solution.py:310
  17.6 0.0 copy-start.1
  17.6 2.5 %collective-permute-start.8 = (bf16[512,128]{1,0:T(8,128)(2,1)}, bf16[512,128]{1,0:T(8,128)(2,1)S(1)}, u32[]{:S(2)}, u32[]{:S(2)}) collective-permute-start(bf16[512,128]{1,0:T(8,128)(2,1)} %get-tuple-element.30), channel_id=1, source_target_pairs={{0,12},{4,8},{8,4},{12,0},{1,13},{5,9},{9,5},{13,1},{2,14},{6,10},... | collective-permute-start | bytes 393224 | tf_op jit(solution)/shard_map/ppermute | solution.py:310
  20.0 5.5 %collective-permute-done.2.in3_ref.flags3_ref = bf16[400,128]{1,0:T(8,128)(2,1)S(1)} collective-permute-done((bf16[400,128]{1,0:T(8,128)(2,1)}, bf16[400,128]{1,0:T(8,128)(2,1)S(1)}, u32[]{:S(2)}, u32[]{:S(2)}) %collective-permute-start.2) | collective-permute-done | bytes 102432 | tf_op jit(solution)/shard_map/ppermute | solution.py:310
  25.5 0.0 copy-start.2
  25.5 0.0 collective-permute-done.in1_ref.flags1_ref
  25.5 0.0 copy-done.1
  25.5 0.6 %copy-done.2 = bf16[400,128]{1,0:T(8,128)(2,1)} copy-done((bf16[400,128]{1,0:T(8,128)(2,1)}, bf16[400,128]{1,0:T(8,128)(2,1)S(1)}, u32[]{:S(2)}) %copy-start.2) | copy-done | bytes 102424
  26.1 0.0 copy-start
  26.1 0.7 %copy-done = bf16[1552,128]{1,0:T(8,128)(2,1)} copy-done((bf16[1552,128]{1,0:T(8,128)(2,1)}, bf16[1552,128]{1,0:T(8,128)(2,1)S(1)}, u32[]{:S(2)}) %copy-start) | copy-done | bytes 397336
  26.9 3.6 %shard_map.83 = (f32[384,128]{1,0:T(8,128)}, f32[3,128]{1,0:T(4,128)}, bf16[400,128]{1,0:T(8,128)(2,1)}, bf16[400,128]{1,0:T(8,128)(2,1)}, bf16[400,128]{1,0:T(8,128)(2,1)}) custom-call(s32[1,1,4]{2,1,0:T(1,128)} %mask_ref.5, s32[1,3]{1,0:T(1,128)} %list_ref.3, s32[1,8]{1,0:T(1,128)} %place_ref.3, bf16[1,128,1280]{2,1,0:T(8,128)(2,1)} %q_ref.5, ...), custom_call_target="tpu_custom_call" | custom-call | tf_op jit(solution)/shard_map/pallas_call | solution.py:332
  30.5 0.0 collective-permute-start.3
  30.5 1.9 %collective-permute-start.4 = (bf16[400,128]{1,0:T(8,128)(2,1)}, bf16[400,128]{1,0:T(8,128)(2,1)S(1)}, u32[]{:S(2)}, u32[]{:S(2)}) collective-permute-start(bf16[400,128]{1,0:T(8,128)(2,1)} %get-tuple-element.26), channel_id=1, source_target_pairs={{0,8},{4,12},{8,0},{12,4},{1,9},{5,13},{9,1},{13,5},{2,10},{6,14},... | collective-permute-start | bytes 307208 | tf_op jit(solution)/shard_map/ppermute | solution.py:310
  32.4 0.0 collective-permute-done.6.in1_ref
  32.4 0.0 copy-start.3
  32.4 2.5 %collective-permute-start.5 = (bf16[400,128]{1,0:T(8,128)(2,1)}, bf16[400,128]{1,0:T(8,128)(2,1)S(1)}, u32[]{:S(2)}, u32[]{:S(2)}) collective-permute-start(bf16[400,128]{1,0:T(8,128)(2,1)} %get-tuple-element.27), channel_id=1, source_target_pairs={{0,12},{4,8},{8,4},{12,0},{1,13},{5,9},{9,5},{13,1},{2,14},{6,10},... | collective-permute-start | bytes 307208 | tf_op jit(solution)/shard_map/ppermute | solution.py:310
  34.9 0.0 collective-permute-done.7.in2_ref
  34.9 0.0 copy-start.4
  34.9 0.0 collective-permute-done.8.in3_ref
  34.9 0.0 copy-done.3
  34.9 0.6 %copy-done.4 = bf16[512,128]{1,0:T(8,128)(2,1)} copy-done((bf16[512,128]{1,0:T(8,128)(2,1)}, bf16[512,128]{1,0:T(8,128)(2,1)S(1)}, u32[]{:S(2)}) %copy-start.4) | copy-done | bytes 131096
  35.6 0.0 copy-start.5
  35.6 0.6 %copy-done.5 = bf16[512,128]{1,0:T(8,128)(2,1)} copy-done((bf16[512,128]{1,0:T(8,128)(2,1)}, bf16[512,128]{1,0:T(8,128)(2,1)S(1)}, u32[]{:S(2)}) %copy-start.5) | copy-done | bytes 131096
  36.2 3.1 %shard_map.84 = (bf16[128,128]{1,0:T(8,128)(2,1)}, bf16[128,128]{1,0:T(8,128)(2,1)}, bf16[128,128]{1,0:T(8,128)(2,1)}, bf16[128,128]{1,0:T(8,128)(2,1)}) custom-call(s32[1,1,4]{2,1,0:T(1,128)} %mask_ref.5, s32[1,3]{1,0:T(1,128)} %list_ref.3, s32[1,8]{1,0:T(1,128)} %place_ref.3, bf16[1,128,1280]{2,1,0:T(8,128)(2,1)} %q_ref.5, bf16[1,128,1280]{2,1,0:T(8,128)(2,1)} %k_ref.5, ...), custom_call_target="tpu_custom_call" | custom-call | tf_op jit(solution)/shard_map/pallas_call | solution.py:342
  39.3 0.0 collective-permute-start.9
  39.3 1.9 %collective-permute-start.10 = (bf16[128,128]{1,0:T(8,128)(2,1)}, bf16[128,128]{1,0:T(8,128)(2,1)S(1)}, u32[]{:S(2)}, u32[]{:S(2)}) collective-permute-start(bf16[128,128]{1,0:T(8,128)(2,1)} %get-tuple-element.33), channel_id=1, source_target_pairs={{0,8},{4,12},{8,0},{12,4},{1,9},{5,13},{9,1},{13,5},{2,10},{6,14},... | collective-permute-start | bytes 98312 | tf_op jit(solution)/shard_map/ppermute | solution.py:310
  41.2 2.2 %collective-permute-done.9.whole1_ref = bf16[128,128]{1,0:T(8,128)(2,1)S(1)} collective-permute-done((bf16[128,128]{1,0:T(8,128)(2,1)}, bf16[128,128]{1,0:T(8,128)(2,1)S(1)}, u32[]{:S(2)}, u32[]{:S(2)}) %collective-permute-start.9) | collective-permute-done | bytes 32800 | tf_op jit(solution)/shard_map/ppermute | solution.py:310
  43.4 0.0 copy-start.9
  43.4 1.3 %collective-permute-start.11 = (bf16[128,128]{1,0:T(8,128)(2,1)}, bf16[128,128]{1,0:T(8,128)(2,1)S(1)}, u32[]{:S(2)}, u32[]{:S(2)}) collective-permute-start(bf16[128,128]{1,0:T(8,128)(2,1)} %get-tuple-element.34), channel_id=1, source_target_pairs={{0,12},{4,8},{8,4},{12,0},{1,13},{5,9},{9,5},{13,1},{2,14},{6,10},... | collective-permute-start | bytes 98312 | tf_op jit(solution)/shard_map/ppermute | solution.py:310
  44.8 0.0 collective-permute-done.10.whole2_ref
  44.8 0.0 copy-start.10
  44.8 4.6 %collective-permute-done.11.whole3_ref = bf16[128,128]{1,0:T(8,128)(2,1)S(1)} collective-permute-done((bf16[128,128]{1,0:T(8,128)(2,1)}, bf16[128,128]{1,0:T(8,128)(2,1)S(1)}, u32[]{:S(2)}, u32[]{:S(2)}) %collective-permute-start.11) | collective-permute-done | bytes 32800 | tf_op jit(solution)/shard_map/ppermute | solution.py:310
  49.3 0.0 copy-start.11
  49.3 0.0 collective-permute-done.3.in1_ref
  49.3 0.0 copy-start.6
  49.4 0.0 collective-permute-done.4.in2_ref
  49.4 0.0 copy-start.7
  49.4 0.0 collective-permute-done.5.in3_ref
  49.4 0.0 copy-start.8
  49.4 0.0 copy-done.9
  49.4 0.0 copy-done.10
  49.4 0.5 %copy-done.11 = bf16[128,128]{1,0:T(8,128)(2,1)} copy-done((bf16[128,128]{1,0:T(8,128)(2,1)}, bf16[128,128]{1,0:T(8,128)(2,1)S(1)}, u32[]{:S(2)}) %copy-start.11) | copy-done | bytes 32792
  50.0 0.1 copy-done.6
  50.0 0.0 copy-done.7
  50.1 0.0 copy-done.8
  50.1 2.1 %shard_map.85 = bf16[1,128,1280]{2,1,0:T(8,128)(2,1)} custom-call(f32[384,128]{1,0:T(8,128)} %get-tuple-element.23.own_ref, f32[3,128]{1,0:T(4,128)} %get-tuple-element.24.own_log_ref, bf16[400,128]{1,0:T(8,128)(2,1)} %copy-done.6, bf16[400,128]{1,0:T(8,128)(2,1)} %copy-done.7, bf16[400,128]{1,0:T(8,128)(2,1)} %copy-done.8, ...), custom_call_target="tpu_custom_call" | custom-call | tf_op jit(solution)/shard_map/pallas_call | solution.py:349
Async XLA Ops:
  2.4 23.1 %collective-permute-start = (bf16[1552,128]{1,0:T(8,128)(2,1)}, bf16[1552,128]{1,0:T(8,128)(2,1)S(1)}, u32[]{:S(2)}, u32[]{:S(2)}) collective-permute-start(bf16[1552,128]{1,0:T(8,128)(2,1)} %get-tuple-element.20), channel_id=1, source_target_pairs={{0,4},{4,0},{8,12},{12,8},{1,5},{5,1},{9,13},{13,9},{2,6},{6,2},{1... | collective-permute-start | bytes 1191944 | tf_op jit(solution)/shard_map/ppermute | solution.py:310
  5.4 12.1 %collective-permute-start.1 = (bf16[400,128]{1,0:T(8,128)(2,1)}, bf16[400,128]{1,0:T(8,128)(2,1)S(1)}, u32[]{:S(2)}, u32[]{:S(2)}) collective-permute-start(bf16[400,128]{1,0:T(8,128)(2,1)} %get-tuple-element.21), channel_id=1, source_target_pairs={{0,8},{4,12},{8,0},{12,4},{1,9},{5,13},{9,1},{13,5},{2,10},{6,14},... | collective-permute-start | bytes 307208 | tf_op jit(solution)/shard_map/ppermute | solution.py:310
  8.0 24.4 %collective-permute-start.6 = (bf16[512,128]{1,0:T(8,128)(2,1)}, bf16[512,128]{1,0:T(8,128)(2,1)S(1)}, u32[]{:S(2)}, u32[]{:S(2)}) collective-permute-start(bf16[512,128]{1,0:T(8,128)(2,1)} %get-tuple-element.28), channel_id=1, source_target_pairs={{0,4},{4,0},{8,12},{12,8},{1,5},{5,1},{9,13},{13,9},{2,6},{6,2},{1... | collective-permute-start | bytes 393224 | tf_op jit(solution)/shard_map/ppermute | solution.py:310
  8.5 17.0 %collective-permute-start.2 = (bf16[400,128]{1,0:T(8,128)(2,1)}, bf16[400,128]{1,0:T(8,128)(2,1)S(1)}, u32[]{:S(2)}, u32[]{:S(2)}) collective-permute-start(bf16[400,128]{1,0:T(8,128)(2,1)} %get-tuple-element.22), channel_id=1, source_target_pairs={{0,12},{4,8},{8,4},{12,0},{1,13},{5,9},{9,5},{13,1},{2,14},{6,10},... | collective-permute-start | bytes 307208 | tf_op jit(solution)/shard_map/ppermute | solution.py:310
  9.8 25.1 %collective-permute-start.7 = (bf16[512,128]{1,0:T(8,128)(2,1)}, bf16[512,128]{1,0:T(8,128)(2,1)S(1)}, u32[]{:S(2)}, u32[]{:S(2)}) collective-permute-start(bf16[512,128]{1,0:T(8,128)(2,1)} %get-tuple-element.29), channel_id=1, source_target_pairs={{0,8},{4,12},{8,0},{12,4},{1,9},{5,13},{9,1},{13,5},{2,10},{6,14},... | collective-permute-start | bytes 393224 | tf_op jit(solution)/shard_map/ppermute | solution.py:310
  17.6 7.9 %copy-start.1 = (bf16[400,128]{1,0:T(8,128)(2,1)}, bf16[400,128]{1,0:T(8,128)(2,1)S(1)}, u32[]{:S(2)}) copy-start(bf16[400,128]{1,0:T(8,128)(2,1)S(1)} %collective-permute-done.1.in2_ref.flags2_ref) | copy-start | bytes 307204
  17.6 17.4 %collective-permute-start.8 = (bf16[512,128]{1,0:T(8,128)(2,1)}, bf16[512,128]{1,0:T(8,128)(2,1)S(1)}, u32[]{:S(2)}, u32[]{:S(2)}) collective-permute-start(bf16[512,128]{1,0:T(8,128)(2,1)} %get-tuple-element.30), channel_id=1, source_target_pairs={{0,12},{4,8},{8,4},{12,0},{1,13},{5,9},{9,5},{13,1},{2,14},{6,10},... | collective-permute-start | bytes 393224 | tf_op jit(solution)/shard_map/ppermute | solution.py:310
  25.5 0.6 %copy-start.2 = (bf16[400,128]{1,0:T(8,128)(2,1)}, bf16[400,128]{1,0:T(8,128)(2,1)S(1)}, u32[]{:S(2)}) copy-start(bf16[400,128]{1,0:T(8,128)(2,1)S(1)} %collective-permute-done.2.in3_ref.flags3_ref) | copy-start | bytes 307204
  26.1 0.7 %copy-start = (bf16[1552,128]{1,0:T(8,128)(2,1)}, bf16[1552,128]{1,0:T(8,128)(2,1)S(1)}, u32[]{:S(2)}) copy-start(bf16[1552,128]{1,0:T(8,128)(2,1)S(1)} %collective-permute-done.in1_ref.flags1_ref) | copy-start | bytes 1191940
  30.5 18.8 %collective-permute-start.3 = (bf16[400,128]{1,0:T(8,128)(2,1)}, bf16[400,128]{1,0:T(8,128)(2,1)S(1)}, u32[]{:S(2)}, u32[]{:S(2)}) collective-permute-start(bf16[400,128]{1,0:T(8,128)(2,1)} %get-tuple-element.25), channel_id=1, source_target_pairs={{0,4},{4,0},{8,12},{12,8},{1,5},{5,1},{9,13},{13,9},{2,6},{6,2},{1... | collective-permute-start | bytes 307208 | tf_op jit(solution)/shard_map/ppermute | solution.py:310
  30.5 18.8 %collective-permute-start.4 = (bf16[400,128]{1,0:T(8,128)(2,1)}, bf16[400,128]{1,0:T(8,128)(2,1)S(1)}, u32[]{:S(2)}, u32[]{:S(2)}) collective-permute-start(bf16[400,128]{1,0:T(8,128)(2,1)} %get-tuple-element.26), channel_id=1, source_target_pairs={{0,8},{4,12},{8,0},{12,4},{1,9},{5,13},{9,1},{13,5},{2,10},{6,14},... | collective-permute-start | bytes 307208 | tf_op jit(solution)/shard_map/ppermute | solution.py:310
  32.4 2.5 %copy-start.3 = (bf16[512,128]{1,0:T(8,128)(2,1)}, bf16[512,128]{1,0:T(8,128)(2,1)S(1)}, u32[]{:S(2)}) copy-start(bf16[512,128]{1,0:T(8,128)(2,1)S(1)} %collective-permute-done.6.in1_ref) | copy-start | bytes 393220
  32.4 16.9 %collective-permute-start.5 = (bf16[400,128]{1,0:T(8,128)(2,1)}, bf16[400,128]{1,0:T(8,128)(2,1)S(1)}, u32[]{:S(2)}, u32[]{:S(2)}) collective-permute-start(bf16[400,128]{1,0:T(8,128)(2,1)} %get-tuple-element.27), channel_id=1, source_target_pairs={{0,12},{4,8},{8,4},{12,0},{1,13},{5,9},{9,5},{13,1},{2,14},{6,10},... | collective-permute-start | bytes 307208 | tf_op jit(solution)/shard_map/ppermute | solution.py:310
  34.9 0.7 %copy-start.4 = (bf16[512,128]{1,0:T(8,128)(2,1)}, bf16[512,128]{1,0:T(8,128)(2,1)S(1)}, u32[]{:S(2)}) copy-start(bf16[512,128]{1,0:T(8,128)(2,1)S(1)} %collective-permute-done.7.in2_ref) | copy-start | bytes 393220
  35.6 0.6 %copy-start.5 = (bf16[512,128]{1,0:T(8,128)(2,1)}, bf16[512,128]{1,0:T(8,128)(2,1)S(1)}, u32[]{:S(2)}) copy-start(bf16[512,128]{1,0:T(8,128)(2,1)S(1)} %collective-permute-done.8.in3_ref) | copy-start | bytes 393220
  39.3 4.1 %collective-permute-start.9 = (bf16[128,128]{1,0:T(8,128)(2,1)}, bf16[128,128]{1,0:T(8,128)(2,1)S(1)}, u32[]{:S(2)}, u32[]{:S(2)}) collective-permute-start(bf16[128,128]{1,0:T(8,128)(2,1)} %get-tuple-element.32), channel_id=1, source_target_pairs={{0,4},{4,0},{8,12},{12,8},{1,5},{5,1},{9,13},{13,9},{2,6},{6,2},{1... | collective-permute-start | bytes 98312 | tf_op jit(solution)/shard_map/ppermute | solution.py:310
  39.3 5.5 %collective-permute-start.10 = (bf16[128,128]{1,0:T(8,128)(2,1)}, bf16[128,128]{1,0:T(8,128)(2,1)S(1)}, u32[]{:S(2)}, u32[]{:S(2)}) collective-permute-start(bf16[128,128]{1,0:T(8,128)(2,1)} %get-tuple-element.33), channel_id=1, source_target_pairs={{0,8},{4,12},{8,0},{12,4},{1,9},{5,13},{9,1},{13,5},{2,10},{6,14},... | collective-permute-start | bytes 98312 | tf_op jit(solution)/shard_map/ppermute | solution.py:310
  43.4 6.0 %copy-start.9 = (bf16[128,128]{1,0:T(8,128)(2,1)}, bf16[128,128]{1,0:T(8,128)(2,1)S(1)}, u32[]{:S(2)}) copy-start(bf16[128,128]{1,0:T(8,128)(2,1)S(1)} %collective-permute-done.9.whole1_ref) | copy-start | bytes 98308
  43.4 5.9 %collective-permute-start.11 = (bf16[128,128]{1,0:T(8,128)(2,1)}, bf16[128,128]{1,0:T(8,128)(2,1)S(1)}, u32[]{:S(2)}, u32[]{:S(2)}) collective-permute-start(bf16[128,128]{1,0:T(8,128)(2,1)} %get-tuple-element.34), channel_id=1, source_target_pairs={{0,12},{4,8},{8,4},{12,0},{1,13},{5,9},{9,5},{13,1},{2,14},{6,10},... | collective-permute-start | bytes 98312 | tf_op jit(solution)/shard_map/ppermute | solution.py:310
  44.8 4.6 %copy-start.10 = (bf16[128,128]{1,0:T(8,128)(2,1)}, bf16[128,128]{1,0:T(8,128)(2,1)S(1)}, u32[]{:S(2)}) copy-start(bf16[128,128]{1,0:T(8,128)(2,1)S(1)} %collective-permute-done.10.whole2_ref) | copy-start | bytes 98308
  49.3 0.6 %copy-start.11 = (bf16[128,128]{1,0:T(8,128)(2,1)}, bf16[128,128]{1,0:T(8,128)(2,1)S(1)}, u32[]{:S(2)}) copy-start(bf16[128,128]{1,0:T(8,128)(2,1)S(1)} %collective-permute-done.11.whole3_ref) | copy-start | bytes 98308
  49.3 0.7 %copy-start.6 = (bf16[400,128]{1,0:T(8,128)(2,1)}, bf16[400,128]{1,0:T(8,128)(2,1)S(1)}, u32[]{:S(2)}) copy-start(bf16[400,128]{1,0:T(8,128)(2,1)S(1)} %collective-permute-done.3.in1_ref) | copy-start | bytes 307204
  49.4 0.7 %copy-start.7 = (bf16[400,128]{1,0:T(8,128)(2,1)}, bf16[400,128]{1,0:T(8,128)(2,1)S(1)}, u32[]{:S(2)}) copy-start(bf16[400,128]{1,0:T(8,128)(2,1)S(1)} %collective-permute-done.4.in2_ref) | copy-start | bytes 307204
  49.4 0.7 %copy-start.8 = (bf16[400,128]{1,0:T(8,128)(2,1)}, bf16[400,128]{1,0:T(8,128)(2,1)S(1)}, u32[]{:S(2)}) copy-start(bf16[400,128]{1,0:T(8,128)(2,1)S(1)} %collective-permute-done.5.in3_ref) | copy-start | bytes 307204

commit v2 on v1

v2 whole, which is shorter than its diff:
```python
import functools
import math

import jax
import jax.numpy as jnp
from jax import lax
from jax.experimental import pallas as pl
from jax.experimental.pallas import tpu as pltpu
from jax.sharding import PartitionSpec as P

HD = 128
TILE = 128
NEG_FILL = -1e30
FACTOR = math.log2(math.e) / math.sqrt(HD)
FLAG_ROWS = 16
VMEM = pl.BlockSpec(memory_space=pltpu.VMEM)
SMEM = pl.BlockSpec(memory_space=pltpu.SMEM)
BF16 = jnp.bfloat16
F32 = jnp.float32


def attend(running, key_part, value_part, live, query_heads):
    videos, length, col_count = key_part.shape
    head_count = col_count // HD

    def update(previous):
        peak_old, total_old, summed_old = previous
        key_heads = key_part.reshape(videos, length, head_count, HD)
        value_heads = value_part.reshape(videos, length, head_count, HD)
        scores = jnp.einsum(
            "vqhd,vkhd->vhqk", query_heads, key_heads, preferred_element_type=jnp.float32
        ) * (1.0 / math.sqrt(HD))
        allowed = live[:, None, :, :]
        scores = jnp.where(allowed, scores, NEG_FILL)
        peak_new = jnp.maximum(peak_old, jnp.max(scores, axis=3))
        weights = jnp.where(allowed, jnp.exp(scores - peak_new[..., None]), 0.0)
        factor = jnp.exp(peak_old - peak_new)
        total_new = total_old * factor + jnp.sum(weights, axis=3)
        product = jnp.einsum(
            "vhqk,vkhd->vhqd",
            weights.astype(jnp.bfloat16),
            value_heads,
            preferred_element_type=jnp.float32,
        )
        summed_new = summed_old * factor[..., None] + product
        return (peak_new, total_new, summed_new)

    def unchanged(previous):
        return previous

    return lax.cond(jnp.any(live), update, unchanged, running)


def gathered(queries, keys, values, cache_keys, cache_values, frame_list, frame_place, tile_mask):
    videos, tok_rows, col_count = queries.shape
    head_count = col_count // HD
    query_heads = queries.reshape(videos, tok_rows, head_count, HD)
    running = (
        jnp.full((videos, head_count, tok_rows), NEG_FILL, jnp.float32),
        jnp.zeros((videos, head_count, tok_rows), jnp.float32),
        jnp.zeros((videos, head_count, tok_rows, HD), jnp.float32),
    )
    frame_tok = cache_keys.shape[2]
    listed = jnp.any(frame_place[:, :, None] == frame_list[:, None, :], axis=2)
    key_piece = lax.all_gather(cache_keys, "seq", axis=1, tiled=True)
    value_piece = lax.all_gather(cache_values, "seq", axis=1, tiled=True)
    count_frames = key_piece.shape[1]
    token_flags = jnp.repeat(listed, frame_tok, axis=1)
    live = jnp.broadcast_to(token_flags[:, None, :], (videos, tok_rows, count_frames * frame_tok))
    key_flat = key_piece.reshape(videos, count_frames * frame_tok, col_count)
    value_flat = value_piece.reshape(videos, count_frames * frame_tok, col_count)
    running = attend(running, key_flat, value_flat, live, query_heads)
    key_piece = lax.all_gather(keys, "seq", axis=1, tiled=True)
    value_piece = lax.all_gather(values, "seq", axis=1, tiled=True)
    length = key_piece.shape[1]
    key_tiles = jnp.arange(length, dtype=jnp.int32) // TILE
    tile_live = jnp.take(tile_mask, key_tiles, axis=2)
    running = attend(
        running, key_piece, value_piece, jnp.repeat(tile_live, TILE, axis=1) > 0, query_heads
    )
    peak, total, summed = running
    result = summed / total[..., None]
    return result.transpose(0, 2, 1, 3).reshape(videos, tok_rows, col_count).astype(jnp.bfloat16)


def head_cols(head):
    start = head * HD
    if not isinstance(head, int):
        start = pl.multiple_of(start, HD)
    return pl.ds(start, HD)


def fill(live):
    return jnp.where(live, 0.0, NEG_FILL)


def frame_fills(place_ref, list_ref, device, frames):
    out = []
    for slot in range(frames):
        held = place_ref[0, device * frames + slot]
        live = held == list_ref[0, 0]
        for entry in range(1, list_ref.shape[1]):
            live = live | (held == list_ref[0, entry])
        out.append(fill(live))
    return out


def rows_of(ref, head):
    if len(ref.shape) == 3:
        return ref[0, :, head_cols(head)]
    return ref[0, :, :, head_cols(head)].reshape(ref.shape[1] * ref.shape[2], HD)


def pack_kernel(
    half, mask_ref, q_ref, k_ref, v_ref, ck_ref, cv_ref,
    split0_ref, split1_ref, whole0_ref, whole1_ref, whole2_ref, whole3_ref,
):
    me = lax.axis_index("seq")
    side = lax.rem(me, 2)
    parts = (q_ref, k_ref, v_ref, ck_ref, cv_ref)
    for rel, out in enumerate((whole0_ref, whole1_ref, whole2_ref, whole3_ref)):
        other = jnp.bitwise_xor(me, rel)
        group = (1 - side) if rel % 2 else side
        row = 0
        for ref in parts:
            block = rows_of(ref, 2 * half + other)
            out[row : row + block.shape[0], :] = block
            row += block.shape[0]
        ident = lax.broadcasted_iota(jnp.int32, (FLAG_ROWS, HD), 0)
        block = jnp.zeros((FLAG_ROWS, HD), F32)
        for key in range(4):
            live = mask_ref[0, 0, jnp.bitwise_xor(other, key)] > 0
            block = jnp.where(ident == key, fill(live), block)
        out[row : row + FLAG_ROWS, :] = block.astype(BF16)
        row += FLAG_ROWS
        for j in range(half):
            if rel >= 2:
                out[row : row + TILE, :] = rows_of(q_ref, group * half + j)
                row += TILE
    for rel, out in enumerate((split0_ref, split1_ref)):
        group = (1 - side) if rel % 2 else side
        row = 0
        for j in range(half):
            for ref in parts:
                block = rows_of(ref, group * half + j)
                out[row : row + block.shape[0], :] = block
                row += block.shape[0]


def softmax_part(key_rows, value_rows, query_rows, fills):
    scores = lax.dot_general(
        key_rows, query_rows, (((1,), (1,)), ((), ())), preferred_element_type=F32
    )
    pieces = []
    row = 0
    for count, value in fills:
        pieces.append(scores[row : row + count, :] * FACTOR + value)
        row += count
    scores = jnp.concatenate(pieces, axis=0)
    peak = jnp.max(scores, axis=0, keepdims=True)
    weights = jnp.exp2(scores - peak)
    total = jnp.sum(weights, axis=0, keepdims=True)
    summed = lax.dot_general(
        value_rows, weights.astype(BF16), (((0,), (0,)), ((), ())), preferred_element_type=F32
    )
    return summed / total, peak + jnp.log2(total)


def query_fills(refs, row, keys):
    blocks = [ref[row : row + FLAG_ROWS, :].astype(F32) for ref in refs]
    return [
        (TILE, jnp.concatenate([block[key : key + 1, :] for block in blocks], axis=1))
        for key in range(keys)
    ]


def stack(refs, start, count):
    return jnp.concatenate([ref[start : start + count, :] for ref in refs], axis=0)


def whole_kernel(
    half, frames, frame_tok,
    list_ref, place_ref, in0_ref, in1_ref, in2_ref, in3_ref,
    own_ref, out1_ref, out2_ref, out3_ref,
):
    me = lax.axis_index("seq")
    cache = frames * frame_tok
    span = 3 * TILE + 2 * cache
    ins = (in0_ref, in1_ref, in2_ref, in3_ref)
    fills = query_fills(ins, span, 4)
    for rel in range(4):
        for value in frame_fills(place_ref, list_ref, jnp.bitwise_xor(me, rel), frames):
            fills.append((frame_tok, value))
    end = 3 * TILE + cache
    query_rows = stack(ins, 0, TILE)
    key_rows = jnp.concatenate([stack(ins, TILE, TILE), stack(ins, 3 * TILE, cache)], axis=0)
    value_rows = jnp.concatenate([stack(ins, 2 * TILE, TILE), stack(ins, end, cache)], axis=0)
    summed, _ = softmax_part(key_rows, value_rows, query_rows, fills)
    for rel, out in enumerate((own_ref, out1_ref, out2_ref, out3_ref)):
        out[...] = summed[:, rel * TILE : (rel + 1) * TILE].astype(BF16)


def split_kernel(
    half, frames, frame_tok,
    list_ref, place_ref, split0_ref, split1_ref,
    in0_ref, in1_ref, in2_ref, in3_ref, whole1_ref, whole2_ref, whole3_ref,
    own_ref, own_log_ref, out1_ref, out2_ref, out3_ref,
):
    me = lax.axis_index("seq")
    cache = frames * frame_tok
    span = 3 * TILE + 2 * cache
    fills = query_fills((in0_ref, in1_ref, in2_ref, in3_ref), span, 2)
    for rel in range(2):
        for value in frame_fills(place_ref, list_ref, jnp.bitwise_xor(me, rel), frames):
            fills.append((frame_tok, value))
    pair = (split0_ref, split1_ref)
    outs = (out1_ref, out2_ref, out3_ref)
    for out, ref in zip(outs, (whole1_ref, whole2_ref, whole3_ref)):
        out[0:HD, :] = ref[...]
    stats = [[], [], []]
    for j in range(half):
        base = j * span
        end = base + 3 * TILE + cache
        far = span + FLAG_ROWS + j * TILE
        query_rows = jnp.concatenate(
            [stack(pair, base, TILE), stack((in2_ref, in3_ref), far, TILE)], axis=0
        )
        key_rows = jnp.concatenate(
            [stack(pair, base + TILE, TILE), stack(pair, base + 3 * TILE, cache)], axis=0
        )
        value_rows = jnp.concatenate(
            [stack(pair, base + 2 * TILE, TILE), stack(pair, end, cache)], axis=0
        )
        summed, logs = softmax_part(key_rows, value_rows, query_rows, fills)
        own_ref[j * HD : (j + 1) * HD, :] = summed[:, :TILE]
        own_log_ref[j : j + 1, :] = logs[:, :TILE]
        for rel, out in enumerate(outs, 1):
            cols = slice(rel * TILE, (rel + 1) * TILE)
            out[(j + 1) * HD : (j + 2) * HD, :] = summed[:, cols].astype(BF16)
            rest = logs[:, cols]
            for _ in range(3):
                part = rest.astype(BF16).astype(F32)
                stats[rel - 1].append(part)
                rest = rest - part
    spare = FLAG_ROWS - 3 * half
    start = (half + 1) * HD
    for rel, out in enumerate(outs, 1):
        block = jnp.concatenate(stats[rel - 1] + [jnp.zeros((spare, TILE), F32)], axis=0)
        out[start : start + FLAG_ROWS, :] = block.astype(BF16)


def merge_kernel(
    half, own_ref, own_log_ref, whole_ref, in1_ref, in2_ref, in3_ref, out_ref,
):
    me = lax.axis_index("seq")
    side = lax.rem(me, 2)
    start = (half + 1) * HD

    def logs_of(ref, j):
        block = ref[start : start + FLAG_ROWS, :].astype(F32)
        row = 3 * j
        return block[row : row + 1, :] + block[row + 1 : row + 2, :] + block[row + 2 : row + 3, :]

    def joined(first, first_log, second, second_log):
        peak = jnp.maximum(first_log, second_log)
        first_weight = jnp.exp2(first_log - peak)
        second_weight = jnp.exp2(second_log - peak)
        return (first * first_weight + second * second_weight) / (first_weight + second_weight)

    for j in range(half):
        rows = slice((j + 1) * HD, (j + 2) * HD)
        close = joined(
            own_ref[j * HD : (j + 1) * HD, :], own_log_ref[j : j + 1, :],
            in2_ref[rows, :].astype(F32), logs_of(in2_ref, j),
        )
        out_ref[0, :, head_cols(side * half + j)] = close.T.astype(BF16)
        far = joined(
            in1_ref[rows, :].astype(F32), logs_of(in1_ref, j),
            in3_ref[rows, :].astype(F32), logs_of(in3_ref, j),
        )
        out_ref[0, :, head_cols((1 - side) * half + j)] = far.T.astype(BF16)
    for rel, ref in enumerate((whole_ref, in1_ref, in2_ref, in3_ref)):
        block = ref[0:HD, :].astype(F32).T.astype(BF16)
        out_ref[0, :, head_cols(2 * half + jnp.bitwise_xor(me, rel))] = block


def send(array, rel):
    return lax.ppermute(array, "seq", [(i, i ^ rel) for i in range(4)])


def near(array):
    return pltpu.with_memory_space_constraint(array, pltpu.VMEM)


def exchanged(queries, keys, values, cache_keys, cache_values, frame_list, frame_place, tile_mask):
    head_count = queries.shape[2] // HD
    half = (head_count - 4) // 2
    frames, frame_tok = cache_keys.shape[1:3]
    span = 3 * TILE + 2 * frames * frame_tok
    split_rows = half * span
    whole_rows = span + FLAG_ROWS
    both_rows = whole_rows + half * TILE
    split0, split1, *whole = pl.pallas_call(
        functools.partial(pack_kernel, half),
        out_shape=(pltpu.VMEM((split_rows, HD), BF16),) * 2
        + (pltpu.VMEM((whole_rows, HD), BF16),) * 2
        + (pltpu.VMEM((both_rows, HD), BF16),) * 2,
        in_specs=[SMEM] + [VMEM] * 5,
        out_specs=(VMEM,) * 6,
    )(tile_mask, queries, keys, values, cache_keys, cache_values)
    whole_in = [near(whole[0])] + [near(send(whole[rel], rel)) for rel in (1, 2, 3)]
    split_in = [near(split0), near(send(split1, 1))]
    whole_out = pl.pallas_call(
        functools.partial(whole_kernel, half, frames, frame_tok),
        out_shape=(pltpu.VMEM((HD, TILE), BF16),) * 4,
        in_specs=[SMEM] * 2 + [VMEM] * 4,
        out_specs=(VMEM,) * 4,
    )(frame_list, frame_place, *whole_in)
    whole_out = [near(array) for array in whole_out]
    own, own_log, *back = pl.pallas_call(
        functools.partial(split_kernel, half, frames, frame_tok),
        out_shape=(
            pltpu.VMEM((half * HD, TILE), F32),
            pltpu.VMEM((half, TILE), F32),
        ) + (pltpu.VMEM(((half + 1) * HD + FLAG_ROWS, TILE), BF16),) * 3,
        in_specs=[SMEM] * 2 + [VMEM] * 9,
        out_specs=(VMEM,) * 5,
    )(frame_list, frame_place, *split_in, *whole_in, *whole_out[1:])
    back = [near(send(back[rel - 1], rel)) for rel in (1, 2, 3)]
    return pl.pallas_call(
        functools.partial(merge_kernel, half),
        out_shape=jax.ShapeDtypeStruct(queries.shape, BF16),
        in_specs=[VMEM] * 6,
        out_specs=VMEM,
    )(near(own), near(own_log), whole_out[0], *back)


def body(queries, keys, values, cache_keys, cache_values, frame_list, frame_place, tile_mask):
    head_count = queries.shape[2] // HD
    fits = (
        lax.axis_size("seq") == 4
        and queries.shape[0] == 1
        and queries.shape[1] == TILE
        and head_count % 2 == 0
        and 6 <= head_count <= 14
    )
    run = exchanged if fits else gathered
    return run(queries, keys, values, cache_keys, cache_values, frame_list, frame_place, tile_mask)


def solution(mesh):
    return jax.shard_map(
        body,
        mesh=mesh,
        in_specs=(
            P(("groups", "batch"), "seq", "head"),
            P(("groups", "batch"), "seq", "head"),
            P(("groups", "batch"), "seq", "head"),
            P(("groups", "batch"), "seq", None, "head"),
            P(("groups", "batch"), "seq", None, "head"),
            P(("groups", "batch"), None),
            P(("groups", "batch"), None),
            P(("groups", "batch"), "seq", None),
        ),
        out_specs=P(("groups", "batch"), "seq", "head"),
        check_vma=False,
    )
```

time: 52.4 us -> 45.6 us (0.87)
  waiting for transfers between devices: 18.3 us -> 28.3 us
  starting transfers between devices: 19.2 us -> 11 us
  Pallas kernels: 11.2 us -> 6.08 us
  local copies, waits for them, and re-layouts: 3.35 us -> 0 us
    ppermute x12 -> x7, waiting for transfers between devices: 18.3 us -> 28.3 us  [send(): return lax.ppermute(array, 'seq', [(i, i ^ rel) for i in range(4)])]
    ppermute x12 -> x7, starting transfers between devices: 19.2 us -> 11 us  [send(): return lax.ppermute(array, 'seq', [(i, i ^ rel) for i in range(4)])]
    unnamed x24 -> x0, local copies, waits for them, and re-layouts: 3.35 us -> none
    pallas_call x2, Pallas kernels: 4.51 us -> 2.54 us  [the longest x1 1.58 us: exchanged(): pl.pallas_call(functools.partial(pack_kernel, half), out_shape=(pltpu.VME...]
    pallas_call x1, Pallas kernels: 3.06 us -> 1.47 us  [exchanged(): pl.pallas_call(functools.partial(whole_kernel, half, frames, frame_tok),...]
    pallas_call x1, Pallas kernels: 3.64 us -> 2.08 us  [exchanged(): pl.pallas_call(functools.partial(split_kernel, half, frames, frame_tok),...]
  transfers between devices with their start and end apart: 12 -> 7, of which waited for: 4 -> 4; matrix products, arithmetic and copies ran while one was open for 0% -> 0% of each run, Pallas kernels for 13% -> 3%
where the time goes in v2:
time: 45.6 us; the launch traced here: 45.4 us
  waiting for transfers between devices  28.3 us (62%)
  starting transfers between devices  11 us (24%)
  Pallas kernels  6.08 us (13%)
    ppermute x7, waiting for transfers between devices, send(): return lax.ppermute(array, 'seq', [(i, i ^ rel) for i in range(4)])  28.3 us
    ppermute x7, starting transfers between devices, send(): return lax.ppermute(array, 'seq', [(i, i ^ rel) for i in range(4)])  11 us
    pallas_call x1, Pallas kernels, exchanged(): pl.pallas_call(functools.partial(split_kernel, half, frames, frame_tok),...  2.08 us
    pallas_call x1, Pallas kernels, exchanged(): pl.pallas_call(functools.partial(pack_kernel, half), out_shape=(pltpu.VME...  1.58 us
    pallas_call x1, Pallas kernels, exchanged(): pl.pallas_call(functools.partial(whole_kernel, half, frames, frame_tok),...  1.47 us
    pallas_call x1, Pallas kernels, exchanged(): pl.pallas_call(functools.partial(merge_kernel, half), out_shape=jax.Shape...  0.96 us
  transfers between devices with their start and end apart: 7, of which 4 were waited for; matrix products, arithmetic and copies ran while one was open for 0% of the time, Pallas kernels for 3%

profile of v2, /device:TPU:0, one launch (start us, length us, event | category | flops | bytes accessed | tf_op | source)
XLA Modules:
  0.0 45.4 jit_solution(1912639741720048187)
XLA Ops:
  0.0 1.6 %shard_map.82 = (bf16[1536,128]{1,0:T(8,128)(2,1)S(1)}, bf16[1536,128]{1,0:T(8,128)(2,1)S(1)}, bf16[528,128]{1,0:T(8,128)(2,1)S(1)}, bf16[528,128]{1,0:T(8,128)(...) custom-call(s32[1,1,4]{2,1,0:T(1,128)} %mask_ref.1, bf16[1,128,1280]{2,1,0:T(8,128)(2,1)} %q_ref.1, ...), custom_call_target="tpu_custom_call" | custom-call | tf_op jit(solution)/shard_map/pallas_call | solution.py:303
  1.6 3.1 %collective-permute-start = (bf16[1536,128]{1,0:T(8,128)(2,1)S(1)}, bf16[1536,128]{1,0:T(8,128)(2,1)S(1)}, u32[]{:S(2)}, u32[]{:S(2)}) collective-permute-start(bf16[1536,128]{1,0:T(8,128)(2,1)S(1)} %get-tuple-element.21), channel_id=1, source_target_pairs={{0,4},{4,0},{8,12},{12,8},{1,5},{5,1},{9,13},{13,9},{2,6},{6,2},{1... | collective-permute-start | bytes 1179656 | tf_op jit(solution)/shard_map/ppermute | solution.py:288
  4.7 2.6 %collective-permute-start.2 = (bf16[912,128]{1,0:T(8,128)(2,1)S(1)}, bf16[912,128]{1,0:T(8,128)(2,1)S(1)}, u32[]{:S(2)}, u32[]{:S(2)}) collective-permute-start(bf16[912,128]{1,0:T(8,128)(2,1)S(1)} %get-tuple-element.24), channel_id=1, source_target_pairs={{0,8},{4,12},{8,0},{12,4},{1,9},{5,13},{9,1},{13,5},{2,10},{6,14},... | collective-permute-start | bytes 700424 | tf_op jit(solution)/shard_map/ppermute | solution.py:288
  7.3 0.0 collective-permute-start.3
  7.3 0.9 %collective-permute-start.1 = (bf16[528,128]{1,0:T(8,128)(2,1)S(1)}, bf16[528,128]{1,0:T(8,128)(2,1)S(1)}, u32[]{:S(2)}, u32[]{:S(2)}) collective-permute-start(bf16[528,128]{1,0:T(8,128)(2,1)S(1)} %get-tuple-element.23), channel_id=1, source_target_pairs={{0,4},{4,0},{8,12},{12,8},{1,5},{5,1},{9,13},{13,9},{2,6},{6,2},{1... | collective-permute-start | bytes 405512 | tf_op jit(solution)/shard_map/ppermute | solution.py:288
  8.2 18.0 %collective-permute-done.1.in1_ref = bf16[528,128]{1,0:T(8,128)(2,1)S(1)} collective-permute-done((bf16[528,128]{1,0:T(8,128)(2,1)S(1)}, bf16[528,128]{1,0:T(8,128)(2,1)S(1)}, u32[]{:S(2)}, u32[]{:S(2)}) %collective-permute-start.1) | collective-permute-done | bytes 135200 | tf_op jit(solution)/shard_map/ppermute | solution.py:288
  26.2 0.0 collective-permute-done.2.in2_ref
  26.2 1.1 %collective-permute-done.3.in3_ref = bf16[912,128]{1,0:T(8,128)(2,1)S(1)} collective-permute-done((bf16[912,128]{1,0:T(8,128)(2,1)S(1)}, bf16[912,128]{1,0:T(8,128)(2,1)S(1)}, u32[]{:S(2)}, u32[]{:S(2)}) %collective-permute-start.3) | collective-permute-done | bytes 233504 | tf_op jit(solution)/shard_map/ppermute | solution.py:288
  27.2 1.5 %shard_map.83 = (bf16[128,128]{1,0:T(8,128)(2,1)S(1)}, bf16[128,128]{1,0:T(8,128)(2,1)S(1)}, bf16[128,128]{1,0:T(8,128)(2,1)S(1)}, bf16[128,128]{1,0:T(8,128)(2,1)S(1)}) custom-call(s32[1,3]{1,0:T(1,128)} %list_ref.3, s32[1,8]{1,0:T(1,128)} %place_ref.3, bf16[528,128]{1,0:T(8,128)(2,1)S(1)} %get-tuple-element.22.in0_ref, ...), custom_call_target="tpu_custom_call" | custom-call | tf_op jit(solution)/shard_map/pallas_call | solution.py:313
  28.7 0.0 collective-permute-done.split1_ref
  28.7 2.1 %shard_map.84 = (f32[384,128]{1,0:T(8,128)S(1)}, f32[3,128]{1,0:T(4,128)S(1)}, bf16[528,128]{1,0:T(8,128)(2,1)S(1)}, bf16[528,128]{1,0:T(8,128)(2,1)S(1)}, bf16[528,128]{1,0:T(8,128)(2,1)S(1)}) custom-call(s32[1,3]{1,0:T(1,128)} %list_ref.3, s32[1,8]{1,0:T(1,128)} %place_ref.3, bf16[1536,128]{1,0:T(8,128)(2,1)S(1)} %get-tuple-element.20.split0_ref, ...), custom_call_target="tpu_custom_call" | custom-call | tf_op jit(solution)/shard_map/pallas_call | solution.py:320
  30.8 1.4 %collective-permute-start.4 = (bf16[528,128]{1,0:T(8,128)(2,1)S(1)}, bf16[528,128]{1,0:T(8,128)(2,1)S(1)}, u32[]{:S(2)}, u32[]{:S(2)}) collective-permute-start(bf16[528,128]{1,0:T(8,128)(2,1)S(1)} %get-tuple-element.32), channel_id=1, source_target_pairs={{0,4},{4,0},{8,12},{12,8},{1,5},{5,1},{9,13},{13,9},{2,6},{6,2},{1... | collective-permute-start | bytes 405512 | tf_op jit(solution)/shard_map/ppermute | solution.py:288
  32.2 2.5 %collective-permute-start.5 = (bf16[528,128]{1,0:T(8,128)(2,1)S(1)}, bf16[528,128]{1,0:T(8,128)(2,1)S(1)}, u32[]{:S(2)}, u32[]{:S(2)}) collective-permute-start(bf16[528,128]{1,0:T(8,128)(2,1)S(1)} %get-tuple-element.33), channel_id=1, source_target_pairs={{0,8},{4,12},{8,0},{12,4},{1,9},{5,13},{9,1},{13,5},{2,10},{6,14},... | collective-permute-start | bytes 405512 | tf_op jit(solution)/shard_map/ppermute | solution.py:288
  34.7 0.6 %collective-permute-start.6 = (bf16[528,128]{1,0:T(8,128)(2,1)S(1)}, bf16[528,128]{1,0:T(8,128)(2,1)S(1)}, u32[]{:S(2)}, u32[]{:S(2)}) collective-permute-start(bf16[528,128]{1,0:T(8,128)(2,1)S(1)} %get-tuple-element.34), channel_id=1, source_target_pairs={{0,12},{4,8},{8,4},{12,0},{1,13},{5,9},{9,5},{13,1},{2,14},{6,10},... | collective-permute-start | bytes 405512 | tf_op jit(solution)/shard_map/ppermute | solution.py:288
  35.3 2.1 %collective-permute-done.4.in1_ref = bf16[528,128]{1,0:T(8,128)(2,1)S(1)} collective-permute-done((bf16[528,128]{1,0:T(8,128)(2,1)S(1)}, bf16[528,128]{1,0:T(8,128)(2,1)S(1)}, u32[]{:S(2)}, u32[]{:S(2)}) %collective-permute-start.4) | collective-permute-done | bytes 135200 | tf_op jit(solution)/shard_map/ppermute | solution.py:288
  37.4 7.1 %collective-permute-done.5.in2_ref = bf16[528,128]{1,0:T(8,128)(2,1)S(1)} collective-permute-done((bf16[528,128]{1,0:T(8,128)(2,1)S(1)}, bf16[528,128]{1,0:T(8,128)(2,1)S(1)}, u32[]{:S(2)}, u32[]{:S(2)}) %collective-permute-start.5) | collective-permute-done | bytes 135200 | tf_op jit(solution)/shard_map/ppermute | solution.py:288
  44.5 0.0 collective-permute-done.6.in3_ref
  44.5 1.0 %shard_map.85 = bf16[1,128,1280]{2,1,0:T(8,128)(2,1)} custom-call(f32[384,128]{1,0:T(8,128)S(1)} %get-tuple-element.29.own_ref, f32[3,128]{1,0:T(4,128)S(1)} %get-tuple-element.30.own_log_ref, bf16[128,128]{1,0:T(8,128)(2,1)S(1)} %get-tuple-element.31.whole_ref, bf16[528,128]{1,0:T(8,128)(2,1)S(1)} %collective-permute-done.4.in1_ref, ...), custom_call_target="tpu_custom_call" | custom-call | tf_op jit(solution)/shard_map/pallas_call | solution.py:330
Async XLA Ops:
  1.6 27.1 %collective-permute-start = (bf16[1536,128]{1,0:T(8,128)(2,1)S(1)}, bf16[1536,128]{1,0:T(8,128)(2,1)S(1)}, u32[]{:S(2)}, u32[]{:S(2)}) collective-permute-start(bf16[1536,128]{1,0:T(8,128)(2,1)S(1)} %get-tuple-element.21), channel_id=1, source_target_pairs={{0,4},{4,0},{8,12},{12,8},{1,5},{5,1},{9,13},{13,9},{2,6},{6,2},{1... | collective-permute-start | bytes 1179656 | tf_op jit(solution)/shard_map/ppermute | solution.py:288
  4.7 21.5 %collective-permute-start.2 = (bf16[912,128]{1,0:T(8,128)(2,1)S(1)}, bf16[912,128]{1,0:T(8,128)(2,1)S(1)}, u32[]{:S(2)}, u32[]{:S(2)}) collective-permute-start(bf16[912,128]{1,0:T(8,128)(2,1)S(1)} %get-tuple-element.24), channel_id=1, source_target_pairs={{0,8},{4,12},{8,0},{12,4},{1,9},{5,13},{9,1},{13,5},{2,10},{6,14},... | collective-permute-start | bytes 700424 | tf_op jit(solution)/shard_map/ppermute | solution.py:288
  7.3 20.0 %collective-permute-start.3 = (bf16[912,128]{1,0:T(8,128)(2,1)S(1)}, bf16[912,128]{1,0:T(8,128)(2,1)S(1)}, u32[]{:S(2)}, u32[]{:S(2)}) collective-permute-start(bf16[912,128]{1,0:T(8,128)(2,1)S(1)} %get-tuple-element.25), channel_id=1, source_target_pairs={{0,12},{4,8},{8,4},{12,0},{1,13},{5,9},{9,5},{13,1},{2,14},{6,10},... | collective-permute-start | bytes 700424 | tf_op jit(solution)/shard_map/ppermute | solution.py:288
  7.3 18.9 %collective-permute-start.1 = (bf16[528,128]{1,0:T(8,128)(2,1)S(1)}, bf16[528,128]{1,0:T(8,128)(2,1)S(1)}, u32[]{:S(2)}, u32[]{:S(2)}) collective-permute-start(bf16[528,128]{1,0:T(8,128)(2,1)S(1)} %get-tuple-element.23), channel_id=1, source_target_pairs={{0,4},{4,0},{8,12},{12,8},{1,5},{5,1},{9,13},{13,9},{2,6},{6,2},{1... | collective-permute-start | bytes 405512 | tf_op jit(solution)/shard_map/ppermute | solution.py:288
  30.8 6.6 %collective-permute-start.4 = (bf16[528,128]{1,0:T(8,128)(2,1)S(1)}, bf16[528,128]{1,0:T(8,128)(2,1)S(1)}, u32[]{:S(2)}, u32[]{:S(2)}) collective-permute-start(bf16[528,128]{1,0:T(8,128)(2,1)S(1)} %get-tuple-element.32), channel_id=1, source_target_pairs={{0,4},{4,0},{8,12},{12,8},{1,5},{5,1},{9,13},{13,9},{2,6},{6,2},{1... | collective-permute-start | bytes 405512 | tf_op jit(solution)/shard_map/ppermute | solution.py:288
  32.2 12.3 %collective-permute-start.5 = (bf16[528,128]{1,0:T(8,128)(2,1)S(1)}, bf16[528,128]{1,0:T(8,128)(2,1)S(1)}, u32[]{:S(2)}, u32[]{:S(2)}) collective-permute-start(bf16[528,128]{1,0:T(8,128)(2,1)S(1)} %get-tuple-element.33), channel_id=1, source_target_pairs={{0,8},{4,12},{8,0},{12,4},{1,9},{5,13},{9,1},{13,5},{2,10},{6,14},... | collective-permute-start | bytes 405512 | tf_op jit(solution)/shard_map/ppermute | solution.py:288
  34.7 9.8 %collective-permute-start.6 = (bf16[528,128]{1,0:T(8,128)(2,1)S(1)}, bf16[528,128]{1,0:T(8,128)(2,1)S(1)}, u32[]{:S(2)}, u32[]{:S(2)}) collective-permute-start(bf16[528,128]{1,0:T(8,128)(2,1)S(1)} %get-tuple-element.34), channel_id=1, source_target_pairs={{0,12},{4,8},{8,4},{12,0},{1,13},{5,9},{9,5},{13,1},{2,14},{6,10},... | collective-permute-start | bytes 405512 | tf_op jit(solution)/shard_map/ppermute | solution.py:288

commit v3 on v0

--- a/solution.py
+++ b/solution.py
@@ -1,15 +1,22 @@
+import functools
 import math
 
 import jax
 import jax.numpy as jnp
 from jax import lax
+from jax.experimental import pallas as pl
+from jax.experimental.pallas import tpu as pltpu
 from jax.sharding import PartitionSpec as P
 
 HD = 128
 TILE = 128
-
-
 NEG_FILL = -1e30
+FACTOR = math.log2(math.e) / math.sqrt(HD)
+FLAG_ROWS = 16
+VMEM = pl.BlockSpec(memory_space=pltpu.VMEM)
+SMEM = pl.BlockSpec(memory_space=pltpu.SMEM)
+BF16 = jnp.bfloat16
+F32 = jnp.float32
 
 
 def attend(running, key_part, value_part, live, query_heads):
@@ -44,7 +51,7 @@
     return lax.cond(jnp.any(live), update, unchanged, running)
 
 
-def body(queries, keys, values, cache_keys, cache_values, frame_list, frame_place, tile_mask):
+def gathered(queries, keys, values, cache_keys, cache_values, frame_list, frame_place, tile_mask):
     videos, tok_rows, col_count = queries.shape
     head_count = col_count // HD
     query_heads = queries.reshape(videos, tok_rows, head_count, HD)
@@ -76,6 +83,280 @@
     return result.transpose(0, 2, 1, 3).reshape(videos, tok_rows, col_count).astype(jnp.bfloat16)
 
 
+def head_cols(head):
+    start = head * HD
+    if not isinstance(head, int):
+        start = pl.multiple_of(start, HD)
+    return pl.ds(start, HD)
+
+
+def fill(live):
+    return jnp.where(live, 0.0, NEG_FILL)
+
+
+def frame_fills(place_ref, list_ref, device, frames):
+    out = []
+    for slot in range(frames):
+        held = place_ref[0, device * frames + slot]
+        live = held == list_ref[0, 0]
+        for entry in range(1, list_ref.shape[1]):
+            live = live | (held == list_ref[0, entry])
+        out.append(fill(live))
+    return out
+
+
+def rows_of(ref, head):
+    if len(ref.shape) == 3:
+        return ref[0, :, head_cols(head)]
+    return ref[0, :, :, head_cols(head)].reshape(ref.shape[1] * ref.shape[2], HD)
+
+
+def put(out, row, refs, head):
+    for ref in refs:
+        block = rows_of(ref, head)
+        out[row : row + block.shape[0], :] = block
+        row += block.shape[0]
+    return row
+
+
+def pack_kernel(
+    half, mask_ref, q_ref, k_ref, v_ref, ck_ref, cv_ref, near0_ref, near1_ref, far2_ref, far3_ref
+):
+    me = lax.axis_index("seq")
+    side = lax.rem(me, 2)
+    parts = (q_ref, k_ref, v_ref, ck_ref, cv_ref)
+    for rel, out in enumerate((near0_ref, near1_ref, far2_ref, far3_ref)):
+        other = jnp.bitwise_xor(me, rel)
+        group = (1 - side) if rel % 2 else side
+        row = 0
+        for j in range(half):
+            row = put(out, row, parts if rel < 2 else parts[:1], group * half + j)
+        row = put(out, row, parts, 2 * half + other)
+        ident = lax.broadcasted_iota(jnp.int32, (FLAG_ROWS, HD), 0)
+        block = jnp.zeros((FLAG_ROWS, HD), F32)
+        for key in range(4):
+            live = mask_ref[0, 0, jnp.bitwise_xor(other, key)] > 0
+            block = jnp.where(ident == key, fill(live), block)
+        out[row : row + FLAG_ROWS, :] = block.astype(BF16)
+
+
+def eights(block, reduce):
+    return reduce(block.reshape(block.shape[0] // 8, 8, block.shape[1]), axis=0)
+
+
+def softmax(scores, fills):
+    peak = None
+    row = 0
+    for count, value in fills:
+        block = eights(scores[row : row + count, :], jnp.max) * FACTOR + value
+        peak = block if peak is None else jnp.maximum(peak, block)
+        row += count
+    peak = jnp.max(peak, axis=0, keepdims=True)
+    weights = []
+    total = None
+    row = 0
+    for count, value in fills:
+        block = jnp.exp2(scores[row : row + count, :] * FACTOR - (peak - 2.0 * value))
+        part = eights(block, jnp.sum)
+        total = part if total is None else total + part
+        weights.append(block.astype(BF16))
+        row += count
+    total = jnp.sum(total, axis=0, keepdims=True)
+    total = jnp.where(total == 0.0, 1.0, total)
+    return jnp.concatenate(weights, axis=0), 1.0 / total, peak + jnp.log2(total)
+
+
+def all_fills(refs, keys, frames, frame_tok, list_ref, place_ref, me):
+    blocks = []
+    for ref in refs:
+        row = ref.shape[0] - FLAG_ROWS
+        blocks.append(ref[row : row + FLAG_ROWS, :].astype(F32))
+    fills = [
+        (TILE, jnp.concatenate([block[key : key + 1, :] for block in blocks], axis=1))
+        for key in range(keys)
+    ]
+    for rel in range(keys):
+        for value in frame_fills(place_ref, list_ref, jnp.bitwise_xor(me, rel), frames):
+            fills.append((frame_tok, value))
+    return fills
+
+
+def stack(places, start, count):
+    return jnp.concatenate(
+        [ref[base + start : base + start + count, :] for ref, base in places], axis=0
+    )
+
+
+def attend_parts(tasks, cache):
+    scores = []
+    for query_places, key_places, _ in tasks:
+        key_rows = jnp.concatenate(
+            [stack(key_places, TILE, TILE), stack(key_places, 3 * TILE, cache)], axis=0
+        )
+        scores.append(
+            lax.dot_general(
+                key_rows, stack(query_places, 0, TILE), (((1,), (1,)), ((), ())),
+                preferred_element_type=F32,
+            )
+        )
+    softmaxed = [softmax(block, fills) for block, (_, _, fills) in zip(scores, tasks)]
+    out = []
+    for (weights, scale, logs), (_, key_places, _) in zip(softmaxed, tasks):
+        value_rows = jnp.concatenate(
+            [stack(key_places, 2 * TILE, TILE), stack(key_places, 3 * TILE + cache, cache)], axis=0
+        )
+        summed = lax.dot_general(
+            value_rows, weights, (((0,), (0,)), ((), ())), preferred_element_type=F32
+        )
+        out.append((summed * scale, logs))
+    return out
+
+
+def three_parts(row):
+    parts = []
+    for _ in range(3):
+        part = row.astype(BF16).astype(F32)
+        parts.append(part)
+        row = row - part
+    return parts
+
+
+def stat_block(rows):
+    spare = FLAG_ROWS - len(rows)
+    return jnp.concatenate(rows + [jnp.zeros((spare, TILE), F32)], axis=0).astype(BF16)
+
+
+def attend_kernel(
+    half, frames, frame_tok,
+    list_ref, place_ref, near0_ref, near1_ref, far3_ref, far2_ref,
+    own_ref, own_log_ref, whole_ref, out1_ref, out2_ref, out3_ref,
+):
+    me = lax.axis_index("seq")
+    cache = frames * frame_tok
+    span = 3 * TILE + 2 * cache
+    ins = (near0_ref, near1_ref, far2_ref, far3_ref)
+    outs = (out1_ref, out2_ref, out3_ref)
+    fills = all_fills(ins, 4, frames, frame_tok, list_ref, place_ref, me)
+    pair_fills = fills[:2] + fills[4 : 4 + 2 * frames]
+    tasks = []
+    for j in range(half):
+        pair = ((near0_ref, j * span), (near1_ref, j * span))
+        tasks.append((pair + ((far2_ref, j * TILE), (far3_ref, j * TILE)), pair, pair_fills))
+    places = [(ref, half * span) for ref in ins[:2]] + [(ref, half * TILE) for ref in ins[2:]]
+    tasks.append((places, places, fills))
+    *parts, (whole, _) = attend_parts(tasks, cache)
+    stats = [[], [], []]
+    for j, (summed, logs) in enumerate(parts):
+        rows = slice(j * HD, (j + 1) * HD)
+        own_ref[rows, :] = summed[:, :TILE]
+        own_log_ref[j : j + 1, :] = logs[:, :TILE]
+        for rel, out in enumerate(outs, 1):
+            cols = slice(rel * TILE, (rel + 1) * TILE)
+            out[rows, :] = summed[:, cols].astype(BF16)
+            stats[rel - 1] += three_parts(logs[:, cols])
+    row = half * HD
+    for rel, out in enumerate(outs, 1):
+        out[row : row + FLAG_ROWS, :] = stat_block(stats[rel - 1])
+        start = row + FLAG_ROWS
+        out[start : start + HD, :] = whole[:, rel * TILE : (rel + 1) * TILE].astype(BF16)
+    whole_ref[...] = whole[:, :TILE].astype(BF16)
+
+
+def merge_kernel(
+    half, own_ref, own_log_ref, in2_ref, in1_ref, in3_ref,
+    whole_ref, out_ref,
+):
+    me = lax.axis_index("seq")
+    side = lax.rem(me, 2)
+    start = half * HD
+
+    def logs_of(ref, j):
+        block = ref[start : start + FLAG_ROWS, :].astype(F32)
+        row = 3 * j
+        return block[row : row + 1, :] + block[row + 1 : row + 2, :] + block[row + 2 : row + 3, :]
+
+    def joined(first, first_log, second, second_log):
+        peak = jnp.maximum(first_log, second_log)
+        first_weight = jnp.exp2(first_log - peak)
+        second_weight = jnp.exp2(second_log - peak)
+        return (first * first_weight + second * second_weight) / (first_weight + second_weight)
+
+    for j in range(half):
+        rows = slice(j * HD, (j + 1) * HD)
+        close = joined(
+            own_ref[rows, :], own_log_ref[j : j + 1, :],
+            in2_ref[rows, :].astype(F32), logs_of(in2_ref, j),
+        )
+        out_ref[0, :, head_cols(side * half + j)] = close.T.astype(BF16)
+        far = joined(
+            in1_ref[rows, :].astype(F32), logs_of(in1_ref, j),
+            in3_ref[rows, :].astype(F32), logs_of(in3_ref, j),
+        )
+        out_ref[0, :, head_cols((1 - side) * half + j)] = far.T.astype(BF16)
+    done = start + FLAG_ROWS
+    blocks = [whole_ref[...]] + [ref[done : done + HD, :] for ref in (in1_ref, in2_ref, in3_ref)]
+    for rel, block in enumerate(blocks):
+        cols = head_cols(2 * half + jnp.bitwise_xor(me, rel))
+        out_ref[0, :, cols] = block.astype(F32).T.astype(BF16)
+
+
+def send(array, rel):
+    return lax.ppermute(array, "seq", [(i, i ^ rel) for i in range(4)])
+
+
+def near(array):
+    return pltpu.with_memory_space_constraint(array, pltpu.VMEM)
+
+
+def exchanged(queries, keys, values, cache_keys, cache_values, frame_list, frame_place, tile_mask):
+    head_count = queries.shape[2] // HD
+    half = (head_count - 4) // 2
+    frames, frame_tok = cache_keys.shape[1:3]
+    span = 3 * TILE + 2 * frames * frame_tok
+    pair_rows = (half + 1) * span + FLAG_ROWS
+    far_rows = half * TILE + span + FLAG_ROWS
+    back_rows = half * HD + FLAG_ROWS
+    near0, near1, far2, far3 = pl.pallas_call(
+        functools.partial(pack_kernel, half),
+        out_shape=(pltpu.VMEM((pair_rows, HD), BF16),) * 2
+        + (pltpu.VMEM((far_rows, HD), BF16),) * 2,
+        in_specs=[SMEM] + [VMEM] * 5,
+        out_specs=(VMEM,) * 4,
+    )(tile_mask, queries, keys, values, cache_keys, cache_values)
+    near0, near1 = near(near0), near(send(near1, 1))
+    far3, far2 = near(send(far3, 3)), near(send(far2, 2))
+    own, own_log, whole, back1, back2, back3 = pl.pallas_call(
+        functools.partial(attend_kernel, half, frames, frame_tok),
+        out_shape=(
+            pltpu.VMEM((half * HD, TILE), F32),
+            pltpu.VMEM((half, TILE), F32),
+            pltpu.VMEM((HD, TILE), BF16),
+        ) + (pltpu.VMEM((back_rows + HD, TILE), BF16),) * 3,
+        in_specs=[SMEM] * 2 + [VMEM] * 4,
+        out_specs=(VMEM,) * 6,
+    )(frame_list, frame_place, near0, near1, far3, far2)
+    back2, back1, back3 = near(send(back2, 2)), near(send(back1, 1)), near(send(back3, 3))
+    return pl.pallas_call(
+        functools.partial(merge_kernel, half),
+        out_shape=jax.ShapeDtypeStruct(queries.shape, BF16),
+        in_specs=[VMEM] * 6,
+        out_specs=VMEM,
+    )(near(own), near(own_log), back2, back1, back3, near(whole))
+
+
+def body(queries, keys, values, cache_keys, cache_values, frame_list, frame_place, tile_mask):
+    head_count = queries.shape[2] // HD
+    fits = (
+        lax.axis_size("seq") == 4
+        and queries.shape[0] == 1
+        and queries.shape[1] == TILE
+        and head_count % 2 == 0
+        and 6 <= head_count <= 14
+    )
+    run = exchanged if fits else gathered
+    return run(queries, keys, values, cache_keys, cache_values, frame_list, frame_place, tile_mask)
+
+
 def solution(mesh):
     return jax.shard_map(
         body,

time: 111 us -> 43.7 us (0.39)
  blocking collectives: 49 us -> 0 us
  between operations: 14.9 us -> 0.02 us
  starting transfers between devices: 0.08 us -> 10.9 us
  local copies, waits for them, and re-layouts: 7.46 us -> 0 us
  matrix products: 5.99 us -> 0 us
  other arithmetic: 5.75 us -> 0 us
  Pallas kernels: 0 us -> 4.79 us
    all_gather x2 -> x0, blocking collectives: 49 us -> none  [the longest x1 27.2 us: body(): key_piece = lax.all_gather(cache_keys, 'seq', axis=1, tiled=True)]
    ppermute x0 -> x6, waiting for transfers between devices: none -> 27.9 us  [send(): return lax.ppermute(array, 'seq', [(i, i ^ rel) for i in range(4)])]
    all_gather x2 -> x0, waiting for transfers between devices: 26.9 us -> none  [the longest x1 26.9 us: body(): value_piece = lax.all_gather(values, 'seq', axis=1, tiled=True)]
    ppermute x0 -> x6, starting transfers between devices: none -> 10.9 us  [send(): return lax.ppermute(array, 'seq', [(i, i ^ rel) for i in range(4)])]
    dot_general x4 -> x0, matrix products: 5.99 us -> none  [the longest x2 3.49 us: update(): jnp.einsum('vhqk,vkhd->vhqd', weights.astype(jnp.bfloat16), value_heads,...]
    pallas_call x0 -> x3, Pallas kernels: none -> 4.79 us  [the longest x1 2.24 us: exchanged(): pl.pallas_call(functools.partial(attend_kernel, half, frames, frame_tok),...]
    unnamed x15 -> x0, local copies, waits for them, and re-layouts: 4.08 us -> none
    gather x1 -> x0, other arithmetic: 2.7 us -> none  [body(): tile_live = jnp.take(tile_mask, key_tiles, axis=2)]
  transfers between devices with their start and end apart: 2 -> 6, of which waited for: 1 -> 5; matrix products, arithmetic and copies ran while one was open for 10% -> 0% of each run, Pallas kernels for 0% -> 0%
where the time goes in v3:
time: 43.7 us; the launch traced here: 43.5 us
  waiting for transfers between devices  27.9 us (64%)
  starting transfers between devices  10.9 us (25%)
  Pallas kernels  4.79 us (11%)
    ppermute x6, waiting for transfers between devices, send(): return lax.ppermute(array, 'seq', [(i, i ^ rel) for i in range(4)])  27.9 us
    ppermute x6, starting transfers between devices, send(): return lax.ppermute(array, 'seq', [(i, i ^ rel) for i in range(4)])  10.9 us
    pallas_call x1, Pallas kernels, exchanged(): pl.pallas_call(functools.partial(attend_kernel, half, frames, frame_tok),...  2.24 us
    pallas_call x1, Pallas kernels, exchanged(): pl.pallas_call(functools.partial(pack_kernel, half), out_shape=(pltpu.VME...  1.6 us
    pallas_call x1, Pallas kernels, exchanged(): pl.pallas_call(functools.partial(merge_kernel, half), out_shape=jax.Shape...  0.96 us
  transfers between devices with their start and end apart: 6, of which 5 were waited for; matrix products, arithmetic and copies ran while one was open for 0% of the time, Pallas kernels for 0%

profile of v3, /device:TPU:0, one launch (start us, length us, event | category | flops | bytes accessed | tf_op | source)
XLA Modules:
  0.0 43.5 jit_solution(14106204269613680023)
XLA Ops:
  0.0 1.6 %shard_map.82 = (bf16[2064,128]{1,0:T(8,128)(2,1)S(1)}, bf16[2064,128]{1,0:T(8,128)(2,1)S(1)}, bf16[912,128]{1,0:T(8,128)(2,1)S(1)}, bf16[912,128]{1,0:T(8,128)(2,1)S(1)}) custom-call(s32[1,1,4]{2,1,0:T(1,128)} %mask_ref.1, bf16[1,128,1280]{2,1,0:T(8,128)(2,1)} %q_ref.1, bf16[1,128,1280]{2,1,0:T(8,128)(2,1)} %k_ref.1, bf16[1,128,1280]{2,1,0:T(8,128)(2,1)} %v_ref.1, ...), custom_call_target="tpu_custom_call" | custom-call | tf_op jit(solution)/shard_map/pallas_call | solution.py:319
  1.6 3.1 %collective-permute-start = (bf16[2064,128]{1,0:T(8,128)(2,1)S(1)}, bf16[2064,128]{1,0:T(8,128)(2,1)S(1)}, u32[]{:S(2)}, u32[]{:S(2)}) collective-permute-start(bf16[2064,128]{1,0:T(8,128)(2,1)S(1)} %get-tuple-element.16), channel_id=1, source_target_pairs={{0,4},{4,0},{8,12},{12,8},{1,5},{5,1},{9,13},{13,9},{2,6},{6,2},{1... | collective-permute-start | bytes 1585160 | tf_op jit(solution)/shard_map/ppermute | solution.py:304
  4.7 2.5 %collective-permute-start.1 = (bf16[912,128]{1,0:T(8,128)(2,1)S(1)}, bf16[912,128]{1,0:T(8,128)(2,1)S(1)}, u32[]{:S(2)}, u32[]{:S(2)}) collective-permute-start(bf16[912,128]{1,0:T(8,128)(2,1)S(1)} %get-tuple-element.17), channel_id=1, source_target_pairs={{0,12},{4,8},{8,4},{12,0},{1,13},{5,9},{9,5},{13,1},{2,14},{6,10},... | collective-permute-start | bytes 700424 | tf_op jit(solution)/shard_map/ppermute | solution.py:304
  7.2 0.1 collective-permute-start.2
  7.3 17.8 %collective-permute-done.1.far3_ref = bf16[912,128]{1,0:T(8,128)(2,1)S(1)} collective-permute-done((bf16[912,128]{1,0:T(8,128)(2,1)S(1)}, bf16[912,128]{1,0:T(8,128)(2,1)S(1)}, u32[]{:S(2)}, u32[]{:S(2)}) %collective-permute-start.1) | collective-permute-done | bytes 233504 | tf_op jit(solution)/shard_map/ppermute | solution.py:304
  25.0 1.0 %collective-permute-done.2.far2_ref = bf16[912,128]{1,0:T(8,128)(2,1)S(1)} collective-permute-done((bf16[912,128]{1,0:T(8,128)(2,1)S(1)}, bf16[912,128]{1,0:T(8,128)(2,1)S(1)}, u32[]{:S(2)}, u32[]{:S(2)}) %collective-permute-start.2) | collective-permute-done | bytes 233504 | tf_op jit(solution)/shard_map/ppermute | solution.py:304
  26.0 0.7 %collective-permute-done.near1_ref = bf16[2064,128]{1,0:T(8,128)(2,1)S(1)} collective-permute-done((bf16[2064,128]{1,0:T(8,128)(2,1)S(1)}, bf16[2064,128]{1,0:T(8,128)(2,1)S(1)}, u32[]{:S(2)}, u32[]{:S(2)}) %collective-permute-start) | collective-permute-done | bytes 528416 | tf_op jit(solution)/shard_map/ppermute | solution.py:304
  26.7 2.2 %shard_map.83 = (f32[384,128]{1,0:T(8,128)S(1)}, f32[3,128]{1,0:T(4,128)S(1)}, bf16[128,128]{1,0:T(8,128)(2,1)S(1)}, bf16[528,128]{1,0:T(8,128)(2,1)S(1)}, bf16[...) custom-call(s32[1,3]{1,0:T(1,128)} %list_ref.1, s32[1,8]{1,0:T(1,128)} %place_ref.1, ...), custom_call_target="tpu_custom_call" | custom-call | tf_op jit(solution)/shard_map/pallas_call | solution.py:328
  29.0 2.8 %collective-permute-start.3 = (bf16[528,128]{1,0:T(8,128)(2,1)S(1)}, bf16[528,128]{1,0:T(8,128)(2,1)S(1)}, u32[]{:S(2)}, u32[]{:S(2)}) collective-permute-start(bf16[528,128]{1,0:T(8,128)(2,1)S(1)} %get-tuple-element.21), channel_id=1, source_target_pairs={{0,8},{4,12},{8,0},{12,4},{1,9},{5,13},{9,1},{13,5},{2,10},{6,14},... | collective-permute-start | bytes 405512 | tf_op jit(solution)/shard_map/ppermute | solution.py:304
  31.8 1.6 %collective-permute-start.4 = (bf16[528,128]{1,0:T(8,128)(2,1)S(1)}, bf16[528,128]{1,0:T(8,128)(2,1)S(1)}, u32[]{:S(2)}, u32[]{:S(2)}) collective-permute-start(bf16[528,128]{1,0:T(8,128)(2,1)S(1)} %get-tuple-element.22), channel_id=1, source_target_pairs={{0,4},{4,0},{8,12},{12,8},{1,5},{5,1},{9,13},{13,9},{2,6},{6,2},{1... | collective-permute-start | bytes 405512 | tf_op jit(solution)/shard_map/ppermute | solution.py:304
  33.4 0.8 %collective-permute-start.5 = (bf16[528,128]{1,0:T(8,128)(2,1)S(1)}, bf16[528,128]{1,0:T(8,128)(2,1)S(1)}, u32[]{:S(2)}, u32[]{:S(2)}) collective-permute-start(bf16[528,128]{1,0:T(8,128)(2,1)S(1)} %get-tuple-element.23), channel_id=1, source_target_pairs={{0,12},{4,8},{8,4},{12,0},{1,13},{5,9},{9,5},{13,1},{2,14},{6,10},... | collective-permute-start | bytes 405512 | tf_op jit(solution)/shard_map/ppermute | solution.py:304
  34.1 6.2 %collective-permute-done.3.in2_ref = bf16[528,128]{1,0:T(8,128)(2,1)S(1)} collective-permute-done((bf16[528,128]{1,0:T(8,128)(2,1)S(1)}, bf16[528,128]{1,0:T(8,128)(2,1)S(1)}, u32[]{:S(2)}, u32[]{:S(2)}) %collective-permute-start.3) | collective-permute-done | bytes 135200 | tf_op jit(solution)/shard_map/ppermute | solution.py:304
  40.3 0.0 collective-permute-done.4.in1_ref
  40.3 2.3 %collective-permute-done.5.in3_ref = bf16[528,128]{1,0:T(8,128)(2,1)S(1)} collective-permute-done((bf16[528,128]{1,0:T(8,128)(2,1)S(1)}, bf16[528,128]{1,0:T(8,128)(2,1)S(1)}, u32[]{:S(2)}, u32[]{:S(2)}) %collective-permute-start.5) | collective-permute-done | bytes 135200 | tf_op jit(solution)/shard_map/ppermute | solution.py:304
  42.6 1.0 %shard_map.84 = bf16[1,128,1280]{2,1,0:T(8,128)(2,1)} custom-call(f32[384,128]{1,0:T(8,128)S(1)} %get-tuple-element.19.own_ref, f32[3,128]{1,0:T(4,128)S(1)} %get-tuple-element.20.own_log_ref, bf16[528,128]{1,0:T(8,128)(2,1)S(1)} %collective-permute-done.3.in2_ref, bf16[528,128]{1,0:T(8,128)(2,1)S(1)} %collective-permute-done.4.in1_ref, ...), custom_call_target="tpu_custom_call" | custom-call | tf_op jit(solution)/shard_map/pallas_call | solution.py:339
Async XLA Ops:
  1.6 25.1 %collective-permute-start = (bf16[2064,128]{1,0:T(8,128)(2,1)S(1)}, bf16[2064,128]{1,0:T(8,128)(2,1)S(1)}, u32[]{:S(2)}, u32[]{:S(2)}) collective-permute-start(bf16[2064,128]{1,0:T(8,128)(2,1)S(1)} %get-tuple-element.16), channel_id=1, source_target_pairs={{0,4},{4,0},{8,12},{12,8},{1,5},{5,1},{9,13},{13,9},{2,6},{6,2},{1... | collective-permute-start | bytes 1585160 | tf_op jit(solution)/shard_map/ppermute | solution.py:304
  4.7 20.4 %collective-permute-start.1 = (bf16[912,128]{1,0:T(8,128)(2,1)S(1)}, bf16[912,128]{1,0:T(8,128)(2,1)S(1)}, u32[]{:S(2)}, u32[]{:S(2)}) collective-permute-start(bf16[912,128]{1,0:T(8,128)(2,1)S(1)} %get-tuple-element.17), channel_id=1, source_target_pairs={{0,12},{4,8},{8,4},{12,0},{1,13},{5,9},{9,5},{13,1},{2,14},{6,10},... | collective-permute-start | bytes 700424 | tf_op jit(solution)/shard_map/ppermute | solution.py:304
  7.2 18.8 %collective-permute-start.2 = (bf16[912,128]{1,0:T(8,128)(2,1)S(1)}, bf16[912,128]{1,0:T(8,128)(2,1)S(1)}, u32[]{:S(2)}, u32[]{:S(2)}) collective-permute-start(bf16[912,128]{1,0:T(8,128)(2,1)S(1)} %get-tuple-element.18), channel_id=1, source_target_pairs={{0,8},{4,12},{8,0},{12,4},{1,9},{5,13},{9,1},{13,5},{2,10},{6,14},... | collective-permute-start | bytes 700424 | tf_op jit(solution)/shard_map/ppermute | solution.py:304
  29.0 11.4 %collective-permute-start.3 = (bf16[528,128]{1,0:T(8,128)(2,1)S(1)}, bf16[528,128]{1,0:T(8,128)(2,1)S(1)}, u32[]{:S(2)}, u32[]{:S(2)}) collective-permute-start(bf16[528,128]{1,0:T(8,128)(2,1)S(1)} %get-tuple-element.21), channel_id=1, source_target_pairs={{0,8},{4,12},{8,0},{12,4},{1,9},{5,13},{9,1},{13,5},{2,10},{6,14},... | collective-permute-start | bytes 405512 | tf_op jit(solution)/shard_map/ppermute | solution.py:304
  31.8 8.6 %collective-permute-start.4 = (bf16[528,128]{1,0:T(8,128)(2,1)S(1)}, bf16[528,128]{1,0:T(8,128)(2,1)S(1)}, u32[]{:S(2)}, u32[]{:S(2)}) collective-permute-start(bf16[528,128]{1,0:T(8,128)(2,1)S(1)} %get-tuple-element.22), channel_id=1, source_target_pairs={{0,4},{4,0},{8,12},{12,8},{1,5},{5,1},{9,13},{13,9},{2,6},{6,2},{1... | collective-permute-start | bytes 405512 | tf_op jit(solution)/shard_map/ppermute | solution.py:304
  33.4 9.2 %collective-permute-start.5 = (bf16[528,128]{1,0:T(8,128)(2,1)S(1)}, bf16[528,128]{1,0:T(8,128)(2,1)S(1)}, u32[]{:S(2)}, u32[]{:S(2)}) collective-permute-start(bf16[528,128]{1,0:T(8,128)(2,1)S(1)} %get-tuple-element.23), channel_id=1, source_target_pairs={{0,12},{4,8},{8,4},{12,0},{1,13},{5,9},{9,5},{13,1},{2,14},{6,10},... | collective-permute-start | bytes 405512 | tf_op jit(solution)/shard_map/ppermute | solution.py:304

commit v4 on v3

--- a/solution.py
+++ b/solution.py
@@ -94,14 +94,15 @@
     return jnp.where(live, 0.0, NEG_FILL)
 
 
-def frame_fills(place_ref, list_ref, device, frames):
+def frame_fills(place_ref, list_ref, me, frames):
     out = []
-    for slot in range(frames):
-        held = place_ref[0, device * frames + slot]
-        live = held == list_ref[0, 0]
-        for entry in range(1, list_ref.shape[1]):
-            live = live | (held == list_ref[0, entry])
-        out.append(fill(live))
+    for rel in range(4):
+        for slot in range(frames):
+            held = place_ref[0, jnp.bitwise_xor(me, rel) * frames + slot]
+            live = held == list_ref[0, 0]
+            for entry in range(1, list_ref.shape[1]):
+                live = live | (held == list_ref[0, entry])
+            out.append(fill(live))
     return out
 
 
@@ -120,12 +121,12 @@
 
 
 def pack_kernel(
-    half, mask_ref, q_ref, k_ref, v_ref, ck_ref, cv_ref, near0_ref, near1_ref, far2_ref, far3_ref
+    half, rels, mask_ref, list_ref, place_ref, q_ref, k_ref, v_ref, ck_ref, cv_ref, *out_refs
 ):
     me = lax.axis_index("seq")
     side = lax.rem(me, 2)
     parts = (q_ref, k_ref, v_ref, ck_ref, cv_ref)
-    for rel, out in enumerate((near0_ref, near1_ref, far2_ref, far3_ref)):
+    for rel, out in zip(rels, out_refs[-len(rels) :]):
         other = jnp.bitwise_xor(me, rel)
         group = (1 - side) if rel % 2 else side
         row = 0
@@ -137,6 +138,9 @@
         for key in range(4):
             live = mask_ref[0, 0, jnp.bitwise_xor(other, key)] > 0
             block = jnp.where(ident == key, fill(live), block)
+        if rel == 0:
+            for key, value in enumerate(frame_fills(place_ref, list_ref, me, ck_ref.shape[1]), 4):
+                block = jnp.where(ident == key, value, block)
         out[row : row + FLAG_ROWS, :] = block.astype(BF16)
 
 
@@ -166,18 +170,18 @@
     return jnp.concatenate(weights, axis=0), 1.0 / total, peak + jnp.log2(total)
 
 
-def all_fills(refs, keys, frames, frame_tok, list_ref, place_ref, me):
+def all_fills(refs, frames, frame_tok):
     blocks = []
     for ref in refs:
         row = ref.shape[0] - FLAG_ROWS
         blocks.append(ref[row : row + FLAG_ROWS, :].astype(F32))
     fills = [
         (TILE, jnp.concatenate([block[key : key + 1, :] for block in blocks], axis=1))
-        for key in range(keys)
+        for key in range(4)
     ]
-    for rel in range(keys):
-        for value in frame_fills(place_ref, list_ref, jnp.bitwise_xor(me, rel), frames):
-            fills.append((frame_tok, value))
+    for key in range(4, 4 + 4 * frames):
+        row = blocks[0][key : key + 1, :]
+        fills.append((frame_tok, jnp.concatenate([row] * 4, axis=1)))
     return fills
 
 
@@ -228,15 +232,14 @@
 
 def attend_kernel(
     half, frames, frame_tok,
-    list_ref, place_ref, near0_ref, near1_ref, far3_ref, far2_ref,
+    near0_ref, near1_ref, far3_ref, far2_ref,
     own_ref, own_log_ref, whole_ref, out1_ref, out2_ref, out3_ref,
 ):
-    me = lax.axis_index("seq")
     cache = frames * frame_tok
     span = 3 * TILE + 2 * cache
     ins = (near0_ref, near1_ref, far2_ref, far3_ref)
     outs = (out1_ref, out2_ref, out3_ref)
-    fills = all_fills(ins, 4, frames, frame_tok, list_ref, place_ref, me)
+    fills = all_fills(ins, frames, frame_tok)
     pair_fills = fills[:2] + fills[4 : 4 + 2 * frames]
     tasks = []
     for j in range(half):
@@ -287,17 +290,17 @@
             own_ref[rows, :], own_log_ref[j : j + 1, :],
             in2_ref[rows, :].astype(F32), logs_of(in2_ref, j),
         )
-        out_ref[0, :, head_cols(side * half + j)] = close.T.astype(BF16)
+        out_ref[0, :, head_cols(side * half + j)] = close.astype(BF16).T
         far = joined(
             in1_ref[rows, :].astype(F32), logs_of(in1_ref, j),
             in3_ref[rows, :].astype(F32), logs_of(in3_ref, j),
         )
-        out_ref[0, :, head_cols((1 - side) * half + j)] = far.T.astype(BF16)
+        out_ref[0, :, head_cols((1 - side) * half + j)] = far.astype(BF16).T
     done = start + FLAG_ROWS
     blocks = [whole_ref[...]] + [ref[done : done + HD, :] for ref in (in1_ref, in2_ref, in3_ref)]
     for rel, block in enumerate(blocks):
         cols = head_cols(2 * half + jnp.bitwise_xor(me, rel))
-        out_ref[0, :, cols] = block.astype(F32).T.astype(BF16)
+        out_ref[0, :, cols] = block.T
 
 
 def send(array, rel):
@@ -316,13 +319,20 @@
     pair_rows = (half + 1) * span + FLAG_ROWS
     far_rows = half * TILE + span + FLAG_ROWS
     back_rows = half * HD + FLAG_ROWS
-    near0, near1, far2, far3 = pl.pallas_call(
-        functools.partial(pack_kernel, half),
-        out_shape=(pltpu.VMEM((pair_rows, HD), BF16),) * 2
-        + (pltpu.VMEM((far_rows, HD), BF16),) * 2,
-        in_specs=[SMEM] + [VMEM] * 5,
-        out_specs=(VMEM,) * 4,
-    )(tile_mask, queries, keys, values, cache_keys, cache_values)
+    arrays = (tile_mask, frame_list, frame_place, queries, keys, values, cache_keys, cache_values)
+    near1 = pl.pallas_call(
+        functools.partial(pack_kernel, half, (1,)),
+        out_shape=pltpu.VMEM((pair_rows, HD), BF16),
+        in_specs=[SMEM] * 3 + [VMEM] * 5,
+        out_specs=VMEM,
+    )(*arrays)
+    far3, far2, near0 = pl.pallas_call(
+        functools.partial(pack_kernel, half, (3, 2, 0)),
+        out_shape=(pltpu.VMEM((far_rows, HD), BF16),) * 2
+        + (pltpu.VMEM((pair_rows, HD), BF16),),
+        in_specs=[SMEM] * 3 + [VMEM] * 6,
+        out_specs=(VMEM,) * 3,
+    )(*arrays, near(near1))
     near0, near1 = near(near0), near(send(near1, 1))
     far3, far2 = near(send(far3, 3)), near(send(far2, 2))
     own, own_log, whole, back1, back2, back3 = pl.pallas_call(
@@ -332,9 +342,9 @@
             pltpu.VMEM((half, TILE), F32),
             pltpu.VMEM((HD, TILE), BF16),
         ) + (pltpu.VMEM((back_rows + HD, TILE), BF16),) * 3,
-        in_specs=[SMEM] * 2 + [VMEM] * 4,
+        in_specs=[VMEM] * 4,
         out_specs=(VMEM,) * 6,
-    )(frame_list, frame_place, near0, near1, far3, far2)
+    )(near0, near1, far3, far2)
     back2, back1, back3 = near(send(back2, 2)), near(send(back1, 1)), near(send(back3, 3))
     return pl.pallas_call(
         functools.partial(merge_kernel, half),
@@ -352,6 +362,7 @@
         and queries.shape[1] == TILE
         and head_count % 2 == 0
         and 6 <= head_count <= 14
+        and 4 + 4 * cache_keys.shape[1] <= FLAG_ROWS
     )
     run = exchanged if fits else gathered
     return run(queries, keys, values, cache_keys, cache_values, frame_list, frame_place, tile_mask)

time: 43.7 us -> 42.9 us (0.982)
  waiting for transfers between devices: 27.9 us -> 27 us
  Pallas kernels: 4.79 us -> 5.46 us
  starting transfers between devices: 10.9 us -> 10.3 us
    pallas_call x1 -> x2, Pallas kernels: 1.6 us -> 2.93 us  [the longest x1 1.51 us: exchanged(): pl.pallas_call(functools.partial(pack_kernel, half, (3, 2, 0)), out_shape...]
    ppermute x6, waiting for transfers between devices: 27.9 us -> 27 us  [send(): return lax.ppermute(array, 'seq', [(i, i ^ rel) for i in range(4)])]
    pallas_call x1, Pallas kernels: 2.24 us -> 1.6 us  [exchanged(): pl.pallas_call(functools.partial(attend_kernel, half, frames, frame_tok),...]
    ppermute x6, starting transfers between devices: 10.9 us -> 10.3 us  [send(): return lax.ppermute(array, 'seq', [(i, i ^ rel) for i in range(4)])]
  transfers between devices with their start and end apart: 6 -> 6, of which waited for: 5 -> 4; matrix products, arithmetic and copies ran while one was open for 0% -> 0% of each run, Pallas kernels for 0% -> 4%
where the time goes in v4:
time: 42.9 us; the launch traced here: 42.8 us
  waiting for transfers between devices  27 us (63%)
  starting transfers between devices  10.3 us (24%)
  Pallas kernels  5.46 us (13%)
    ppermute x6, waiting for transfers between devices, send(): return lax.ppermute(array, 'seq', [(i, i ^ rel) for i in range(4)])  27 us
    ppermute x6, starting transfers between devices, send(): return lax.ppermute(array, 'seq', [(i, i ^ rel) for i in range(4)])  10.3 us
    pallas_call x1, Pallas kernels, exchanged(): pl.pallas_call(functools.partial(attend_kernel, half, frames, frame_tok),...  1.6 us
    pallas_call x1, Pallas kernels, exchanged(): pl.pallas_call(functools.partial(pack_kernel, half, (3, 2, 0)), out_shape...  1.51 us
    pallas_call x1, Pallas kernels, exchanged(): pl.pallas_call(functools.partial(pack_kernel, half, (1,)), out_shape=pltp...  1.42 us
    pallas_call x1, Pallas kernels, exchanged(): pl.pallas_call(functools.partial(merge_kernel, half), out_shape=jax.Shape...  0.93 us
  transfers between devices with their start and end apart: 6, of which 4 were waited for; matrix products, arithmetic and copies ran while one was open for 0% of the time, Pallas kernels for 4%

profile of v4, /device:TPU:0, one launch (start us, length us, event | category | flops | bytes accessed | tf_op | source)
XLA Modules:
  0.0 42.8 jit_solution(13643523780124506927)
XLA Ops:
  0.0 1.4 %shard_map.82.out_refs_0_ = bf16[2064,128]{1,0:T(8,128)(2,1)S(1)} custom-call(s32[1,1,4]{2,1,0:T(1,128)} %mask_ref.3, s32[1,3]{1,0:T(1,128)} %list_ref.3, s32[1,8]{1,0:T(1,128)} %place_ref.3, bf16[1,128,1280]{2,1,0:T(8,128)(2,1)} %q_ref.3, bf16[1,128,1280]{2,1,0:T(8,128)(2,1)} %k_ref.3, bf16[1,128,1280]{2,1,0:T(8,128)(2,1)} %v_ref.3, ...), custom_call_target="tpu_custom_call" | custom-call | tf_op jit(solution)/shard_map/pallas_call | solution.py:323
  1.4 3.1 %collective-permute-start = (bf16[2064,128]{1,0:T(8,128)(2,1)S(1)}, bf16[2064,128]{1,0:T(8,128)(2,1)S(1)}, u32[]{:S(2)}, u32[]{:S(2)}) collective-permute-start(bf16[2064,128]{1,0:T(8,128)(2,1)S(1)} %shard_map.82.out_refs_0_), channel_id=1, source_target_pairs={{0,4},{4,0},{8,12},{12,8},{1,5},{5,1},{9,13},{13,9},{2,6},{6,2},{1... | collective-permute-start | bytes 1585160 | tf_op jit(solution)/shard_map/ppermute | solution.py:307
  4.5 1.5 %shard_map.83 = (bf16[912,128]{1,0:T(8,128)(2,1)S(1)}, bf16[912,128]{1,0:T(8,128)(2,1)S(1)}, bf16[2064,128]{1,0:T(8,128)(2,1)S(1)}) custom-call(s32[1,1,4]{2,1,0:T(1,128)} %mask_ref.3, s32[1,3]{1,0:T(1,128)} %list_ref.3, s32[1,8]{1,0:T(1,128)} %place_ref.3, bf16[1,128,1280]{2,1,0:T(8,128)(2,1)} %q_ref.3, bf16[1,128,1280]{2,1,0:T(8,128)(2,1)} %k_ref.3, ...), custom_call_target="tpu_custom_call" | custom-call | tf_op jit(solution)/shard_map/pallas_call | solution.py:329
  6.0 2.5 %collective-permute-start.1 = (bf16[912,128]{1,0:T(8,128)(2,1)S(1)}, bf16[912,128]{1,0:T(8,128)(2,1)S(1)}, u32[]{:S(2)}, u32[]{:S(2)}) collective-permute-start(bf16[912,128]{1,0:T(8,128)(2,1)S(1)} %get-tuple-element.15), channel_id=1, source_target_pairs={{0,12},{4,8},{8,4},{12,0},{1,13},{5,9},{9,5},{13,1},{2,14},{6,10},... | collective-permute-start | bytes 700424 | tf_op jit(solution)/shard_map/ppermute | solution.py:307
  8.6 0.2 collective-permute-start.2
  8.8 16.2 %collective-permute-done.1.far3_ref = bf16[912,128]{1,0:T(8,128)(2,1)S(1)} collective-permute-done((bf16[912,128]{1,0:T(8,128)(2,1)S(1)}, bf16[912,128]{1,0:T(8,128)(2,1)S(1)}, u32[]{:S(2)}, u32[]{:S(2)}) %collective-permute-start.1) | collective-permute-done | bytes 233504 | tf_op jit(solution)/shard_map/ppermute | solution.py:307
  25.0 4.2 %collective-permute-done.2.far2_ref = bf16[912,128]{1,0:T(8,128)(2,1)S(1)} collective-permute-done((bf16[912,128]{1,0:T(8,128)(2,1)S(1)}, bf16[912,128]{1,0:T(8,128)(2,1)S(1)}, u32[]{:S(2)}, u32[]{:S(2)}) %collective-permute-start.2) | collective-permute-done | bytes 233504 | tf_op jit(solution)/shard_map/ppermute | solution.py:307
  29.2 0.0 collective-permute-done.near1_ref
  29.2 1.6 %shard_map.84 = (f32[384,128]{1,0:T(8,128)S(1)}, f32[3,128]{1,0:T(4,128)S(1)}, bf16[128,128]{1,0:T(8,128)(2,1)S(1)}, bf16[528,128]{1,0:T(8,128)(2,1)S(1)}, bf16[...) custom-call(bf16[2064,128]{1,0:T(8,128)(2,1)S(1)} %get-tuple-element.14.near0_ref, ...), custom_call_target="tpu_custom_call" | custom-call | tf_op jit(solution)/shard_map/pallas_call | solution.py:338
  30.8 0.1 collective-permute-start.3
  30.9 3.2 %collective-permute-start.4 = (bf16[528,128]{1,0:T(8,128)(2,1)S(1)}, bf16[528,128]{1,0:T(8,128)(2,1)S(1)}, u32[]{:S(2)}, u32[]{:S(2)}) collective-permute-start(bf16[528,128]{1,0:T(8,128)(2,1)S(1)} %get-tuple-element.20), channel_id=1, source_target_pairs={{0,4},{4,0},{8,12},{12,8},{1,5},{5,1},{9,13},{13,9},{2,6},{6,2},{1... | collective-permute-start | bytes 405512 | tf_op jit(solution)/shard_map/ppermute | solution.py:307
  34.0 1.2 %collective-permute-start.5 = (bf16[528,128]{1,0:T(8,128)(2,1)S(1)}, bf16[528,128]{1,0:T(8,128)(2,1)S(1)}, u32[]{:S(2)}, u32[]{:S(2)}) collective-permute-start(bf16[528,128]{1,0:T(8,128)(2,1)S(1)} %get-tuple-element.21), channel_id=1, source_target_pairs={{0,12},{4,8},{8,4},{12,0},{1,13},{5,9},{9,5},{13,1},{2,14},{6,10},... | collective-permute-start | bytes 405512 | tf_op jit(solution)/shard_map/ppermute | solution.py:307
  35.2 5.0 %collective-permute-done.3.in2_ref = bf16[528,128]{1,0:T(8,128)(2,1)S(1)} collective-permute-done((bf16[528,128]{1,0:T(8,128)(2,1)S(1)}, bf16[528,128]{1,0:T(8,128)(2,1)S(1)}, u32[]{:S(2)}, u32[]{:S(2)}) %collective-permute-start.3) | collective-permute-done | bytes 135200 | tf_op jit(solution)/shard_map/ppermute | solution.py:307
  40.2 0.0 collective-permute-done.4.in1_ref
  40.3 1.6 %collective-permute-done.5.in3_ref = bf16[528,128]{1,0:T(8,128)(2,1)S(1)} collective-permute-done((bf16[528,128]{1,0:T(8,128)(2,1)S(1)}, bf16[528,128]{1,0:T(8,128)(2,1)S(1)}, u32[]{:S(2)}, u32[]{:S(2)}) %collective-permute-start.5) | collective-permute-done | bytes 135200 | tf_op jit(solution)/shard_map/ppermute | solution.py:307
  41.8 0.9 %shard_map.85 = bf16[1,128,1280]{2,1,0:T(8,128)(2,1)} custom-call(f32[384,128]{1,0:T(8,128)S(1)} %get-tuple-element.17.own_ref, f32[3,128]{1,0:T(4,128)S(1)} %get-tuple-element.18.own_log_ref, bf16[528,128]{1,0:T(8,128)(2,1)S(1)} %collective-permute-done.3.in2_ref, bf16[528,128]{1,0:T(8,128)(2,1)S(1)} %collective-permute-done.4.in1_ref, ...), custom_call_target="tpu_custom_call" | custom-call | tf_op jit(solution)/shard_map/pallas_call | solution.py:349
Async XLA Ops:
  1.4 27.7 %collective-permute-start = (bf16[2064,128]{1,0:T(8,128)(2,1)S(1)}, bf16[2064,128]{1,0:T(8,128)(2,1)S(1)}, u32[]{:S(2)}, u32[]{:S(2)}) collective-permute-start(bf16[2064,128]{1,0:T(8,128)(2,1)S(1)} %shard_map.82.out_refs_0_), channel_id=1, source_target_pairs={{0,4},{4,0},{8,12},{12,8},{1,5},{5,1},{9,13},{13,9},{2,6},{6,2},{1... | collective-permute-start | bytes 1585160 | tf_op jit(solution)/shard_map/ppermute | solution.py:307
  6.0 18.9 %collective-permute-start.1 = (bf16[912,128]{1,0:T(8,128)(2,1)S(1)}, bf16[912,128]{1,0:T(8,128)(2,1)S(1)}, u32[]{:S(2)}, u32[]{:S(2)}) collective-permute-start(bf16[912,128]{1,0:T(8,128)(2,1)S(1)} %get-tuple-element.15), channel_id=1, source_target_pairs={{0,12},{4,8},{8,4},{12,0},{1,13},{5,9},{9,5},{13,1},{2,14},{6,10},... | collective-permute-start | bytes 700424 | tf_op jit(solution)/shard_map/ppermute | solution.py:307
  8.6 20.6 %collective-permute-start.2 = (bf16[912,128]{1,0:T(8,128)(2,1)S(1)}, bf16[912,128]{1,0:T(8,128)(2,1)S(1)}, u32[]{:S(2)}, u32[]{:S(2)}) collective-permute-start(bf16[912,128]{1,0:T(8,128)(2,1)S(1)} %get-tuple-element.16), channel_id=1, source_target_pairs={{0,8},{4,12},{8,0},{12,4},{1,9},{5,13},{9,1},{13,5},{2,10},{6,14},... | collective-permute-start | bytes 700424 | tf_op jit(solution)/shard_map/ppermute | solution.py:307
  30.8 9.5 %collective-permute-start.3 = (bf16[528,128]{1,0:T(8,128)(2,1)S(1)}, bf16[528,128]{1,0:T(8,128)(2,1)S(1)}, u32[]{:S(2)}, u32[]{:S(2)}) collective-permute-start(bf16[528,128]{1,0:T(8,128)(2,1)S(1)} %get-tuple-element.19), channel_id=1, source_target_pairs={{0,8},{4,12},{8,0},{12,4},{1,9},{5,13},{9,1},{13,5},{2,10},{6,14},... | collective-permute-start | bytes 405512 | tf_op jit(solution)/shard_map/ppermute | solution.py:307
  30.9 9.4 %collective-permute-start.4 = (bf16[528,128]{1,0:T(8,128)(2,1)S(1)}, bf16[528,128]{1,0:T(8,128)(2,1)S(1)}, u32[]{:S(2)}, u32[]{:S(2)}) collective-permute-start(bf16[528,128]{1,0:T(8,128)(2,1)S(1)} %get-tuple-element.20), channel_id=1, source_target_pairs={{0,4},{4,0},{8,12},{12,8},{1,5},{5,1},{9,13},{13,9},{2,6},{6,2},{1... | collective-permute-start | bytes 405512 | tf_op jit(solution)/shard_map/ppermute | solution.py:307
  34.0 7.8 %collective-permute-start.5 = (bf16[528,128]{1,0:T(8,128)(2,1)S(1)}, bf16[528,128]{1,0:T(8,128)(2,1)S(1)}, u32[]{:S(2)}, u32[]{:S(2)}) collective-permute-start(bf16[528,128]{1,0:T(8,128)(2,1)S(1)} %get-tuple-element.21), channel_id=1, source_target_pairs={{0,12},{4,8},{8,4},{12,0},{1,13},{5,9},{9,5},{13,1},{2,14},{6,10},... | collective-permute-start | bytes 405512 | tf_op jit(solution)/shard_map/ppermute | solution.py:307

commit v5 on v4

--- a/solution.py
+++ b/solution.py
@@ -267,7 +267,7 @@
 
 def merge_kernel(
     half, own_ref, own_log_ref, in2_ref, in1_ref, in3_ref,
-    whole_ref, out_ref,
+    whole_ref, out_hbm, out_ref, sems,
 ):
     me = lax.axis_index("seq")
     side = lax.rem(me, 2)
@@ -282,8 +282,33 @@
         peak = jnp.maximum(first_log, second_log)
         first_weight = jnp.exp2(first_log - peak)
         second_weight = jnp.exp2(second_log - peak)
-        return (first * first_weight + second * second_weight) / (first_weight + second_weight)
-
+        scale = 1.0 / (first_weight + second_weight)
+        return first * (first_weight * scale) + second * (second_weight * scale)
+
+    copies = []
+
+    def leave(head, count):
+        cols = pl.ds(pl.multiple_of(head * HD, HD), count * HD)
+        copy = pltpu.make_async_copy(
+            out_ref.at[0, :, cols], out_hbm.at[0, :, cols], sems.at[len(copies)]
+        )
+        copy.start()
+        copies.append(copy)
+
+    done = start + FLAG_ROWS
+    blocks = [whole_ref[...]] + [ref[done : done + HD, :] for ref in (in1_ref, in2_ref, in3_ref)]
+    for rel, block in enumerate(blocks):
+        cols = head_cols(2 * half + jnp.bitwise_xor(me, rel))
+        out_ref[0, :, cols] = block.T
+    leave(2 * half, 4)
+    for j in range(half):
+        rows = slice(j * HD, (j + 1) * HD)
+        far = joined(
+            in1_ref[rows, :].astype(F32), logs_of(in1_ref, j),
+            in3_ref[rows, :].astype(F32), logs_of(in3_ref, j),
+        )
+        out_ref[0, :, head_cols((1 - side) * half + j)] = far.astype(BF16).T
+    leave((1 - side) * half, half)
     for j in range(half):
         rows = slice(j * HD, (j + 1) * HD)
         close = joined(
@@ -291,16 +316,9 @@
             in2_ref[rows, :].astype(F32), logs_of(in2_ref, j),
         )
         out_ref[0, :, head_cols(side * half + j)] = close.astype(BF16).T
-        far = joined(
-            in1_ref[rows, :].astype(F32), logs_of(in1_ref, j),
-            in3_ref[rows, :].astype(F32), logs_of(in3_ref, j),
-        )
-        out_ref[0, :, head_cols((1 - side) * half + j)] = far.astype(BF16).T
-    done = start + FLAG_ROWS
-    blocks = [whole_ref[...]] + [ref[done : done + HD, :] for ref in (in1_ref, in2_ref, in3_ref)]
-    for rel, block in enumerate(blocks):
-        cols = head_cols(2 * half + jnp.bitwise_xor(me, rel))
-        out_ref[0, :, cols] = block.T
+    leave(side * half, half)
+    for copy in copies:
+        copy.wait()
 
 
 def send(array, rel):
@@ -320,19 +338,19 @@
     far_rows = half * TILE + span + FLAG_ROWS
     back_rows = half * HD + FLAG_ROWS
     arrays = (tile_mask, frame_list, frame_place, queries, keys, values, cache_keys, cache_values)
-    near1 = pl.pallas_call(
-        functools.partial(pack_kernel, half, (1,)),
+    near1, far3, far2 = pl.pallas_call(
+        functools.partial(pack_kernel, half, (1, 3, 2)),
+        out_shape=(pltpu.VMEM((pair_rows, HD), BF16),)
+        + (pltpu.VMEM((far_rows, HD), BF16),) * 2,
+        in_specs=[SMEM] * 3 + [VMEM] * 5,
+        out_specs=(VMEM,) * 3,
+    )(*arrays)
+    near0 = pl.pallas_call(
+        functools.partial(pack_kernel, half, (0,)),
         out_shape=pltpu.VMEM((pair_rows, HD), BF16),
-        in_specs=[SMEM] * 3 + [VMEM] * 5,
+        in_specs=[SMEM] * 3 + [VMEM] * 6,
         out_specs=VMEM,
-    )(*arrays)
-    far3, far2, near0 = pl.pallas_call(
-        functools.partial(pack_kernel, half, (3, 2, 0)),
-        out_shape=(pltpu.VMEM((far_rows, HD), BF16),) * 2
-        + (pltpu.VMEM((pair_rows, HD), BF16),),
-        in_specs=[SMEM] * 3 + [VMEM] * 6,
-        out_specs=(VMEM,) * 3,
-    )(*arrays, near(near1))
+    )(*arrays, near(far2))
     near0, near1 = near(near0), near(send(near1, 1))
     far3, far2 = near(send(far3, 3)), near(send(far2, 2))
     own, own_log, whole, back1, back2, back3 = pl.pallas_call(
@@ -350,7 +368,8 @@
         functools.partial(merge_kernel, half),
         out_shape=jax.ShapeDtypeStruct(queries.shape, BF16),
         in_specs=[VMEM] * 6,
-        out_specs=VMEM,
+        out_specs=pl.BlockSpec(memory_space=pl.ANY),
+        scratch_shapes=[pltpu.VMEM(queries.shape, BF16), pltpu.SemaphoreType.DMA((3,))],
     )(near(own), near(own_log), back2, back1, back3, near(whole))
 
 

time: 42.9 us -> 42.8 us (level)
  waiting for transfers between devices: 27 us -> 26.4 us
  starting transfers between devices: 10.3 us -> 10.9 us
    ppermute x6, waiting for transfers between devices: 27 us -> 26.4 us  [send(): return lax.ppermute(array, 'seq', [(i, i ^ rel) for i in range(4)])]
    ppermute x6, starting transfers between devices: 10.3 us -> 10.9 us  [send(): return lax.ppermute(array, 'seq', [(i, i ^ rel) for i in range(4)])]
  transfers between devices with their start and end apart: 6 -> 6, of which waited for: 4 -> 5; matrix products, arithmetic and copies ran while one was open for 0% -> 0% of each run, Pallas kernels for 4% -> 3%
where the time goes in v5:
time: 42.8 us; the launch traced here: 42.7 us
  waiting for transfers between devices  26.4 us (62%)
  starting transfers between devices  10.9 us (25%)
  Pallas kernels  5.4 us (13%)
    ppermute x6, waiting for transfers between devices, send(): return lax.ppermute(array, 'seq', [(i, i ^ rel) for i in range(4)])  26.4 us
    ppermute x6, starting transfers between devices, send(): return lax.ppermute(array, 'seq', [(i, i ^ rel) for i in range(4)])  10.9 us
    pallas_call x1, Pallas kernels, exchanged(): pl.pallas_call(functools.partial(attend_kernel, half, frames, frame_tok),...  1.62 us
    pallas_call x1, Pallas kernels, exchanged(): pl.pallas_call(functools.partial(pack_kernel, half, (1, 3, 2)), out_shape...  1.5 us
    pallas_call x1, Pallas kernels, exchanged(): pl.pallas_call(functools.partial(pack_kernel, half, (0,)), out_shape=pltp...  1.43 us
  transfers between devices with their start and end apart: 6, of which 5 were waited for; matrix products, arithmetic and copies ran while one was open for 0% of the time, Pallas kernels for 3%

profile of v5, /device:TPU:0, one launch (start us, length us, event | category | flops | bytes accessed | tf_op | source)
XLA Modules:
  0.0 42.7 jit_solution(2348868371874957955)
XLA Ops:
  0.0 1.5 %shard_map.82 = (bf16[2064,128]{1,0:T(8,128)(2,1)S(1)}, bf16[912,128]{1,0:T(8,128)(2,1)S(1)}, bf16[912,128]{1,0:T(8,128)(2,1)S(1)}) custom-call(s32[1,1,4]{2,1,0:T(1,128)} %mask_ref.3, s32[1,3]{1,0:T(1,128)} %list_ref.3, s32[1,8]{1,0:T(1,128)} %place_ref.3, bf16[1,128,1280]{2,1,0:T(8,128)(2,1)} %q_ref.3, bf16[1,128,1280]{2,1,0:T(8,128)(2,1)} %k_ref.3, ...), custom_call_target="tpu_custom_call" | custom-call | tf_op jit(solution)/shard_map/pallas_call | solution.py:341
  1.5 3.1 %collective-permute-start = (bf16[2064,128]{1,0:T(8,128)(2,1)S(1)}, bf16[2064,128]{1,0:T(8,128)(2,1)S(1)}, u32[]{:S(2)}, u32[]{:S(2)}) collective-permute-start(bf16[2064,128]{1,0:T(8,128)(2,1)S(1)} %get-tuple-element.15), channel_id=1, source_target_pairs={{0,4},{4,0},{8,12},{12,8},{1,5},{5,1},{9,13},{13,9},{2,6},{6,2},{1... | collective-permute-start | bytes 1585160 | tf_op jit(solution)/shard_map/ppermute | solution.py:325
  4.6 2.5 %collective-permute-start.1 = (bf16[912,128]{1,0:T(8,128)(2,1)S(1)}, bf16[912,128]{1,0:T(8,128)(2,1)S(1)}, u32[]{:S(2)}, u32[]{:S(2)}) collective-permute-start(bf16[912,128]{1,0:T(8,128)(2,1)S(1)} %get-tuple-element.16), channel_id=1, source_target_pairs={{0,12},{4,8},{8,4},{12,0},{1,13},{5,9},{9,5},{13,1},{2,14},{6,10},... | collective-permute-start | bytes 700424 | tf_op jit(solution)/shard_map/ppermute | solution.py:325
  7.1 0.1 collective-permute-start.2
  7.2 1.4 %shard_map.83.near0_ref = bf16[2064,128]{1,0:T(8,128)(2,1)S(1)} custom-call(s32[1,1,4]{2,1,0:T(1,128)} %mask_ref.3, s32[1,3]{1,0:T(1,128)} %list_ref.3, s32[1,8]{1,0:T(1,128)} %place_ref.3, bf16[1,128,1280]{2,1,0:T(8,128)(2,1)} %q_ref.3, bf16[1,128,1280]{2,1,0:T(8,128)(2,1)} %k_ref.3, bf16[1,128,1280]{2,1,0:T(8,128)(2,1)} %v_ref.3, ...), custom_call_target="tpu_custom_call" | custom-call | tf_op jit(solution)/shard_map/pallas_call | solution.py:348
  8.6 16.3 %collective-permute-done.1.far3_ref = bf16[912,128]{1,0:T(8,128)(2,1)S(1)} collective-permute-done((bf16[912,128]{1,0:T(8,128)(2,1)S(1)}, bf16[912,128]{1,0:T(8,128)(2,1)S(1)}, u32[]{:S(2)}, u32[]{:S(2)}) %collective-permute-start.1) | collective-permute-done | bytes 233504 | tf_op jit(solution)/shard_map/ppermute | solution.py:325
  24.9 1.0 %collective-permute-done.2.far2_ref = bf16[912,128]{1,0:T(8,128)(2,1)S(1)} collective-permute-done((bf16[912,128]{1,0:T(8,128)(2,1)S(1)}, bf16[912,128]{1,0:T(8,128)(2,1)S(1)}, u32[]{:S(2)}, u32[]{:S(2)}) %collective-permute-start.2) | collective-permute-done | bytes 233504 | tf_op jit(solution)/shard_map/ppermute | solution.py:325
  25.9 0.7 %collective-permute-done.near1_ref = bf16[2064,128]{1,0:T(8,128)(2,1)S(1)} collective-permute-done((bf16[2064,128]{1,0:T(8,128)(2,1)S(1)}, bf16[2064,128]{1,0:T(8,128)(2,1)S(1)}, u32[]{:S(2)}, u32[]{:S(2)}) %collective-permute-start) | collective-permute-done | bytes 528416 | tf_op jit(solution)/shard_map/ppermute | solution.py:325
  26.6 1.6 %shard_map.84 = (f32[384,128]{1,0:T(8,128)S(1)}, f32[3,128]{1,0:T(4,128)S(1)}, bf16[128,128]{1,0:T(8,128)(2,1)S(1)}, bf16[528,128]{1,0:T(8,128)(2,1)S(1)}, bf16[...) custom-call(bf16[2064,128]{1,0:T(8,128)(2,1)S(1)} %shard_map.83.near0_ref, ...), custom_call_target="tpu_custom_call" | custom-call | tf_op jit(solution)/shard_map/pallas_call | solution.py:356
  28.2 2.8 %collective-permute-start.3 = (bf16[528,128]{1,0:T(8,128)(2,1)S(1)}, bf16[528,128]{1,0:T(8,128)(2,1)S(1)}, u32[]{:S(2)}, u32[]{:S(2)}) collective-permute-start(bf16[528,128]{1,0:T(8,128)(2,1)S(1)} %get-tuple-element.19), channel_id=1, source_target_pairs={{0,8},{4,12},{8,0},{12,4},{1,9},{5,13},{9,1},{13,5},{2,10},{6,14},... | collective-permute-start | bytes 405512 | tf_op jit(solution)/shard_map/ppermute | solution.py:325
  31.0 1.6 %collective-permute-start.4 = (bf16[528,128]{1,0:T(8,128)(2,1)S(1)}, bf16[528,128]{1,0:T(8,128)(2,1)S(1)}, u32[]{:S(2)}, u32[]{:S(2)}) collective-permute-start(bf16[528,128]{1,0:T(8,128)(2,1)S(1)} %get-tuple-element.20), channel_id=1, source_target_pairs={{0,4},{4,0},{8,12},{12,8},{1,5},{5,1},{9,13},{13,9},{2,6},{6,2},{1... | collective-permute-start | bytes 405512 | tf_op jit(solution)/shard_map/ppermute | solution.py:325
  32.6 0.8 %collective-permute-start.5 = (bf16[528,128]{1,0:T(8,128)(2,1)S(1)}, bf16[528,128]{1,0:T(8,128)(2,1)S(1)}, u32[]{:S(2)}, u32[]{:S(2)}) collective-permute-start(bf16[528,128]{1,0:T(8,128)(2,1)S(1)} %get-tuple-element.21), channel_id=1, source_target_pairs={{0,12},{4,8},{8,4},{12,0},{1,13},{5,9},{9,5},{13,1},{2,14},{6,10},... | collective-permute-start | bytes 405512 | tf_op jit(solution)/shard_map/ppermute | solution.py:325
  33.4 6.3 %collective-permute-done.3.in2_ref = bf16[528,128]{1,0:T(8,128)(2,1)S(1)} collective-permute-done((bf16[528,128]{1,0:T(8,128)(2,1)S(1)}, bf16[528,128]{1,0:T(8,128)(2,1)S(1)}, u32[]{:S(2)}, u32[]{:S(2)}) %collective-permute-start.3) | collective-permute-done | bytes 135200 | tf_op jit(solution)/shard_map/ppermute | solution.py:325
  39.7 0.0 collective-permute-done.4.in1_ref
  39.7 2.1 %collective-permute-done.5.in3_ref = bf16[528,128]{1,0:T(8,128)(2,1)S(1)} collective-permute-done((bf16[528,128]{1,0:T(8,128)(2,1)S(1)}, bf16[528,128]{1,0:T(8,128)(2,1)S(1)}, u32[]{:S(2)}, u32[]{:S(2)}) %collective-permute-start.5) | collective-permute-done | bytes 135200 | tf_op jit(solution)/shard_map/ppermute | solution.py:325
  41.8 0.9 %shard_map.85 = bf16[1,128,1280]{2,1,0:T(8,128)(2,1)} custom-call(f32[384,128]{1,0:T(8,128)S(1)} %get-tuple-element.17.own_ref, f32[3,128]{1,0:T(4,128)S(1)} %get-tuple-element.18.own_log_ref, bf16[528,128]{1,0:T(8,128)(2,1)S(1)} %collective-permute-done.3.in2_ref, bf16[528,128]{1,0:T(8,128)(2,1)S(1)} %collective-permute-done.4.in1_ref, ...), custom_call_target="tpu_custom_call" | custom-call | tf_op jit(solution)/shard_map/pallas_call | solution.py:367
Async XLA Ops:
  1.5 25.1 %collective-permute-start = (bf16[2064,128]{1,0:T(8,128)(2,1)S(1)}, bf16[2064,128]{1,0:T(8,128)(2,1)S(1)}, u32[]{:S(2)}, u32[]{:S(2)}) collective-permute-start(bf16[2064,128]{1,0:T(8,128)(2,1)S(1)} %get-tuple-element.15), channel_id=1, source_target_pairs={{0,4},{4,0},{8,12},{12,8},{1,5},{5,1},{9,13},{13,9},{2,6},{6,2},{1... | collective-permute-start | bytes 1585160 | tf_op jit(solution)/shard_map/ppermute | solution.py:325
  4.6 20.4 %collective-permute-start.1 = (bf16[912,128]{1,0:T(8,128)(2,1)S(1)}, bf16[912,128]{1,0:T(8,128)(2,1)S(1)}, u32[]{:S(2)}, u32[]{:S(2)}) collective-permute-start(bf16[912,128]{1,0:T(8,128)(2,1)S(1)} %get-tuple-element.16), channel_id=1, source_target_pairs={{0,12},{4,8},{8,4},{12,0},{1,13},{5,9},{9,5},{13,1},{2,14},{6,10},... | collective-permute-start | bytes 700424 | tf_op jit(solution)/shard_map/ppermute | solution.py:325
  7.1 18.8 %collective-permute-start.2 = (bf16[912,128]{1,0:T(8,128)(2,1)S(1)}, bf16[912,128]{1,0:T(8,128)(2,1)S(1)}, u32[]{:S(2)}, u32[]{:S(2)}) collective-permute-start(bf16[912,128]{1,0:T(8,128)(2,1)S(1)} %get-tuple-element.14.out_refs_0_), channel_id=1, source_target_pairs={{0,8},{4,12},{8,0},{12,4},{1,9},{5,13},{9,1},{13,5},{2,10},{6,14},... | collective-permute-start | bytes 700424 | tf_op jit(solution)/shard_map/ppermute | solution.py:325
  28.2 11.5 %collective-permute-start.3 = (bf16[528,128]{1,0:T(8,128)(2,1)S(1)}, bf16[528,128]{1,0:T(8,128)(2,1)S(1)}, u32[]{:S(2)}, u32[]{:S(2)}) collective-permute-start(bf16[528,128]{1,0:T(8,128)(2,1)S(1)} %get-tuple-element.19), channel_id=1, source_target_pairs={{0,8},{4,12},{8,0},{12,4},{1,9},{5,13},{9,1},{13,5},{2,10},{6,14},... | collective-permute-start | bytes 405512 | tf_op jit(solution)/shard_map/ppermute | solution.py:325
  31.0 8.7 %collective-permute-start.4 = (bf16[528,128]{1,0:T(8,128)(2,1)S(1)}, bf16[528,128]{1,0:T(8,128)(2,1)S(1)}, u32[]{:S(2)}, u32[]{:S(2)}) collective-permute-start(bf16[528,128]{1,0:T(8,128)(2,1)S(1)} %get-tuple-element.20), channel_id=1, source_target_pairs={{0,4},{4,0},{8,12},{12,8},{1,5},{5,1},{9,13},{13,9},{2,6},{6,2},{1... | collective-permute-start | bytes 405512 | tf_op jit(solution)/shard_map/ppermute | solution.py:325
  32.6 9.2 %collective-permute-start.5 = (bf16[528,128]{1,0:T(8,128)(2,1)S(1)}, bf16[528,128]{1,0:T(8,128)(2,1)S(1)}, u32[]{:S(2)}, u32[]{:S(2)}) collective-permute-start(bf16[528,128]{1,0:T(8,128)(2,1)S(1)} %get-tuple-element.21), channel_id=1, source_target_pairs={{0,12},{4,8},{8,4},{12,0},{1,13},{5,9},{9,5},{13,1},{2,14},{6,10},... | collective-permute-start | bytes 405512 | tf_op jit(solution)/shard_map/ppermute | solution.py:325

commit v6 on v5

--- a/solution.py
+++ b/solution.py
@@ -120,28 +120,55 @@
     return row
 
 
-def pack_kernel(
-    half, rels, mask_ref, list_ref, place_ref, q_ref, k_ref, v_ref, ck_ref, cv_ref, *out_refs
-):
+def pack_copies(half, rel, me, parts, out):
+    side = lax.rem(me, 2)
+    group = (1 - side) if rel % 2 else side
+    heads = [group * half + j for j in range(half)] + [2 * half + jnp.bitwise_xor(me, rel)]
+    views = []
+    row = 0
+    for j, head in enumerate(heads):
+        for part in parts if rel < 2 or j == half else parts[:1]:
+            pieces = [(0,)] if len(part.shape) == 3 else [(0, i) for i in range(part.shape[1])]
+            for piece in pieces:
+                count = part.shape[-2]
+                source = part.at[(*piece, slice(None), head_cols(head))]
+                views.append((source, out.at[pl.ds(row, count), :]))
+                row += count
+    return views
+
+
+def pack_kernel(half, rels, *refs):
+    scalars, parts = refs[:3], refs[3:8]
+    mask_ref, list_ref, place_ref, sems = refs[-4:]
+    out_refs = refs[-4 - len(rels) : -4]
     me = lax.axis_index("seq")
-    side = lax.rem(me, 2)
-    parts = (q_ref, k_ref, v_ref, ck_ref, cv_ref)
-    for rel, out in zip(rels, out_refs[-len(rels) :]):
+    views = list(zip(scalars, (mask_ref, list_ref, place_ref)))[: 3 if 0 in rels else 1]
+    used = len(views)
+    for rel, out in zip(rels, out_refs):
+        views += pack_copies(half, rel, me, parts, out)
+    copies = [
+        pltpu.make_async_copy(source, target, sems.at[i])
+        for i, (source, target) in enumerate(views)
+    ]
+    for copy in copies:
+        copy.start()
+    for copy in copies[:used]:
+        copy.wait()
+    for rel, out in zip(rels, out_refs):
         other = jnp.bitwise_xor(me, rel)
-        group = (1 - side) if rel % 2 else side
-        row = 0
-        for j in range(half):
-            row = put(out, row, parts if rel < 2 else parts[:1], group * half + j)
-        row = put(out, row, parts, 2 * half + other)
         ident = lax.broadcasted_iota(jnp.int32, (FLAG_ROWS, HD), 0)
         block = jnp.zeros((FLAG_ROWS, HD), F32)
         for key in range(4):
             live = mask_ref[0, 0, jnp.bitwise_xor(other, key)] > 0
             block = jnp.where(ident == key, fill(live), block)
         if rel == 0:
-            for key, value in enumerate(frame_fills(place_ref, list_ref, me, ck_ref.shape[1]), 4):
+            frames = parts[3].shape[1]
+            for key, value in enumerate(frame_fills(place_ref, list_ref, me, frames), 4):
                 block = jnp.where(ident == key, value, block)
+        row = out.shape[0] - FLAG_ROWS
         out[row : row + FLAG_ROWS, :] = block.astype(BF16)
+    for copy in copies[used:]:
+        copy.wait()
 
 
 def eights(block, reduce):
@@ -181,7 +208,7 @@
     ]
     for key in range(4, 4 + 4 * frames):
         row = blocks[0][key : key + 1, :]
-        fills.append((frame_tok, jnp.concatenate([row] * 4, axis=1)))
+        fills.append((frame_tok, jnp.concatenate([row] * len(refs), axis=1)))
     return fills
 
 
@@ -230,39 +257,63 @@
     return jnp.concatenate(rows + [jnp.zeros((spare, TILE), F32)], axis=0).astype(BF16)
 
 
-def attend_kernel(
-    half, frames, frame_tok,
-    near0_ref, near1_ref, far3_ref, far2_ref,
-    own_ref, own_log_ref, whole_ref, out1_ref, out2_ref, out3_ref,
+def early_kernel(
+    half, frames, frame_tok, near0_ref, near1_ref, far3_ref,
+    own_ref, own_log_ref, out1_ref, out3_ref,
+):
+    cache = frames * frame_tok
+    span = 3 * TILE + 2 * cache
+    fills = all_fills((near0_ref, near1_ref, far3_ref), frames, frame_tok)
+    fills = fills[:2] + fills[4 : 4 + 2 * frames]
+    tasks = []
+    for j in range(half):
+        pair = ((near0_ref, j * span), (near1_ref, j * span))
+        tasks.append((pair + ((far3_ref, j * TILE),), pair, fills))
+    stats = [[], []]
+    outs = (out1_ref, out3_ref)
+    for j, (summed, logs) in enumerate(attend_parts(tasks, cache)):
+        rows = slice(j * HD, (j + 1) * HD)
+        own_ref[rows, :] = summed[:, :TILE]
+        own_log_ref[j : j + 1, :] = logs[:, :TILE]
+        for i, out in enumerate(outs):
+            cols = slice((i + 1) * TILE, (i + 2) * TILE)
+            out[rows, :] = summed[:, cols].astype(BF16)
+            stats[i] += three_parts(logs[:, cols])
+    for i, out in enumerate(outs):
+        out[half * HD : half * HD + FLAG_ROWS, :] = stat_block(stats[i])
+
+
+def late_kernel(
+    half, frames, frame_tok, near0_ref, near1_ref, far3_ref, far2_ref, early1_ref, early3_ref,
+    whole_ref, out1_ref, out2_ref, out3_ref,
 ):
     cache = frames * frame_tok
     span = 3 * TILE + 2 * cache
     ins = (near0_ref, near1_ref, far2_ref, far3_ref)
-    outs = (out1_ref, out2_ref, out3_ref)
     fills = all_fills(ins, frames, frame_tok)
-    pair_fills = fills[:2] + fills[4 : 4 + 2 * frames]
+    cols = slice(2 * TILE, 3 * TILE)
+    pair_fills = [
+        (count, value[:, cols]) for count, value in fills[:2] + fills[4 : 4 + 2 * frames]
+    ]
     tasks = []
     for j in range(half):
         pair = ((near0_ref, j * span), (near1_ref, j * span))
-        tasks.append((pair + ((far2_ref, j * TILE), (far3_ref, j * TILE)), pair, pair_fills))
+        tasks.append((((far2_ref, j * TILE),), pair, pair_fills))
     places = [(ref, half * span) for ref in ins[:2]] + [(ref, half * TILE) for ref in ins[2:]]
     tasks.append((places, places, fills))
     *parts, (whole, _) = attend_parts(tasks, cache)
-    stats = [[], [], []]
+    stats = []
     for j, (summed, logs) in enumerate(parts):
-        rows = slice(j * HD, (j + 1) * HD)
-        own_ref[rows, :] = summed[:, :TILE]
-        own_log_ref[j : j + 1, :] = logs[:, :TILE]
-        for rel, out in enumerate(outs, 1):
-            cols = slice(rel * TILE, (rel + 1) * TILE)
-            out[rows, :] = summed[:, cols].astype(BF16)
-            stats[rel - 1] += three_parts(logs[:, cols])
+        out2_ref[j * HD : (j + 1) * HD, :] = summed.astype(BF16)
+        stats += three_parts(logs)
     row = half * HD
-    for rel, out in enumerate(outs, 1):
-        out[row : row + FLAG_ROWS, :] = stat_block(stats[rel - 1])
-        start = row + FLAG_ROWS
+    start = row + FLAG_ROWS
+    out2_ref[row:start, :] = stat_block(stats)
+    out1_ref[0:start, :] = early1_ref[...]
+    out3_ref[0:start, :] = early3_ref[...]
+    whole_ref[...] = whole[:, :TILE].astype(BF16)
+    for rel, out in enumerate((out1_ref, out2_ref, out3_ref), 1):
         out[start : start + HD, :] = whole[:, rel * TILE : (rel + 1) * TILE].astype(BF16)
-    whole_ref[...] = whole[:, :TILE].astype(BF16)
 
 
 def merge_kernel(
@@ -337,32 +388,48 @@
     pair_rows = (half + 1) * span + FLAG_ROWS
     far_rows = half * TILE + span + FLAG_ROWS
     back_rows = half * HD + FLAG_ROWS
+    scalars = [pltpu.SMEM(array.shape, jnp.int32) for array in (tile_mask, frame_list, frame_place)]
+    once = [pl.BlockSpec(memory_space=pl.ANY)]
     arrays = (tile_mask, frame_list, frame_place, queries, keys, values, cache_keys, cache_values)
-    near1, far3, far2 = pl.pallas_call(
-        functools.partial(pack_kernel, half, (1, 3, 2)),
-        out_shape=(pltpu.VMEM((pair_rows, HD), BF16),)
-        + (pltpu.VMEM((far_rows, HD), BF16),) * 2,
-        in_specs=[SMEM] * 3 + [VMEM] * 5,
-        out_specs=(VMEM,) * 3,
+    near1 = pl.pallas_call(
+        functools.partial(pack_kernel, half, (1,)),
+        out_shape=pltpu.VMEM((pair_rows, HD), BF16),
+        in_specs=once * 8,
+        out_specs=VMEM,
+        scratch_shapes=scalars + [pltpu.SemaphoreType.DMA((3 + (half + 1) * (3 + 2 * frames),))],
     )(*arrays)
+    far3, far2 = pl.pallas_call(
+        functools.partial(pack_kernel, half, (3, 2)),
+        out_shape=(pltpu.VMEM((far_rows, HD), BF16),) * 2,
+        in_specs=once * 9,
+        out_specs=(VMEM,) * 2,
+        scratch_shapes=scalars + [pltpu.SemaphoreType.DMA((3 + 2 * (half + 3 + 2 * frames),))],
+    )(*arrays, near(near1))
     near0 = pl.pallas_call(
         functools.partial(pack_kernel, half, (0,)),
         out_shape=pltpu.VMEM((pair_rows, HD), BF16),
-        in_specs=[SMEM] * 3 + [VMEM] * 6,
+        in_specs=once * 9,
         out_specs=VMEM,
+        scratch_shapes=scalars + [pltpu.SemaphoreType.DMA((3 + (half + 1) * (3 + 2 * frames),))],
     )(*arrays, near(far2))
     near0, near1 = near(near0), near(send(near1, 1))
     far3, far2 = near(send(far3, 3)), near(send(far2, 2))
-    own, own_log, whole, back1, back2, back3 = pl.pallas_call(
-        functools.partial(attend_kernel, half, frames, frame_tok),
+    own, own_log, early1, early3 = pl.pallas_call(
+        functools.partial(early_kernel, half, frames, frame_tok),
         out_shape=(
             pltpu.VMEM((half * HD, TILE), F32),
             pltpu.VMEM((half, TILE), F32),
-            pltpu.VMEM((HD, TILE), BF16),
-        ) + (pltpu.VMEM((back_rows + HD, TILE), BF16),) * 3,
-        in_specs=[VMEM] * 4,
-        out_specs=(VMEM,) * 6,
-    )(near0, near1, far3, far2)
+        ) + (pltpu.VMEM((back_rows, TILE), BF16),) * 2,
+        in_specs=[VMEM] * 3,
+        out_specs=(VMEM,) * 4,
+    )(near0, near1, far3)
+    whole, back1, back2, back3 = pl.pallas_call(
+        functools.partial(late_kernel, half, frames, frame_tok),
+        out_shape=(pltpu.VMEM((HD, TILE), BF16),)
+        + (pltpu.VMEM((back_rows + HD, TILE), BF16),) * 3,
+        in_specs=[VMEM] * 6,
+        out_specs=(VMEM,) * 4,
+    )(near0, near1, far3, far2, near(early1), near(early3))
     back2, back1, back3 = near(send(back2, 2)), near(send(back1, 1)), near(send(back3, 3))
     return pl.pallas_call(
         functools.partial(merge_kernel, half),

time: 42.8 us -> 42.5 us (level)
  Pallas kernels: 5.4 us -> 6.53 us
  waiting for transfers between devices: 26.4 us -> 25.3 us
  starting transfers between devices: 10.9 us -> 10.3 us
    pallas_call x2 -> x4, Pallas kernels: 3.11 us -> 4.36 us  [the longest x1 1.32 us: exchanged(): pl.pallas_call(functools.partial(pack_kernel, half, (1,)), out_shape=pltp...]
    ppermute x6, waiting for transfers between devices: 26.4 us -> 25.3 us  [send(): return lax.ppermute(array, 'seq', [(i, i ^ rel) for i in range(4)])]
    ppermute x6, starting transfers between devices: 10.9 us -> 10.3 us  [send(): return lax.ppermute(array, 'seq', [(i, i ^ rel) for i in range(4)])]
  transfers between devices with their start and end apart: 6 -> 6, of which waited for: 5 -> 4; matrix products, arithmetic and copies ran while one was open for 0% -> 0% of each run, Pallas kernels for 3% -> 8%
where the time goes in v6:
time: 42.5 us; the launch traced here: 42.1 us
  waiting for transfers between devices  25.3 us (60%)
  starting transfers between devices  10.3 us (24%)
  Pallas kernels  6.53 us (15%)
    ppermute x6, waiting for transfers between devices, send(): return lax.ppermute(array, 'seq', [(i, i ^ rel) for i in range(4)])  25.3 us
    ppermute x6, starting transfers between devices, send(): return lax.ppermute(array, 'seq', [(i, i ^ rel) for i in range(4)])  10.3 us
    pallas_call x1, Pallas kernels, exchanged(): pl.pallas_call(functools.partial(pack_kernel, half, (0,)), out_shape=pltp...  1.32 us
    pallas_call x1, Pallas kernels, exchanged(): pl.pallas_call(functools.partial(pack_kernel, half, (1,)), out_shape=pltp...  1.32 us
    pallas_call x1, Pallas kernels, exchanged(): pl.pallas_call(functools.partial(pack_kernel, half, (3, 2)), out_shape=(p...  1.19 us
    pallas_call x1, Pallas kernels, exchanged(): pl.pallas_call(functools.partial(late_kernel, half, frames, frame_tok), o...  0.98 us
    pallas_call x1, Pallas kernels, exchanged(): pl.pallas_call(functools.partial(early_kernel, half, frames, frame_tok),...  0.87 us
    pallas_call x1, Pallas kernels, exchanged(): pl.pallas_call(functools.partial(merge_kernel, half), out_shape=jax.Shape...  0.86 us
  transfers between devices with their start and end apart: 6, of which 4 were waited for; matrix products, arithmetic and copies ran while one was open for 0% of the time, Pallas kernels for 8%

profile of v6, /device:TPU:0, one launch (start us, length us, event | category | flops | bytes accessed | tf_op | source)
XLA Modules:
  0.0 42.1 jit_solution(13905201719438811304)
XLA Ops:
  0.0 1.3 %shard_map.82.refs_8_ = bf16[2064,128]{1,0:T(8,128)(2,1)S(1)} custom-call(s32[1,1,4]{2,1,0:T(1,128)} %refs_0_.5, s32[1,3]{1,0:T(1,128)} %refs_1_.5, s32[1,8]{1,0:T(1,128)} %refs_2_.5, bf16[1,128,1280]{2,1,0:T(8,128)(2,1)} %refs_3_.5, bf16[1,128,1280]{2,1,0:T(8,128)(2,1)} %refs_4_.5, bf16[1,128,1280]{2,1,0:T(8,128)(2,1)} %refs_5_.5, ...), custom_call_target="tpu_custom_call" | custom-call | tf_op jit(solution)/shard_map/pallas_call | solution.py:394
  1.3 3.1 %collective-permute-start = (bf16[2064,128]{1,0:T(8,128)(2,1)S(1)}, bf16[2064,128]{1,0:T(8,128)(2,1)S(1)}, u32[]{:S(2)}, u32[]{:S(2)}) collective-permute-start(bf16[2064,128]{1,0:T(8,128)(2,1)S(1)} %shard_map.82.refs_8_), channel_id=1, source_target_pairs={{0,4},{4,0},{8,12},{12,8},{1,5},{5,1},{9,13},{13,9},{2,6},{6,2},{1... | collective-permute-start | bytes 1585160 | tf_op jit(solution)/shard_map/ppermute | solution.py:376
  4.4 1.2 %shard_map.83 = (bf16[912,128]{1,0:T(8,128)(2,1)S(1)}, bf16[912,128]{1,0:T(8,128)(2,1)S(1)}) custom-call(s32[1,1,4]{2,1,0:T(1,128)} %refs_0_.5, s32[1,3]{1,0:T(1,128)} %refs_1_.5, s32[1,8]{1,0:T(1,128)} %refs_2_.5, bf16[1,128,1280]{2,1,0:T(8,128)(2,1)} %refs_3_.5, bf16[1,128,1280]{2,1,0:T(8,128)(2,1)} %refs_4_.5, bf16[1,128,1280]{2,1,0:T(8,128)(2,1)} %refs_5_.5, ...), custom_call_target="tpu_custom_call" | custom-call | tf_op jit(solution)/shard_map/pallas_call | solution.py:401
  5.6 2.5 %collective-permute-start.1 = (bf16[912,128]{1,0:T(8,128)(2,1)S(1)}, bf16[912,128]{1,0:T(8,128)(2,1)S(1)}, u32[]{:S(2)}, u32[]{:S(2)}) collective-permute-start(bf16[912,128]{1,0:T(8,128)(2,1)S(1)} %get-tuple-element.16), channel_id=1, source_target_pairs={{0,12},{4,8},{8,4},{12,0},{1,13},{5,9},{9,5},{13,1},{2,14},{6,10},... | collective-permute-start | bytes 700424 | tf_op jit(solution)/shard_map/ppermute | solution.py:376
  8.2 0.2 collective-permute-start.2
  8.3 1.3 %shard_map.84.near0_ref = bf16[2064,128]{1,0:T(8,128)(2,1)S(1)} custom-call(s32[1,1,4]{2,1,0:T(1,128)} %refs_0_.5, s32[1,3]{1,0:T(1,128)} %refs_1_.5, s32[1,8]{1,0:T(1,128)} %refs_2_.5, bf16[1,128,1280]{2,1,0:T(8,128)(2,1)} %refs_3_.5, bf16[1,128,1280]{2,1,0:T(8,128)(2,1)} %refs_4_.5, bf16[1,128,1280]{2,1,0:T(8,128)(2,1)} %refs_5_.5, ...), custom_call_target="tpu_custom_call" | custom-call | tf_op jit(solution)/shard_map/pallas_call | solution.py:408
  9.7 15.2 %collective-permute-done.1.far3_ref = bf16[912,128]{1,0:T(8,128)(2,1)S(1)} collective-permute-done((bf16[912,128]{1,0:T(8,128)(2,1)S(1)}, bf16[912,128]{1,0:T(8,128)(2,1)S(1)}, u32[]{:S(2)}, u32[]{:S(2)}) %collective-permute-start.1) | collective-permute-done | bytes 233504 | tf_op jit(solution)/shard_map/ppermute | solution.py:376
  24.9 1.6 %collective-permute-done.near1_ref = bf16[2064,128]{1,0:T(8,128)(2,1)S(1)} collective-permute-done((bf16[2064,128]{1,0:T(8,128)(2,1)S(1)}, bf16[2064,128]{1,0:T(8,128)(2,1)S(1)}, u32[]{:S(2)}, u32[]{:S(2)}) %collective-permute-start) | collective-permute-done | bytes 528416 | tf_op jit(solution)/shard_map/ppermute | solution.py:376
  26.4 0.9 %shard_map.85 = (f32[384,128]{1,0:T(8,128)S(1)}, f32[3,128]{1,0:T(4,128)S(1)}, bf16[400,128]{1,0:T(8,128)(2,1)S(1)}, bf16[400,128]{1,0:T(8,128)(2,1)S(1)}) custom-call(bf16[2064,128]{1,0:T(8,128)(2,1)S(1)} %shard_map.84.near0_ref, bf16[2064,128]{1,0:T(8,128)(2,1)S(1)} %collective-permute-done.near1_ref, bf16[912,128]{1,0:T(8,128)(2,1)S(1)} %collective-permute-done.1.far3_ref), custom_call_target="tpu_custom_call" | custom-call | tf_op jit(solution)/shard_map/pallas_call | solution.py:417
  27.3 1.4 %collective-permute-done.2.far2_ref = bf16[912,128]{1,0:T(8,128)(2,1)S(1)} collective-permute-done((bf16[912,128]{1,0:T(8,128)(2,1)S(1)}, bf16[912,128]{1,0:T(8,128)(2,1)S(1)}, u32[]{:S(2)}, u32[]{:S(2)}) %collective-permute-start.2) | collective-permute-done | bytes 233504 | tf_op jit(solution)/shard_map/ppermute | solution.py:376
  28.7 1.0 %shard_map.86 = (bf16[128,128]{1,0:T(8,128)(2,1)S(1)}, bf16[528,128]{1,0:T(8,128)(2,1)S(1)}, bf16[528,128]{1,0:T(8,128)(2,1)S(1)}, bf16[528,128]{1,0:T(8,128)(2,1)S(1)}) custom-call(bf16[2064,128]{1,0:T(8,128)(2,1)S(1)} %shard_map.84.near0_ref, bf16[2064,128]{1,0:T(8,128)(2,1)S(1)} %collective-permute-done.near1_ref, ...), custom_call_target="tpu_custom_call" | custom-call | tf_op jit(solution)/shard_map/pallas_call | solution.py:426
  29.7 0.5 %collective-permute-start.3 = (bf16[528,128]{1,0:T(8,128)(2,1)S(1)}, bf16[528,128]{1,0:T(8,128)(2,1)S(1)}, u32[]{:S(2)}, u32[]{:S(2)}) collective-permute-start(bf16[528,128]{1,0:T(8,128)(2,1)S(1)} %get-tuple-element.21), channel_id=1, source_target_pairs={{0,8},{4,12},{8,0},{12,4},{1,9},{5,13},{9,1},{13,5},{2,10},{6,14},... | collective-permute-start | bytes 405512 | tf_op jit(solution)/shard_map/ppermute | solution.py:376
  30.2 2.8 %collective-permute-start.4 = (bf16[528,128]{1,0:T(8,128)(2,1)S(1)}, bf16[528,128]{1,0:T(8,128)(2,1)S(1)}, u32[]{:S(2)}, u32[]{:S(2)}) collective-permute-start(bf16[528,128]{1,0:T(8,128)(2,1)S(1)} %get-tuple-element.22), channel_id=1, source_target_pairs={{0,4},{4,0},{8,12},{12,8},{1,5},{5,1},{9,13},{13,9},{2,6},{6,2},{1... | collective-permute-start | bytes 405512 | tf_op jit(solution)/shard_map/ppermute | solution.py:376
  33.0 1.2 %collective-permute-start.5 = (bf16[528,128]{1,0:T(8,128)(2,1)S(1)}, bf16[528,128]{1,0:T(8,128)(2,1)S(1)}, u32[]{:S(2)}, u32[]{:S(2)}) collective-permute-start(bf16[528,128]{1,0:T(8,128)(2,1)S(1)} %get-tuple-element.23), channel_id=1, source_target_pairs={{0,12},{4,8},{8,4},{12,0},{1,13},{5,9},{9,5},{13,1},{2,14},{6,10},... | collective-permute-start | bytes 405512 | tf_op jit(solution)/shard_map/ppermute | solution.py:376
  34.2 7.1 %collective-permute-done.3.in2_ref = bf16[528,128]{1,0:T(8,128)(2,1)S(1)} collective-permute-done((bf16[528,128]{1,0:T(8,128)(2,1)S(1)}, bf16[528,128]{1,0:T(8,128)(2,1)S(1)}, u32[]{:S(2)}, u32[]{:S(2)}) %collective-permute-start.3) | collective-permute-done | bytes 135200 | tf_op jit(solution)/shard_map/ppermute | solution.py:376
  41.3 0.0 collective-permute-done.4.in1_ref
  41.3 0.0 collective-permute-done.5.in3_ref
  41.3 0.9 %shard_map.87 = bf16[1,128,1280]{2,1,0:T(8,128)(2,1)} custom-call(f32[384,128]{1,0:T(8,128)S(1)} %get-tuple-element.17.own_ref, f32[3,128]{1,0:T(4,128)S(1)} %get-tuple-element.18.own_log_ref, bf16[528,128]{1,0:T(8,128)(2,1)S(1)} %collective-permute-done.3.in2_ref, bf16[528,128]{1,0:T(8,128)(2,1)S(1)} %collective-permute-done.4.in1_ref, ...), custom_call_target="tpu_custom_call" | custom-call | tf_op jit(solution)/shard_map/pallas_call | solution.py:434
Async XLA Ops:
  1.3 25.1 %collective-permute-start = (bf16[2064,128]{1,0:T(8,128)(2,1)S(1)}, bf16[2064,128]{1,0:T(8,128)(2,1)S(1)}, u32[]{:S(2)}, u32[]{:S(2)}) collective-permute-start(bf16[2064,128]{1,0:T(8,128)(2,1)S(1)} %shard_map.82.refs_8_), channel_id=1, source_target_pairs={{0,4},{4,0},{8,12},{12,8},{1,5},{5,1},{9,13},{13,9},{2,6},{6,2},{1... | collective-permute-start | bytes 1585160 | tf_op jit(solution)/shard_map/ppermute | solution.py:376
  5.6 19.3 %collective-permute-start.1 = (bf16[912,128]{1,0:T(8,128)(2,1)S(1)}, bf16[912,128]{1,0:T(8,128)(2,1)S(1)}, u32[]{:S(2)}, u32[]{:S(2)}) collective-permute-start(bf16[912,128]{1,0:T(8,128)(2,1)S(1)} %get-tuple-element.16), channel_id=1, source_target_pairs={{0,12},{4,8},{8,4},{12,0},{1,13},{5,9},{9,5},{13,1},{2,14},{6,10},... | collective-permute-start | bytes 700424 | tf_op jit(solution)/shard_map/ppermute | solution.py:376
  8.2 20.6 %collective-permute-start.2 = (bf16[912,128]{1,0:T(8,128)(2,1)S(1)}, bf16[912,128]{1,0:T(8,128)(2,1)S(1)}, u32[]{:S(2)}, u32[]{:S(2)}) collective-permute-start(bf16[912,128]{1,0:T(8,128)(2,1)S(1)} %get-tuple-element.15.refs_8_), channel_id=1, source_target_pairs={{0,8},{4,12},{8,0},{12,4},{1,9},{5,13},{9,1},{13,5},{2,10},{6,14},... | collective-permute-start | bytes 700424 | tf_op jit(solution)/shard_map/ppermute | solution.py:376
  29.7 11.5 %collective-permute-start.3 = (bf16[528,128]{1,0:T(8,128)(2,1)S(1)}, bf16[528,128]{1,0:T(8,128)(2,1)S(1)}, u32[]{:S(2)}, u32[]{:S(2)}) collective-permute-start(bf16[528,128]{1,0:T(8,128)(2,1)S(1)} %get-tuple-element.21), channel_id=1, source_target_pairs={{0,8},{4,12},{8,0},{12,4},{1,9},{5,13},{9,1},{13,5},{2,10},{6,14},... | collective-permute-start | bytes 405512 | tf_op jit(solution)/shard_map/ppermute | solution.py:376
  30.2 11.0 %collective-permute-start.4 = (bf16[528,128]{1,0:T(8,128)(2,1)S(1)}, bf16[528,128]{1,0:T(8,128)(2,1)S(1)}, u32[]{:S(2)}, u32[]{:S(2)}) collective-permute-start(bf16[528,128]{1,0:T(8,128)(2,1)S(1)} %get-tuple-element.22), channel_id=1, source_target_pairs={{0,4},{4,0},{8,12},{12,8},{1,5},{5,1},{9,13},{13,9},{2,6},{6,2},{1... | collective-permute-start | bytes 405512 | tf_op jit(solution)/shard_map/ppermute | solution.py:376
  33.0 8.3 %collective-permute-start.5 = (bf16[528,128]{1,0:T(8,128)(2,1)S(1)}, bf16[528,128]{1,0:T(8,128)(2,1)S(1)}, u32[]{:S(2)}, u32[]{:S(2)}) collective-permute-start(bf16[528,128]{1,0:T(8,128)(2,1)S(1)} %get-tuple-element.23), channel_id=1, source_target_pairs={{0,12},{4,8},{8,4},{12,0},{1,13},{5,9},{9,5},{13,1},{2,14},{6,10},... | collective-permute-start | bytes 405512 | tf_op jit(solution)/shard_map/ppermute | solution.py:376

commit v7 on v6

--- a/solution.py
+++ b/solution.py
@@ -280,13 +280,17 @@
             out[rows, :] = summed[:, cols].astype(BF16)
             stats[i] += three_parts(logs[:, cols])
     for i, out in enumerate(outs):
-        out[half * HD : half * HD + FLAG_ROWS, :] = stat_block(stats[i])
+        row = half * HD
+        out[row : row + FLAG_ROWS, :] = stat_block(stats[i])
+        row += FLAG_ROWS
+        out[row:, :] = jnp.zeros((out.shape[0] - row, TILE), BF16)
 
 
 def late_kernel(
-    half, frames, frame_tok, near0_ref, near1_ref, far3_ref, far2_ref, early1_ref, early3_ref,
-    whole_ref, out1_ref, out2_ref, out3_ref,
+    half, frames, frame_tok, near0_ref, near1_ref, far3_ref, far2_ref, before_ref,
+    out2_ref, *whole_refs,
 ):
+    del before_ref
     cache = frames * frame_tok
     span = 3 * TILE + 2 * cache
     ins = (near0_ref, near1_ref, far2_ref, far3_ref)
@@ -307,67 +311,58 @@
         out2_ref[j * HD : (j + 1) * HD, :] = summed.astype(BF16)
         stats += three_parts(logs)
     row = half * HD
-    start = row + FLAG_ROWS
-    out2_ref[row:start, :] = stat_block(stats)
-    out1_ref[0:start, :] = early1_ref[...]
-    out3_ref[0:start, :] = early3_ref[...]
-    whole_ref[...] = whole[:, :TILE].astype(BF16)
-    for rel, out in enumerate((out1_ref, out2_ref, out3_ref), 1):
-        out[start : start + HD, :] = whole[:, rel * TILE : (rel + 1) * TILE].astype(BF16)
+    out2_ref[row : row + FLAG_ROWS, :] = stat_block(stats)
+    for rel, out in enumerate(whole_refs):
+        out[...] = whole[:, rel * TILE : (rel + 1) * TILE].astype(BF16)
+
+
+def joined(half, j, first, first_log, second_ref):
+    start = half * HD
+    block = second_ref[start : start + FLAG_ROWS, :].astype(F32)
+    row = 3 * j
+    second_log = block[row : row + 1, :] + block[row + 1 : row + 2, :] + block[row + 2 : row + 3, :]
+    second = second_ref[j * HD : (j + 1) * HD, :].astype(F32)
+    peak = jnp.maximum(first_log, second_log)
+    first_weight = jnp.exp2(first_log - peak)
+    second_weight = jnp.exp2(second_log - peak)
+    scale = 1.0 / (first_weight + second_weight)
+    both = first * (first_weight * scale) + second * (second_weight * scale)
+    return both.astype(BF16).T
+
+
+def far_kernel(half, in3_ref, in1_ref, out_ref):
+    block = in1_ref[half * HD : half * HD + FLAG_ROWS, :].astype(F32)
+    for j in range(half):
+        row = 3 * j
+        log = block[row : row + 1, :] + block[row + 1 : row + 2, :] + block[row + 2 : row + 3, :]
+        rows = slice(j * HD, (j + 1) * HD)
+        out_ref[:, rows] = joined(half, j, in1_ref[rows, :].astype(F32), log, in3_ref)
 
 
 def merge_kernel(
-    half, own_ref, own_log_ref, in2_ref, in1_ref, in3_ref,
-    whole_ref, out_hbm, out_ref, sems,
+    half, own_ref, own_log_ref, far_ref, in2_ref,
+    whole0_ref, whole2_ref, whole3_ref, whole1_ref, out_hbm, split_ref, whole_ref, sems,
 ):
     me = lax.axis_index("seq")
     side = lax.rem(me, 2)
-    start = half * HD
-
-    def logs_of(ref, j):
-        block = ref[start : start + FLAG_ROWS, :].astype(F32)
-        row = 3 * j
-        return block[row : row + 1, :] + block[row + 1 : row + 2, :] + block[row + 2 : row + 3, :]
-
-    def joined(first, first_log, second, second_log):
-        peak = jnp.maximum(first_log, second_log)
-        first_weight = jnp.exp2(first_log - peak)
-        second_weight = jnp.exp2(second_log - peak)
-        scale = 1.0 / (first_weight + second_weight)
-        return first * (first_weight * scale) + second * (second_weight * scale)
-
     copies = []
 
-    def leave(head, count):
-        cols = pl.ds(pl.multiple_of(head * HD, HD), count * HD)
-        copy = pltpu.make_async_copy(
-            out_ref.at[0, :, cols], out_hbm.at[0, :, cols], sems.at[len(copies)]
-        )
+    def leave(block_ref, head):
+        cols = pl.ds(pl.multiple_of(head * HD, HD), block_ref.shape[1])
+        copy = pltpu.make_async_copy(block_ref, out_hbm.at[0, :, cols], sems.at[len(copies)])
         copy.start()
         copies.append(copy)
 
-    done = start + FLAG_ROWS
-    blocks = [whole_ref[...]] + [ref[done : done + HD, :] for ref in (in1_ref, in2_ref, in3_ref)]
-    for rel, block in enumerate(blocks):
-        cols = head_cols(2 * half + jnp.bitwise_xor(me, rel))
-        out_ref[0, :, cols] = block.T
-    leave(2 * half, 4)
+    leave(far_ref, (1 - side) * half)
+    for rel, ref in enumerate((whole0_ref, whole1_ref, whole2_ref, whole3_ref)):
+        whole_ref[:, head_cols(jnp.bitwise_xor(me, rel))] = ref[...].T
+    leave(whole_ref, 2 * half)
     for j in range(half):
         rows = slice(j * HD, (j + 1) * HD)
-        far = joined(
-            in1_ref[rows, :].astype(F32), logs_of(in1_ref, j),
-            in3_ref[rows, :].astype(F32), logs_of(in3_ref, j),
-        )
-        out_ref[0, :, head_cols((1 - side) * half + j)] = far.astype(BF16).T
-    leave((1 - side) * half, half)
-    for j in range(half):
-        rows = slice(j * HD, (j + 1) * HD)
-        close = joined(
-            own_ref[rows, :], own_log_ref[j : j + 1, :],
-            in2_ref[rows, :].astype(F32), logs_of(in2_ref, j),
-        )
-        out_ref[0, :, head_cols(side * half + j)] = close.astype(BF16).T
-    leave(side * half, half)
+        split_ref[:, rows] = joined(
+            half, j, own_ref[rows, :], own_log_ref[j : j + 1, :], in2_ref
+        )
+    leave(split_ref, side * half)
     for copy in copies:
         copy.wait()
 
@@ -414,30 +409,42 @@
     )(*arrays, near(far2))
     near0, near1 = near(near0), near(send(near1, 1))
     far3, far2 = near(send(far3, 3)), near(send(far2, 2))
-    own, own_log, early1, early3 = pl.pallas_call(
+    own, own_log, back1, back3 = pl.pallas_call(
         functools.partial(early_kernel, half, frames, frame_tok),
         out_shape=(
             pltpu.VMEM((half * HD, TILE), F32),
             pltpu.VMEM((half, TILE), F32),
-        ) + (pltpu.VMEM((back_rows, TILE), BF16),) * 2,
+        ) + (pltpu.VMEM((back_rows + 8, TILE), BF16),) * 2,
         in_specs=[VMEM] * 3,
         out_specs=(VMEM,) * 4,
     )(near0, near1, far3)
-    whole, back1, back2, back3 = pl.pallas_call(
+    back3, back1 = near(send(back3, 3)), near(send(back1, 1))
+    back2, *whole = pl.pallas_call(
         functools.partial(late_kernel, half, frames, frame_tok),
-        out_shape=(pltpu.VMEM((HD, TILE), BF16),)
-        + (pltpu.VMEM((back_rows + HD, TILE), BF16),) * 3,
-        in_specs=[VMEM] * 6,
-        out_specs=(VMEM,) * 4,
-    )(near0, near1, far3, far2, near(early1), near(early3))
-    back2, back1, back3 = near(send(back2, 2)), near(send(back1, 1)), near(send(back3, 3))
+        out_shape=(pltpu.VMEM((back_rows, TILE), BF16),)
+        + (pltpu.VMEM((HD, TILE), BF16),) * 4,
+        in_specs=[VMEM] * 5,
+        out_specs=(VMEM,) * 5,
+    )(near0, near1, far3, far2, near(own_log))
+    back2 = near(send(back2, 2))
+    whole = [near(whole[0])] + [near(send(whole[rel], rel)) for rel in (2, 3, 1)]
+    far = pl.pallas_call(
+        functools.partial(far_kernel, half),
+        out_shape=pltpu.VMEM((TILE, half * HD), BF16),
+        in_specs=[VMEM] * 2,
+        out_specs=VMEM,
+    )(back3, back1)
     return pl.pallas_call(
         functools.partial(merge_kernel, half),
         out_shape=jax.ShapeDtypeStruct(queries.shape, BF16),
-        in_specs=[VMEM] * 6,
+        in_specs=[VMEM] * 8,
         out_specs=pl.BlockSpec(memory_space=pl.ANY),
-        scratch_shapes=[pltpu.VMEM(queries.shape, BF16), pltpu.SemaphoreType.DMA((3,))],
-    )(near(own), near(own_log), back2, back1, back3, near(whole))
+        scratch_shapes=[
+            pltpu.VMEM((TILE, half * HD), BF16),
+            pltpu.VMEM((TILE, 4 * HD), BF16),
+            pltpu.SemaphoreType.DMA((3,)),
+        ],
+    )(near(own), near(own_log), near(far), back2, *whole)
 
 
 def body(queries, keys, values, cache_keys, cache_values, frame_list, frame_place, tile_mask):

time: 42.5 us -> 42.2 us (level)
  waiting for transfers between devices: 25.3 us -> 21.3 us
  starting transfers between devices: 10.3 us -> 13.8 us
    ppermute x6 -> x9, waiting for transfers between devices: 25.3 us -> 21.3 us  [send(): return lax.ppermute(array, 'seq', [(i, i ^ rel) for i in range(4)])]
    ppermute x6 -> x9, starting transfers between devices: 10.3 us -> 13.8 us  [send(): return lax.ppermute(array, 'seq', [(i, i ^ rel) for i in range(4)])]
  transfers between devices with their start and end apart: 6 -> 9, of which waited for: 4 -> 4; matrix products, arithmetic and copies ran while one was open for 0% -> 0% of each run, Pallas kernels for 8% -> 11%
where the time goes in v7:
time: 42.2 us; the launch traced here: 41.8 us
  waiting for transfers between devices  21.3 us (50%)
  starting transfers between devices  13.8 us (33%)
  Pallas kernels  6.6 us (16%)
    ppermute x9, waiting for transfers between devices, send(): return lax.ppermute(array, 'seq', [(i, i ^ rel) for i in range(4)])  21.3 us
    ppermute x9, starting transfers between devices, send(): return lax.ppermute(array, 'seq', [(i, i ^ rel) for i in range(4)])  13.8 us
    pallas_call x1, Pallas kernels, exchanged(): pl.pallas_call(functools.partial(pack_kernel, half, (0,)), out_shape=pltp...  1.32 us
    pallas_call x1, Pallas kernels, exchanged(): pl.pallas_call(functools.partial(pack_kernel, half, (1,)), out_shape=pltp...  1.32 us
    pallas_call x1, Pallas kernels, exchanged(): pl.pallas_call(functools.partial(pack_kernel, half, (3, 2)), out_shape=(p...  1.19 us
    pallas_call x1, Pallas kernels, exchanged(): pl.pallas_call(functools.partial(late_kernel, half, frames, frame_tok), o...  0.98 us
    pallas_call x1, Pallas kernels, exchanged(): pl.pallas_call(functools.partial(early_kernel, half, frames, frame_tok),...  0.86 us
  transfers between devices with their start and end apart: 9, of which 4 were waited for; matrix products, arithmetic and copies ran while one was open for 0% of the time, Pallas kernels for 11%

profile of v7, /device:TPU:0, one launch (start us, length us, event | category | flops | bytes accessed | tf_op | source)
XLA Modules:
  0.0 41.8 jit_solution(9472672266828035431)
XLA Ops:
  0.0 1.3 %shard_map.82.refs_8_ = bf16[2064,128]{1,0:T(8,128)(2,1)S(1)} custom-call(s32[1,1,4]{2,1,0:T(1,128)} %refs_0_.5, s32[1,3]{1,0:T(1,128)} %refs_1_.5, s32[1,8]{1,0:T(1,128)} %refs_2_.5, bf16[1,128,1280]{2,1,0:T(8,128)(2,1)} %refs_3_.5, bf16[1,128,1280]{2,1,0:T(8,128)(2,1)} %refs_4_.5, bf16[1,128,1280]{2,1,0:T(8,128)(2,1)} %refs_5_.5, ...), custom_call_target="tpu_custom_call" | custom-call | tf_op jit(solution)/shard_map/pallas_call | solution.py:389
  1.3 3.1 %collective-permute-start = (bf16[2064,128]{1,0:T(8,128)(2,1)S(1)}, bf16[2064,128]{1,0:T(8,128)(2,1)S(1)}, u32[]{:S(2)}, u32[]{:S(2)}) collective-permute-start(bf16[2064,128]{1,0:T(8,128)(2,1)S(1)} %shard_map.82.refs_8_), channel_id=1, source_target_pairs={{0,4},{4,0},{8,12},{12,8},{1,5},{5,1},{9,13},{13,9},{2,6},{6,2},{1... | collective-permute-start | bytes 1585160 | tf_op jit(solution)/shard_map/ppermute | solution.py:371
  4.4 1.2 %shard_map.83 = (bf16[912,128]{1,0:T(8,128)(2,1)S(1)}, bf16[912,128]{1,0:T(8,128)(2,1)S(1)}) custom-call(s32[1,1,4]{2,1,0:T(1,128)} %refs_0_.5, s32[1,3]{1,0:T(1,128)} %refs_1_.5, s32[1,8]{1,0:T(1,128)} %refs_2_.5, bf16[1,128,1280]{2,1,0:T(8,128)(2,1)} %refs_3_.5, bf16[1,128,1280]{2,1,0:T(8,128)(2,1)} %refs_4_.5, bf16[1,128,1280]{2,1,0:T(8,128)(2,1)} %refs_5_.5, ...), custom_call_target="tpu_custom_call" | custom-call | tf_op jit(solution)/shard_map/pallas_call | solution.py:396
  5.6 2.5 %collective-permute-start.1 = (bf16[912,128]{1,0:T(8,128)(2,1)S(1)}, bf16[912,128]{1,0:T(8,128)(2,1)S(1)}, u32[]{:S(2)}, u32[]{:S(2)}) collective-permute-start(bf16[912,128]{1,0:T(8,128)(2,1)S(1)} %get-tuple-element.17), channel_id=1, source_target_pairs={{0,12},{4,8},{8,4},{12,0},{1,13},{5,9},{9,5},{13,1},{2,14},{6,10},... | collective-permute-start | bytes 700424 | tf_op jit(solution)/shard_map/ppermute | solution.py:371
  8.2 0.2 collective-permute-start.4
  8.3 1.3 %shard_map.84.near0_ref = bf16[2064,128]{1,0:T(8,128)(2,1)S(1)} custom-call(s32[1,1,4]{2,1,0:T(1,128)} %refs_0_.5, s32[1,3]{1,0:T(1,128)} %refs_1_.5, s32[1,8]{1,0:T(1,128)} %refs_2_.5, bf16[1,128,1280]{2,1,0:T(8,128)(2,1)} %refs_3_.5, bf16[1,128,1280]{2,1,0:T(8,128)(2,1)} %refs_4_.5, bf16[1,128,1280]{2,1,0:T(8,128)(2,1)} %refs_5_.5, ...), custom_call_target="tpu_custom_call" | custom-call | tf_op jit(solution)/shard_map/pallas_call | solution.py:403
  9.7 15.2 %collective-permute-done.1.far3_ref = bf16[912,128]{1,0:T(8,128)(2,1)S(1)} collective-permute-done((bf16[912,128]{1,0:T(8,128)(2,1)S(1)}, bf16[912,128]{1,0:T(8,128)(2,1)S(1)}, u32[]{:S(2)}, u32[]{:S(2)}) %collective-permute-start.1) | collective-permute-done | bytes 233504 | tf_op jit(solution)/shard_map/ppermute | solution.py:371
  24.9 1.6 %collective-permute-done.near1_ref = bf16[2064,128]{1,0:T(8,128)(2,1)S(1)} collective-permute-done((bf16[2064,128]{1,0:T(8,128)(2,1)S(1)}, bf16[2064,128]{1,0:T(8,128)(2,1)S(1)}, u32[]{:S(2)}, u32[]{:S(2)}) %collective-permute-start) | collective-permute-done | bytes 528416 | tf_op jit(solution)/shard_map/ppermute | solution.py:371
  26.4 0.9 %shard_map.85 = (f32[384,128]{1,0:T(8,128)S(1)}, f32[3,128]{1,0:T(4,128)S(1)}, bf16[408,128]{1,0:T(8,128)(2,1)S(1)}, bf16[408,128]{1,0:T(8,128)(2,1)S(1)}) custom-call(bf16[2064,128]{1,0:T(8,128)(2,1)S(1)} %shard_map.84.near0_ref, bf16[2064,128]{1,0:T(8,128)(2,1)S(1)} %collective-permute-done.near1_ref, bf16[912,128]{1,0:T(8,128)(2,1)S(1)} %collective-permute-done.1.far3_ref), custom_call_target="tpu_custom_call" | custom-call | tf_op jit(solution)/shard_map/pallas_call | solution.py:412
  27.3 2.5 %collective-permute-start.2 = (bf16[408,128]{1,0:T(8,128)(2,1)S(1)}, bf16[408,128]{1,0:T(8,128)(2,1)S(1)}, u32[]{:S(2)}, u32[]{:S(2)}) collective-permute-start(bf16[408,128]{1,0:T(8,128)(2,1)S(1)} %get-tuple-element.20), channel_id=1, source_target_pairs={{0,12},{4,8},{8,4},{12,0},{1,13},{5,9},{9,5},{13,1},{2,14},{6,10},... | collective-permute-start | bytes 313352 | tf_op jit(solution)/shard_map/ppermute | solution.py:371
  29.8 0.0 collective-permute-start.3
  29.8 0.0 collective-permute-done.4.far2_ref
  29.8 1.0 %shard_map.87 = (bf16[400,128]{1,0:T(8,128)(2,1)S(1)}, bf16[128,128]{1,0:T(8,128)(2,1)S(1)}, bf16[128,128]{1,0:T(8,128)(2,1)S(1)}, bf16[128,128]{1,0:T(8,128)(2,1)S(1)}, bf16[128,128]{1,0:T(8,128)(2,1)S(1)}) custom-call(bf16[2064,128]{1,0:T(8,128)(2,1)S(1)} %shard_map.84.near0_ref, bf16[2064,128]{1,0:T(8,128)(2,1)S(1)} %collective-permute-done.near1_ref, ...), custom_call_target="tpu_custom_call" | custom-call | tf_op jit(solution)/shard_map/pallas_call | solution.py:422
  30.8 2.0 %collective-permute-start.5 = (bf16[400,128]{1,0:T(8,128)(2,1)S(1)}, bf16[400,128]{1,0:T(8,128)(2,1)S(1)}, u32[]{:S(2)}, u32[]{:S(2)}) collective-permute-start(bf16[400,128]{1,0:T(8,128)(2,1)S(1)} %get-tuple-element.22), channel_id=1, source_target_pairs={{0,8},{4,12},{8,0},{12,4},{1,9},{5,13},{9,1},{13,5},{2,10},{6,14},... | collective-permute-start | bytes 307208 | tf_op jit(solution)/shard_map/ppermute | solution.py:371
  32.8 1.0 %collective-permute-start.6 = (bf16[128,128]{1,0:T(8,128)(2,1)S(1)}, bf16[128,128]{1,0:T(8,128)(2,1)S(1)}, u32[]{:S(2)}, u32[]{:S(2)}) collective-permute-start(bf16[128,128]{1,0:T(8,128)(2,1)S(1)} %get-tuple-element.24), channel_id=1, source_target_pairs={{0,8},{4,12},{8,0},{12,4},{1,9},{5,13},{9,1},{13,5},{2,10},{6,14},... | collective-permute-start | bytes 98312 | tf_op jit(solution)/shard_map/ppermute | solution.py:371
  33.8 2.5 %collective-permute-start.7 = (bf16[128,128]{1,0:T(8,128)(2,1)S(1)}, bf16[128,128]{1,0:T(8,128)(2,1)S(1)}, u32[]{:S(2)}, u32[]{:S(2)}) collective-permute-start(bf16[128,128]{1,0:T(8,128)(2,1)S(1)} %get-tuple-element.25), channel_id=1, source_target_pairs={{0,12},{4,8},{8,4},{12,0},{1,13},{5,9},{9,5},{13,1},{2,14},{6,10},... | collective-permute-start | bytes 98312 | tf_op jit(solution)/shard_map/ppermute | solution.py:371
  36.3 0.0 collective-permute-done.2.in3_ref
  36.3 0.0 collective-permute-start.8
  36.3 1.2 %collective-permute-done.3.in1_ref = bf16[408,128]{1,0:T(8,128)(2,1)S(1)} collective-permute-done((bf16[408,128]{1,0:T(8,128)(2,1)S(1)}, bf16[408,128]{1,0:T(8,128)(2,1)S(1)}, u32[]{:S(2)}, u32[]{:S(2)}) %collective-permute-start.3) | collective-permute-done | bytes 104480 | tf_op jit(solution)/shard_map/ppermute | solution.py:371
  37.5 0.1 shard_map.86.far_ref
  37.6 3.3 %collective-permute-done.6.whole2_ref = bf16[128,128]{1,0:T(8,128)(2,1)S(1)} collective-permute-done((bf16[128,128]{1,0:T(8,128)(2,1)S(1)}, bf16[128,128]{1,0:T(8,128)(2,1)S(1)}, u32[]{:S(2)}, u32[]{:S(2)}) %collective-permute-start.6) | collective-permute-done | bytes 32800 | tf_op jit(solution)/shard_map/ppermute | solution.py:371
  41.0 0.0 collective-permute-done.7.whole3_ref
  41.0 0.0 collective-permute-done.8.whole1_ref
  41.0 0.0 collective-permute-done.5.in2_ref
  41.0 0.8 %shard_map.88 = bf16[1,128,1280]{2,1,0:T(8,128)(2,1)} custom-call(f32[384,128]{1,0:T(8,128)S(1)} %get-tuple-element.18.own_ref, f32[3,128]{1,0:T(4,128)S(1)} %get-tuple-element.19.before_ref.own_log_ref, bf16[128,384]{1,0:T(8,128)(2,1)S(1)} %shard_map.86.far_ref, bf16[400,128]{1,0:T(8,128)(2,1)S(1)} %collective-permute-done.5.in2_ref, ...), custom_call_target="tpu_custom_call" | custom-call | tf_op jit(solution)/shard_map/pallas_call | solution.py:437
Async XLA Ops:
  1.3 25.1 %collective-permute-start = (bf16[2064,128]{1,0:T(8,128)(2,1)S(1)}, bf16[2064,128]{1,0:T(8,128)(2,1)S(1)}, u32[]{:S(2)}, u32[]{:S(2)}) collective-permute-start(bf16[2064,128]{1,0:T(8,128)(2,1)S(1)} %shard_map.82.refs_8_), channel_id=1, source_target_pairs={{0,4},{4,0},{8,12},{12,8},{1,5},{5,1},{9,13},{13,9},{2,6},{6,2},{1... | collective-permute-start | bytes 1585160 | tf_op jit(solution)/shard_map/ppermute | solution.py:371
  5.6 19.3 %collective-permute-start.1 = (bf16[912,128]{1,0:T(8,128)(2,1)S(1)}, bf16[912,128]{1,0:T(8,128)(2,1)S(1)}, u32[]{:S(2)}, u32[]{:S(2)}) collective-permute-start(bf16[912,128]{1,0:T(8,128)(2,1)S(1)} %get-tuple-element.17), channel_id=1, source_target_pairs={{0,12},{4,8},{8,4},{12,0},{1,13},{5,9},{9,5},{13,1},{2,14},{6,10},... | collective-permute-start | bytes 700424 | tf_op jit(solution)/shard_map/ppermute | solution.py:371
  8.2 21.7 %collective-permute-start.4 = (bf16[912,128]{1,0:T(8,128)(2,1)S(1)}, bf16[912,128]{1,0:T(8,128)(2,1)S(1)}, u32[]{:S(2)}, u32[]{:S(2)}) collective-permute-start(bf16[912,128]{1,0:T(8,128)(2,1)S(1)} %get-tuple-element.16.refs_8_), channel_id=1, source_target_pairs={{0,8},{4,12},{8,0},{12,4},{1,9},{5,13},{9,1},{13,5},{2,10},{6,14},... | collective-permute-start | bytes 700424 | tf_op jit(solution)/shard_map/ppermute | solution.py:371
  27.3 9.0 %collective-permute-start.2 = (bf16[408,128]{1,0:T(8,128)(2,1)S(1)}, bf16[408,128]{1,0:T(8,128)(2,1)S(1)}, u32[]{:S(2)}, u32[]{:S(2)}) collective-permute-start(bf16[408,128]{1,0:T(8,128)(2,1)S(1)} %get-tuple-element.20), channel_id=1, source_target_pairs={{0,12},{4,8},{8,4},{12,0},{1,13},{5,9},{9,5},{13,1},{2,14},{6,10},... | collective-permute-start | bytes 313352 | tf_op jit(solution)/shard_map/ppermute | solution.py:371
  29.8 7.7 %collective-permute-start.3 = (bf16[408,128]{1,0:T(8,128)(2,1)S(1)}, bf16[408,128]{1,0:T(8,128)(2,1)S(1)}, u32[]{:S(2)}, u32[]{:S(2)}) collective-permute-start(bf16[408,128]{1,0:T(8,128)(2,1)S(1)} %get-tuple-element.21), channel_id=1, source_target_pairs={{0,4},{4,0},{8,12},{12,8},{1,5},{5,1},{9,13},{13,9},{2,6},{6,2},{1... | collective-permute-start | bytes 313352 | tf_op jit(solution)/shard_map/ppermute | solution.py:371
  30.8 10.2 %collective-permute-start.5 = (bf16[400,128]{1,0:T(8,128)(2,1)S(1)}, bf16[400,128]{1,0:T(8,128)(2,1)S(1)}, u32[]{:S(2)}, u32[]{:S(2)}) collective-permute-start(bf16[400,128]{1,0:T(8,128)(2,1)S(1)} %get-tuple-element.22), channel_id=1, source_target_pairs={{0,8},{4,12},{8,0},{12,4},{1,9},{5,13},{9,1},{13,5},{2,10},{6,14},... | collective-permute-start | bytes 307208 | tf_op jit(solution)/shard_map/ppermute | solution.py:371
  32.8 8.2 %collective-permute-start.6 = (bf16[128,128]{1,0:T(8,128)(2,1)S(1)}, bf16[128,128]{1,0:T(8,128)(2,1)S(1)}, u32[]{:S(2)}, u32[]{:S(2)}) collective-permute-start(bf16[128,128]{1,0:T(8,128)(2,1)S(1)} %get-tuple-element.24), channel_id=1, source_target_pairs={{0,8},{4,12},{8,0},{12,4},{1,9},{5,13},{9,1},{13,5},{2,10},{6,14},... | collective-permute-start | bytes 98312 | tf_op jit(solution)/shard_map/ppermute | solution.py:371
  33.8 7.2 %collective-permute-start.7 = (bf16[128,128]{1,0:T(8,128)(2,1)S(1)}, bf16[128,128]{1,0:T(8,128)(2,1)S(1)}, u32[]{:S(2)}, u32[]{:S(2)}) collective-permute-start(bf16[128,128]{1,0:T(8,128)(2,1)S(1)} %get-tuple-element.25), channel_id=1, source_target_pairs={{0,12},{4,8},{8,4},{12,0},{1,13},{5,9},{9,5},{13,1},{2,14},{6,10},... | collective-permute-start | bytes 98312 | tf_op jit(solution)/shard_map/ppermute | solution.py:371
  36.3 4.7 %collective-permute-start.8 = (bf16[128,128]{1,0:T(8,128)(2,1)S(1)}, bf16[128,128]{1,0:T(8,128)(2,1)S(1)}, u32[]{:S(2)}, u32[]{:S(2)}) collective-permute-start(bf16[128,128]{1,0:T(8,128)(2,1)S(1)} %get-tuple-element.26), channel_id=1, source_target_pairs={{0,4},{4,0},{8,12},{12,8},{1,5},{5,1},{9,13},{13,9},{2,6},{6,2},{1... | collective-permute-start | bytes 98312 | tf_op jit(solution)/shard_map/ppermute | solution.py:371

commit v8 on v7

--- a/solution.py
+++ b/solution.py
@@ -283,14 +283,15 @@
         row = half * HD
         out[row : row + FLAG_ROWS, :] = stat_block(stats[i])
         row += FLAG_ROWS
-        out[row:, :] = jnp.zeros((out.shape[0] - row, TILE), BF16)
+        if row < out.shape[0]:
+            out[row:, :] = jnp.zeros((out.shape[0] - row, TILE), BF16)
 
 
 def late_kernel(
-    half, frames, frame_tok, near0_ref, near1_ref, far3_ref, far2_ref, before_ref,
-    out2_ref, *whole_refs,
+    half, frames, frame_tok, near0_ref, near1_ref, far3_ref, far2_ref, early1_ref,
+    out2_ref, out1_ref, *whole_refs,
 ):
-    del before_ref
+    out1_ref[...] = early1_ref[...]
     cache = frames * frame_tok
     span = 3 * TILE + 2 * cache
     ins = (near0_ref, near1_ref, far2_ref, far3_ref)
@@ -330,29 +331,30 @@
     return both.astype(BF16).T
 
 
-def far_kernel(half, in3_ref, in1_ref, out_ref):
+def keep_kernel(in3_ref, out_ref):
+    out_ref[...] = in3_ref[: out_ref.shape[0], :]
+
+
+def merge_kernel(
+    half, own_ref, own_log_ref, in3_ref, in2_ref, in1_ref,
+    whole0_ref, whole2_ref, whole3_ref, whole1_ref, out_hbm, far_ref, split_ref, whole_ref, sems,
+):
+    me = lax.axis_index("seq")
+    side = lax.rem(me, 2)
+    copies = []
+
+    def leave(block_ref, head):
+        cols = pl.ds(pl.multiple_of(head * HD, HD), block_ref.shape[1])
+        copy = pltpu.make_async_copy(block_ref, out_hbm.at[0, :, cols], sems.at[len(copies)])
+        copy.start()
+        copies.append(copy)
+
     block = in1_ref[half * HD : half * HD + FLAG_ROWS, :].astype(F32)
     for j in range(half):
         row = 3 * j
         log = block[row : row + 1, :] + block[row + 1 : row + 2, :] + block[row + 2 : row + 3, :]
         rows = slice(j * HD, (j + 1) * HD)
-        out_ref[:, rows] = joined(half, j, in1_ref[rows, :].astype(F32), log, in3_ref)
-
-
-def merge_kernel(
-    half, own_ref, own_log_ref, far_ref, in2_ref,
-    whole0_ref, whole2_ref, whole3_ref, whole1_ref, out_hbm, split_ref, whole_ref, sems,
-):
-    me = lax.axis_index("seq")
-    side = lax.rem(me, 2)
-    copies = []
-
-    def leave(block_ref, head):
-        cols = pl.ds(pl.multiple_of(head * HD, HD), block_ref.shape[1])
-        copy = pltpu.make_async_copy(block_ref, out_hbm.at[0, :, cols], sems.at[len(copies)])
-        copy.start()
-        copies.append(copy)
-
+        far_ref[:, rows] = joined(half, j, in1_ref[rows, :].astype(F32), log, in3_ref)
     leave(far_ref, (1 - side) * half)
     for rel, ref in enumerate((whole0_ref, whole1_ref, whole2_ref, whole3_ref)):
         whole_ref[:, head_cols(jnp.bitwise_xor(me, rel))] = ref[...].T
@@ -414,37 +416,38 @@
         out_shape=(
             pltpu.VMEM((half * HD, TILE), F32),
             pltpu.VMEM((half, TILE), F32),
-        ) + (pltpu.VMEM((back_rows + 8, TILE), BF16),) * 2,
+        ) + (pltpu.VMEM((back_rows, TILE), BF16), pltpu.VMEM((back_rows + 8, TILE), BF16)),
         in_specs=[VMEM] * 3,
         out_specs=(VMEM,) * 4,
     )(near0, near1, far3)
-    back3, back1 = near(send(back3, 3)), near(send(back1, 1))
-    back2, *whole = pl.pallas_call(
+    back3 = near(send(back3, 3))
+    back2, back1, *whole = pl.pallas_call(
         functools.partial(late_kernel, half, frames, frame_tok),
-        out_shape=(pltpu.VMEM((back_rows, TILE), BF16),)
+        out_shape=(pltpu.VMEM((back_rows, TILE), BF16),) * 2
         + (pltpu.VMEM((HD, TILE), BF16),) * 4,
         in_specs=[VMEM] * 5,
-        out_specs=(VMEM,) * 5,
-    )(near0, near1, far3, far2, near(own_log))
-    back2 = near(send(back2, 2))
+        out_specs=(VMEM,) * 6,
+    )(near0, near1, far3, far2, near(back1))
+    back2, back1 = near(send(back2, 2)), near(send(back1, 1))
     whole = [near(whole[0])] + [near(send(whole[rel], rel)) for rel in (2, 3, 1)]
-    far = pl.pallas_call(
-        functools.partial(far_kernel, half),
-        out_shape=pltpu.VMEM((TILE, half * HD), BF16),
-        in_specs=[VMEM] * 2,
+    kept3 = pl.pallas_call(
+        keep_kernel,
+        out_shape=pltpu.VMEM((back_rows, TILE), BF16),
+        in_specs=[VMEM],
         out_specs=VMEM,
-    )(back3, back1)
+    )(back3)
     return pl.pallas_call(
         functools.partial(merge_kernel, half),
         out_shape=jax.ShapeDtypeStruct(queries.shape, BF16),
-        in_specs=[VMEM] * 8,
+        in_specs=[VMEM] * 9,
         out_specs=pl.BlockSpec(memory_space=pl.ANY),
         scratch_shapes=[
+            pltpu.VMEM((TILE, half * HD), BF16),
             pltpu.VMEM((TILE, half * HD), BF16),
             pltpu.VMEM((TILE, 4 * HD), BF16),
             pltpu.SemaphoreType.DMA((3,)),
         ],
-    )(near(own), near(own_log), near(far), back2, *whole)
+    )(near(own), near(own_log), near(kept3), back2, back1, *whole)
 
 
 def body(queries, keys, values, cache_keys, cache_values, frame_list, frame_place, tile_mask):

time: 42.2 us -> 41.8 us (level)
  waiting for transfers between devices: 21.3 us -> 19.9 us
  starting transfers between devices: 13.8 us -> 15 us
    ppermute x9, waiting for transfers between devices: 21.3 us -> 19.9 us  [send(): return lax.ppermute(array, 'seq', [(i, i ^ rel) for i in range(4)])]
    ppermute x9, starting transfers between devices: 13.8 us -> 15 us  [send(): return lax.ppermute(array, 'seq', [(i, i ^ rel) for i in range(4)])]
where the time goes in v8:
time: 41.8 us; the launch traced here: 41.4 us
  waiting for transfers between devices  19.9 us (48%)
  starting transfers between devices  15 us (36%)
  Pallas kernels  6.55 us (16%)
    ppermute x9, waiting for transfers between devices, send(): return lax.ppermute(array, 'seq', [(i, i ^ rel) for i in range(4)])  19.9 us
    ppermute x9, starting transfers between devices, send(): return lax.ppermute(array, 'seq', [(i, i ^ rel) for i in range(4)])  15 us
    pallas_call x1, Pallas kernels, exchanged(): pl.pallas_call(functools.partial(pack_kernel, half, (0,)), out_shape=pltp...  1.32 us
    pallas_call x1, Pallas kernels, exchanged(): pl.pallas_call(functools.partial(pack_kernel, half, (1,)), out_shape=pltp...  1.32 us
    pallas_call x1, Pallas kernels, exchanged(): pl.pallas_call(functools.partial(pack_kernel, half, (3, 2)), out_shape=(p...  1.19 us
    pallas_call x1, Pallas kernels, exchanged(): pl.pallas_call(functools.partial(late_kernel, half, frames, frame_tok), o...  0.98 us
    pallas_call x1, Pallas kernels, exchanged(): pl.pallas_call(functools.partial(merge_kernel, half), out_shape=jax.Shape...  0.88 us
    pallas_call x1, Pallas kernels, exchanged(): pl.pallas_call(functools.partial(early_kernel, half, frames, frame_tok),...  0.86 us
  transfers between devices with their start and end apart: 9, of which 4 were waited for; matrix products, arithmetic and copies ran while one was open for 0% of the time, Pallas kernels for 11%

profile of v8, /device:TPU:0, one launch (start us, length us, event | category | flops | bytes accessed | tf_op | source)
XLA Modules:
  0.0 41.4 jit_solution(11686987010266250919)
XLA Ops:
  0.0 1.3 %shard_map.82.refs_8_ = bf16[2064,128]{1,0:T(8,128)(2,1)S(1)} custom-call(s32[1,1,4]{2,1,0:T(1,128)} %refs_0_.5, s32[1,3]{1,0:T(1,128)} %refs_1_.5, s32[1,8]{1,0:T(1,128)} %refs_2_.5, bf16[1,128,1280]{2,1,0:T(8,128)(2,1)} %refs_3_.5, bf16[1,128,1280]{2,1,0:T(8,128)(2,1)} %refs_4_.5, bf16[1,128,1280]{2,1,0:T(8,128)(2,1)} %refs_5_.5, ...), custom_call_target="tpu_custom_call" | custom-call | tf_op jit(solution)/shard_map/pallas_call | solution.py:391
  1.3 3.1 %collective-permute-start = (bf16[2064,128]{1,0:T(8,128)(2,1)S(1)}, bf16[2064,128]{1,0:T(8,128)(2,1)S(1)}, u32[]{:S(2)}, u32[]{:S(2)}) collective-permute-start(bf16[2064,128]{1,0:T(8,128)(2,1)S(1)} %shard_map.82.refs_8_), channel_id=1, source_target_pairs={{0,4},{4,0},{8,12},{12,8},{1,5},{5,1},{9,13},{13,9},{2,6},{6,2},{1... | collective-permute-start | bytes 1585160 | tf_op jit(solution)/shard_map/ppermute | solution.py:373
  4.4 1.2 %shard_map.83 = (bf16[912,128]{1,0:T(8,128)(2,1)S(1)}, bf16[912,128]{1,0:T(8,128)(2,1)S(1)}) custom-call(s32[1,1,4]{2,1,0:T(1,128)} %refs_0_.5, s32[1,3]{1,0:T(1,128)} %refs_1_.5, s32[1,8]{1,0:T(1,128)} %refs_2_.5, bf16[1,128,1280]{2,1,0:T(8,128)(2,1)} %refs_3_.5, bf16[1,128,1280]{2,1,0:T(8,128)(2,1)} %refs_4_.5, bf16[1,128,1280]{2,1,0:T(8,128)(2,1)} %refs_5_.5, ...), custom_call_target="tpu_custom_call" | custom-call | tf_op jit(solution)/shard_map/pallas_call | solution.py:398
  5.6 2.5 %collective-permute-start.1 = (bf16[912,128]{1,0:T(8,128)(2,1)S(1)}, bf16[912,128]{1,0:T(8,128)(2,1)S(1)}, u32[]{:S(2)}, u32[]{:S(2)}) collective-permute-start(bf16[912,128]{1,0:T(8,128)(2,1)S(1)} %get-tuple-element.18), channel_id=1, source_target_pairs={{0,12},{4,8},{8,4},{12,0},{1,13},{5,9},{9,5},{13,1},{2,14},{6,10},... | collective-permute-start | bytes 700424 | tf_op jit(solution)/shard_map/ppermute | solution.py:373
  8.2 0.2 collective-permute-start.3
  8.3 1.3 %shard_map.84.near0_ref = bf16[2064,128]{1,0:T(8,128)(2,1)S(1)} custom-call(s32[1,1,4]{2,1,0:T(1,128)} %refs_0_.5, s32[1,3]{1,0:T(1,128)} %refs_1_.5, s32[1,8]{1,0:T(1,128)} %refs_2_.5, bf16[1,128,1280]{2,1,0:T(8,128)(2,1)} %refs_3_.5, bf16[1,128,1280]{2,1,0:T(8,128)(2,1)} %refs_4_.5, bf16[1,128,1280]{2,1,0:T(8,128)(2,1)} %refs_5_.5, ...), custom_call_target="tpu_custom_call" | custom-call | tf_op jit(solution)/shard_map/pallas_call | solution.py:405
  9.7 15.2 %collective-permute-done.1.far3_ref = bf16[912,128]{1,0:T(8,128)(2,1)S(1)} collective-permute-done((bf16[912,128]{1,0:T(8,128)(2,1)S(1)}, bf16[912,128]{1,0:T(8,128)(2,1)S(1)}, u32[]{:S(2)}, u32[]{:S(2)}) %collective-permute-start.1) | collective-permute-done | bytes 233504 | tf_op jit(solution)/shard_map/ppermute | solution.py:373
  24.9 1.6 %collective-permute-done.near1_ref = bf16[2064,128]{1,0:T(8,128)(2,1)S(1)} collective-permute-done((bf16[2064,128]{1,0:T(8,128)(2,1)S(1)}, bf16[2064,128]{1,0:T(8,128)(2,1)S(1)}, u32[]{:S(2)}, u32[]{:S(2)}) %collective-permute-start) | collective-permute-done | bytes 528416 | tf_op jit(solution)/shard_map/ppermute | solution.py:373
  26.4 0.9 %shard_map.85 = (f32[384,128]{1,0:T(8,128)S(1)}, f32[3,128]{1,0:T(4,128)S(1)}, bf16[400,128]{1,0:T(8,128)(2,1)S(1)}, bf16[408,128]{1,0:T(8,128)(2,1)S(1)}) custom-call(bf16[2064,128]{1,0:T(8,128)(2,1)S(1)} %shard_map.84.near0_ref, bf16[2064,128]{1,0:T(8,128)(2,1)S(1)} %collective-permute-done.near1_ref, bf16[912,128]{1,0:T(8,128)(2,1)S(1)} %collective-permute-done.1.far3_ref), custom_call_target="tpu_custom_call" | custom-call | tf_op jit(solution)/shard_map/pallas_call | solution.py:414
  27.3 2.5 %collective-permute-start.2 = (bf16[408,128]{1,0:T(8,128)(2,1)S(1)}, bf16[408,128]{1,0:T(8,128)(2,1)S(1)}, u32[]{:S(2)}, u32[]{:S(2)}) collective-permute-start(bf16[408,128]{1,0:T(8,128)(2,1)S(1)} %get-tuple-element.21), channel_id=1, source_target_pairs={{0,12},{4,8},{8,4},{12,0},{1,13},{5,9},{9,5},{13,1},{2,14},{6,10},... | collective-permute-start | bytes 313352 | tf_op jit(solution)/shard_map/ppermute | solution.py:373
  29.8 0.0 collective-permute-done.3.far2_ref
  29.8 1.0 %shard_map.87 = (bf16[400,128]{1,0:T(8,128)(2,1)S(1)}, bf16[400,128]{1,0:T(8,128)(2,1)S(1)}, bf16[128,128]{1,0:T(8,128)(2,1)S(1)}, bf16[128,128]{1,0:T(8,128)(2,...) custom-call(bf16[2064,128]{1,0:T(8,128)(2,1)S(1)} %shard_map.84.near0_ref, ...), custom_call_target="tpu_custom_call" | custom-call | tf_op jit(solution)/shard_map/pallas_call | solution.py:424
  30.8 0.1 collective-permute-start.4
  30.9 3.0 %collective-permute-start.5 = (bf16[400,128]{1,0:T(8,128)(2,1)S(1)}, bf16[400,128]{1,0:T(8,128)(2,1)S(1)}, u32[]{:S(2)}, u32[]{:S(2)}) collective-permute-start(bf16[400,128]{1,0:T(8,128)(2,1)S(1)} %get-tuple-element.24), channel_id=1, source_target_pairs={{0,4},{4,0},{8,12},{12,8},{1,5},{5,1},{9,13},{13,9},{2,6},{6,2},{1... | collective-permute-start | bytes 307208 | tf_op jit(solution)/shard_map/ppermute | solution.py:373
  33.9 0.1 collective-permute-start.6
  34.0 2.3 %collective-permute-start.7 = (bf16[128,128]{1,0:T(8,128)(2,1)S(1)}, bf16[128,128]{1,0:T(8,128)(2,1)S(1)}, u32[]{:S(2)}, u32[]{:S(2)}) collective-permute-start(bf16[128,128]{1,0:T(8,128)(2,1)S(1)} %get-tuple-element.27), channel_id=1, source_target_pairs={{0,12},{4,8},{8,4},{12,0},{1,13},{5,9},{9,5},{13,1},{2,14},{6,10},... | collective-permute-start | bytes 98312 | tf_op jit(solution)/shard_map/ppermute | solution.py:373
  36.3 0.0 collective-permute-done.2.in3_ref
  36.3 1.1 %collective-permute-start.8 = (bf16[128,128]{1,0:T(8,128)(2,1)S(1)}, bf16[128,128]{1,0:T(8,128)(2,1)S(1)}, u32[]{:S(2)}, u32[]{:S(2)}) collective-permute-start(bf16[128,128]{1,0:T(8,128)(2,1)S(1)} %get-tuple-element.28), channel_id=1, source_target_pairs={{0,4},{4,0},{8,12},{12,8},{1,5},{5,1},{9,13},{13,9},{2,6},{6,2},{1... | collective-permute-start | bytes 98312 | tf_op jit(solution)/shard_map/ppermute | solution.py:373
  37.4 2.8 %collective-permute-done.6.whole2_ref = bf16[128,128]{1,0:T(8,128)(2,1)S(1)} collective-permute-done((bf16[128,128]{1,0:T(8,128)(2,1)S(1)}, bf16[128,128]{1,0:T(8,128)(2,1)S(1)}, u32[]{:S(2)}, u32[]{:S(2)}) %collective-permute-start.6) | collective-permute-done | bytes 32800 | tf_op jit(solution)/shard_map/ppermute | solution.py:373
  40.2 0.0 collective-permute-done.7.whole3_ref
  40.2 0.3 collective-permute-done.8.whole1_ref
  40.5 0.0 collective-permute-done.4.in2_ref
  40.5 0.0 collective-permute-done.5.in1_ref
  40.5 0.9 %shard_map.88 = bf16[1,128,1280]{2,1,0:T(8,128)(2,1)} custom-call(f32[384,128]{1,0:T(8,128)S(1)} %get-tuple-element.19.own_ref, f32[3,128]{1,0:T(4,128)S(1)} %get-tuple-element.20.own_log_ref, bf16[400,128]{1,0:T(8,128)(2,1)S(1)} %shard_map.86.in3_ref, bf16[400,128]{1,0:T(8,128)(2,1)S(1)} %collective-permute-done.4.in2_ref, ...), custom_call_target="tpu_custom_call" | custom-call | tf_op jit(solution)/shard_map/pallas_call | solution.py:439
  (1 shorter events, 0.0 us)
Async XLA Ops:
  1.3 25.1 %collective-permute-start = (bf16[2064,128]{1,0:T(8,128)(2,1)S(1)}, bf16[2064,128]{1,0:T(8,128)(2,1)S(1)}, u32[]{:S(2)}, u32[]{:S(2)}) collective-permute-start(bf16[2064,128]{1,0:T(8,128)(2,1)S(1)} %shard_map.82.refs_8_), channel_id=1, source_target_pairs={{0,4},{4,0},{8,12},{12,8},{1,5},{5,1},{9,13},{13,9},{2,6},{6,2},{1... | collective-permute-start | bytes 1585160 | tf_op jit(solution)/shard_map/ppermute | solution.py:373
  5.6 19.3 %collective-permute-start.1 = (bf16[912,128]{1,0:T(8,128)(2,1)S(1)}, bf16[912,128]{1,0:T(8,128)(2,1)S(1)}, u32[]{:S(2)}, u32[]{:S(2)}) collective-permute-start(bf16[912,128]{1,0:T(8,128)(2,1)S(1)} %get-tuple-element.18), channel_id=1, source_target_pairs={{0,12},{4,8},{8,4},{12,0},{1,13},{5,9},{9,5},{13,1},{2,14},{6,10},... | collective-permute-start | bytes 700424 | tf_op jit(solution)/shard_map/ppermute | solution.py:373
  8.2 21.7 %collective-permute-start.3 = (bf16[912,128]{1,0:T(8,128)(2,1)S(1)}, bf16[912,128]{1,0:T(8,128)(2,1)S(1)}, u32[]{:S(2)}, u32[]{:S(2)}) collective-permute-start(bf16[912,128]{1,0:T(8,128)(2,1)S(1)} %get-tuple-element.17.refs_8_), channel_id=1, source_target_pairs={{0,8},{4,12},{8,0},{12,4},{1,9},{5,13},{9,1},{13,5},{2,10},{6,14},... | collective-permute-start | bytes 700424 | tf_op jit(solution)/shard_map/ppermute | solution.py:373
  27.3 9.0 %collective-permute-start.2 = (bf16[408,128]{1,0:T(8,128)(2,1)S(1)}, bf16[408,128]{1,0:T(8,128)(2,1)S(1)}, u32[]{:S(2)}, u32[]{:S(2)}) collective-permute-start(bf16[408,128]{1,0:T(8,128)(2,1)S(1)} %get-tuple-element.21), channel_id=1, source_target_pairs={{0,12},{4,8},{8,4},{12,0},{1,13},{5,9},{9,5},{13,1},{2,14},{6,10},... | collective-permute-start | bytes 313352 | tf_op jit(solution)/shard_map/ppermute | solution.py:373
  30.8 9.7 %collective-permute-start.4 = (bf16[400,128]{1,0:T(8,128)(2,1)S(1)}, bf16[400,128]{1,0:T(8,128)(2,1)S(1)}, u32[]{:S(2)}, u32[]{:S(2)}) collective-permute-start(bf16[400,128]{1,0:T(8,128)(2,1)S(1)} %get-tuple-element.23), channel_id=1, source_target_pairs={{0,8},{4,12},{8,0},{12,4},{1,9},{5,13},{9,1},{13,5},{2,10},{6,14},... | collective-permute-start | bytes 307208 | tf_op jit(solution)/shard_map/ppermute | solution.py:373
  30.9 9.6 %collective-permute-start.5 = (bf16[400,128]{1,0:T(8,128)(2,1)S(1)}, bf16[400,128]{1,0:T(8,128)(2,1)S(1)}, u32[]{:S(2)}, u32[]{:S(2)}) collective-permute-start(bf16[400,128]{1,0:T(8,128)(2,1)S(1)} %get-tuple-element.24), channel_id=1, source_target_pairs={{0,4},{4,0},{8,12},{12,8},{1,5},{5,1},{9,13},{13,9},{2,6},{6,2},{1... | collective-permute-start | bytes 307208 | tf_op jit(solution)/shard_map/ppermute | solution.py:373
  33.9 6.3 %collective-permute-start.6 = (bf16[128,128]{1,0:T(8,128)(2,1)S(1)}, bf16[128,128]{1,0:T(8,128)(2,1)S(1)}, u32[]{:S(2)}, u32[]{:S(2)}) collective-permute-start(bf16[128,128]{1,0:T(8,128)(2,1)S(1)} %get-tuple-element.26), channel_id=1, source_target_pairs={{0,8},{4,12},{8,0},{12,4},{1,9},{5,13},{9,1},{13,5},{2,10},{6,14},... | collective-permute-start | bytes 98312 | tf_op jit(solution)/shard_map/ppermute | solution.py:373
  34.0 6.2 %collective-permute-start.7 = (bf16[128,128]{1,0:T(8,128)(2,1)S(1)}, bf16[128,128]{1,0:T(8,128)(2,1)S(1)}, u32[]{:S(2)}, u32[]{:S(2)}) collective-permute-start(bf16[128,128]{1,0:T(8,128)(2,1)S(1)} %get-tuple-element.27), channel_id=1, source_target_pairs={{0,12},{4,8},{8,4},{12,0},{1,13},{5,9},{9,5},{13,1},{2,14},{6,10},... | collective-permute-start | bytes 98312 | tf_op jit(solution)/shard_map/ppermute | solution.py:373
  36.3 4.2 %collective-permute-start.8 = (bf16[128,128]{1,0:T(8,128)(2,1)S(1)}, bf16[128,128]{1,0:T(8,128)(2,1)S(1)}, u32[]{:S(2)}, u32[]{:S(2)}) collective-permute-start(bf16[128,128]{1,0:T(8,128)(2,1)S(1)} %get-tuple-element.28), channel_id=1, source_target_pairs={{0,4},{4,0},{8,12},{12,8},{1,5},{5,1},{9,13},{13,9},{2,6},{6,2},{1... | collective-permute-start | bytes 98312 | tf_op jit(solution)/shard_map/ppermute | solution.py:373
